TPU v7x, 32 devices: a whole 2x2x4 slice. The times are simulated.
32 devices in a mesh: gx: 8 (over z, y), gy: 4 (over x, core).
Axes of the slice: x: 2, y: 2, z: 4, core: 2. Of those that a mesh axis runs over, the one named last changes fastest.
Arguments:
- right_hand: float32 [4, 6, 32, 1536], P(None, None, 'gx', 'gy'), may hold values from -40 to 40
- region_labels: int32 [32, 1536], P('gx', 'gy'), may hold values from 0 to 2
- potential_table: float32 [3, 6], replicated, may hold values from 0.5 to 3
- coupling: float32 [3, 6, 6], replicated, may hold values from -0.1 to 1, as said below
- aggregate_map: int32 [8, 96], P('gx', 'gy'), may hold values from 0 to 63
- coarse_inverse: float32 [384, 384], replicated, may hold values from -0.2 to 2
Outputs:
- solution: float32 [4, 6, 32, 1536], P(None, None, 'gx', 'gy')
Inputs may be any that keep to these rules, and one draw needn't show every extreme that they name: `coupling`: symmetric in the two band indices.
All inputs are finite; a program needn't handle non-finite values.
Results may differ from a plain program's by a relative error of at most 0.0003.
Values sent between devices are 32-bit elements; how exact they have to be, the bound alone decides.
No kernel may reach another device: no remote copies, remote signals or barrier semaphores. Data moves between devices by JAX's collectives and lax.ppermute only.
A program may use at most 64 MiB of HBM per device.

v0:
```python
import jax
import jax.numpy as jnp
from jax import lax
from jax.sharding import PartitionSpec as P

NZ = 48
BANDS = 6
VECS = 4
REGIONS = 3
ITERS = 3
LEVELS = 3
NAGG = 64


HIGHEST = lax.Precision.HIGHEST
OMEGA = 0.7


def extended(block, sides, width):
    for axis, dim in sides:
        count = lax.axis_size(axis)
        forward = [(i, i + 1) for i in range(count - 1)]
        backward = [(target, source) for source, target in forward]
        low = lax.ppermute(
            lax.slice_in_dim(block, block.shape[dim] - width, None, axis=dim), axis, forward
        )
        high = lax.ppermute(lax.slice_in_dim(block, 0, width, axis=dim), axis, backward)
        block = jnp.concatenate([low, block, high], axis=dim)
    return block


def couple(matrix, values):
    return jnp.einsum("ab,vbxyz->vaxyz", matrix, values, precision=HIGHEST)


def stencil(padded, values, coupling, potential, depth_index):
    level_scale = 0.25**depth_index
    along_x = padded[:, :, 2:, 1:-1, 1:-1] + padded[:, :, :-2, 1:-1, 1:-1]
    along_y = padded[:, :, 1:-1, 2:, 1:-1] + padded[:, :, 1:-1, :-2, 1:-1]
    along_z = padded[:, :, 1:-1, 1:-1, 2:] + padded[:, :, 1:-1, 1:-1, :-2]
    centre = 2.0 * level_scale * (coupling[0] + coupling[1] + coupling[2])
    result = couple(centre, values) - couple(level_scale * coupling[0], along_x)
    result = (
        result
        - couple(level_scale * coupling[1], along_y)
        - couple(level_scale * coupling[2], along_z)
    )
    return result + potential[None] * values


def restrict(values):
    leading = values.shape[:-3]
    size_x, size_y, size_z = values.shape[-3:]
    grouped = values.reshape(leading + (size_x // 2, 2, size_y // 2, 2, size_z // 2, 2))
    offset = len(leading)
    return jnp.mean(grouped, axis=(offset + 1, offset + 3, offset + 5))


def prolong(values):
    return jnp.repeat(jnp.repeat(jnp.repeat(values, 2, axis=2), 2, axis=3), 2, axis=4)


def inverse_diagonal(coupling, potential, depth_index):
    level_scale = 0.25**depth_index
    centre = 2.0 * level_scale * (coupling[0] + coupling[1] + coupling[2])
    return 1.0 / (jnp.diagonal(centre)[:, None, None, None] + potential)


def vcycle(residual, depth_index, operator, coarsest, inverses):
    correction = OMEGA * inverses[depth_index] * residual
    defect = residual - operator(correction, depth_index)
    if depth_index + 1 < LEVELS:
        correction = correction + prolong(
            vcycle(restrict(defect), depth_index + 1, operator, coarsest, inverses)
        )
    else:
        correction = correction + coarsest(defect)
    return correction + OMEGA * inverses[depth_index] * (
        residual - operator(correction, depth_index)
    )


def solve_small(normal_matrix, right_side, count):
    factor = {}
    for i in range(count):
        for k in range(i + 1):
            running = normal_matrix[i][k]
            for m in range(k):
                running = running - factor[i, m] * factor[k, m]
            if i == k:
                factor[i, i] = jnp.sqrt(running)
            else:
                factor[i, k] = running / factor[k, k]
    forward = []
    for i in range(count):
        running = right_side[i]
        for k in range(i):
            running = running - factor[i, k] * forward[k]
        forward.append(running / factor[i, i])
    answer = [None] * count
    for i in reversed(range(count)):
        running = forward[i]
        for k in range(i + 1, count):
            running = running - factor[k, i] * answer[k]
        answer[i] = running / factor[i, i]
    return answer


def inner_product(left, right_side):
    return jnp.sum(left * right_side, axis=(1, 2, 3, 4))


def expand(values):
    return values[:, None, None, None, None]


def least_squares(hessenberg, initial_norm):
    normal_matrix = [[None] * ITERS for i in range(ITERS)]
    for j in range(ITERS):
        for k in range(ITERS):
            running = hessenberg[0][j] * hessenberg[0][k]
            for i in range(1, ITERS + 1):
                running = running + hessenberg[i][j] * hessenberg[i][k]
            normal_matrix[j][k] = running
    right_side = [initial_norm * hessenberg[0][j] for j in range(ITERS)]
    return solve_small(normal_matrix, right_side, ITERS)


def shards(right_hand, region_labels, potential_table, coupling, aggregate_map, coarse_inverse):
    tile_x = right_hand.shape[2]
    tile_y = right_hand.shape[3] // NZ
    source = right_hand.reshape(VECS, BANDS, tile_x, tile_y, NZ)
    cell_labels = region_labels.reshape(tile_x, tile_y, NZ)
    potential = jnp.zeros((BANDS, tile_x, tile_y, NZ), jnp.float32)
    for r in range(REGIONS):
        potential = potential + jnp.where(
            cell_labels == r, potential_table[r][:, None, None, None], 0.0
        )
    potentials = [potential]
    for depth_index in range(1, LEVELS):
        potentials.append(restrict(potentials[-1]))
    inverses = [inverse_diagonal(coupling, potentials[d], d) for d in range(LEVELS)]
    onehot = (
        aggregate_map.reshape(-1)[:, None] == jnp.arange(NAGG, dtype=jnp.int32)[None, :]
    ).astype(jnp.float32)

    def operator(values, depth_index):
        padded = extended(values, (("gx", 2), ("gy", 3)), 1)
        padded = jnp.pad(padded, ((0, 0), (0, 0), (0, 0), (0, 0), (1, 1)))
        return stencil(padded, values, coupling, potentials[depth_index], depth_index)

    def coarsest(defect):
        flattened = defect.reshape(VECS, BANDS, -1)
        partial_value = jnp.einsum("vbc,ca->abv", flattened, onehot, precision=HIGHEST).reshape(
            NAGG * BANDS, VECS
        )
        summed = lax.psum(partial_value, ("gx", "gy"))
        solved = jnp.dot(coarse_inverse, summed, precision=HIGHEST).reshape(NAGG, BANDS, VECS)
        return jnp.einsum("ca,abv->vbc", onehot, solved, precision=HIGHEST).reshape(defect.shape)

    initial_norm = jnp.sqrt(lax.psum(inner_product(source, source), ("gx", "gy")))
    krylov_basis = [source / expand(initial_norm)]
    stored = []
    zeros_vec = jnp.zeros((VECS,), jnp.float32)
    hessenberg = [[zeros_vec] * ITERS for i in range(ITERS + 1)]
    for j in range(ITERS):
        preconditioned = vcycle(krylov_basis[j], 0, operator, coarsest, inverses)
        stored.append(preconditioned)
        mapped = operator(preconditioned, 0)
        local_terms = jnp.stack([inner_product(krylov_basis[i], mapped) for i in range(j + 1)])
        projection = lax.psum(local_terms, ("gx", "gy"))
        for i in range(j + 1):
            mapped = mapped - expand(projection[i]) * krylov_basis[i]
        norm_square = lax.psum(inner_product(mapped, mapped), ("gx", "gy"))
        for i in range(j + 1):
            hessenberg[i][j] = projection[i]
        hessenberg[j + 1][j] = jnp.sqrt(norm_square)
        if j + 1 < ITERS:
            krylov_basis.append(mapped / expand(hessenberg[j + 1][j]))
    weights = least_squares(hessenberg, initial_norm)
    combined = expand(weights[0]) * krylov_basis[0]
    for j in range(1, ITERS):
        combined = combined + expand(weights[j]) * krylov_basis[j]
    solution = vcycle(combined, 0, operator, coarsest, inverses)
    return solution.reshape(VECS, BANDS, tile_x, tile_y * NZ)


def solution(mesh):
    return jax.shard_map(
        shards,
        mesh=mesh,
        in_specs=(P(None, None, "gx", "gy"), P("gx", "gy"), P(), P(), P("gx", "gy"), P()),
        out_specs=P(None, None, "gx", "gy"),
        check_vma=False,
    )
```

profile of v0, /device:TPU:0, one launch (start us, length us, event | category | flops | bytes accessed | tf_op | source)
XLA Modules:
  0.0 1036.8 jit_solution(271920854889854742)
XLA Ops:
  4.7 42.0 %psum.77 = f32[4]{0:T(128)S(1)} all-reduce(f32[4]{0:T(128)S(1)} %multiply_reduce_fusion.9), channel_id=1, replica_groups=mesh['gx'=8,'gy'=4] {'gx','gy'}, use_global_device_ids=true, to_apply=%region_1.2 | all-reduce | flops 4 | bytes 32 | tf_op jit(solution)/shard_map/psum | solution.py:161
  49.8 4.8 collective-permute-start.1
  81.2 5.4 collective-permute-start.5
  97.4 5.0 collective-permute-start.9
  105.3 4.5 collective-permute-start.11
  111.8 47.7 %psum.78 = f32[384,4]{0,1:T(4,128)S(1)} all-reduce(f32[384,4]{0,1:T(4,128)S(1)} %reshape.692), channel_id=1, replica_groups=mesh['gx'=8,'gy'=4] {'gx','gy'}, use_global_device_ids=true, to_apply=%region_8.9 | all-reduce | flops 1536 | bytes 12288 | tf_op jit(solution)/shard_map/psum | solution.py:157
  162.0 4.8 collective-permute-start.13
  176.0 5.4 collective-permute-start.17
  198.1 5.4 collective-permute-start.21
  207.5 9.0 fusion.508
  217.9 5.1 collective-permute-start.23
  227.2 5.8 collective-permute-start.25
  245.6 47.0 %psum.79 = f32[4]{0:T(128)S(1)} all-reduce(f32[4]{0:T(128)S(1)} %get-tuple-element.144), channel_id=1, replica_groups=mesh['gx'=8,'gy'=4] {'gx','gy'}, use_global_device_ids=true, to_apply=%region_10.11 | all-reduce | flops 4 | bytes 32 | tf_op jit(solution)/shard_map/psum | solution.py:171
  292.9 41.3 %psum.80 = f32[4]{0:T(128)S(1)} all-reduce(f32[4]{0:T(128)S(1)} %multiply_reduce_fusion.7), channel_id=1, replica_groups=mesh['gx'=8,'gy'=4] {'gx','gy'}, use_global_device_ids=true, to_apply=%region_12.13 | all-reduce | flops 4 | bytes 32 | tf_op jit(solution)/shard_map/psum | solution.py:174
  335.9 4.8 collective-permute-start.29
  358.4 5.1 collective-permute-start.33
  374.5 5.0 collective-permute-start.37
  382.4 5.0 collective-permute-start.39
  389.4 47.7 %psum.81 = f32[384,4]{0,1:T(4,128)S(1)} all-reduce(f32[384,4]{0,1:T(4,128)S(1)} %reshape.707), channel_id=1, replica_groups=mesh['gx'=8,'gy'=4] {'gx','gy'}, use_global_device_ids=true, to_apply=%region_16.17 | all-reduce | flops 1536 | bytes 12288 | tf_op jit(solution)/shard_map/psum | solution.py:157
  439.6 4.8 collective-permute-start.41
  453.5 5.4 collective-permute-start.45
  477.3 5.0 collective-permute-start.49
  496.3 4.7 collective-permute-start.53
  505.2 6.4 collective-permute-start.55
  514.4 48.3 %psum.82 = f32[2,4]{1,0:T(2,128)S(1)} all-reduce(f32[2,4]{1,0:T(2,128)S(1)} %pad_maximum_fusion.420), channel_id=1, replica_groups=mesh['gx'=8,'gy'=4] {'gx','gy'}, use_global_device_ids=true, to_apply=%region_19.20 | all-reduce | flops 8 | bytes 64 | tf_op jit(solution)/shard_map/psum | solution.py:171
  563.1 39.5 %psum.83 = f32[4]{0:T(128)S(1)} all-reduce(f32[4]{0:T(128)S(1)} %get-tuple-element.21), channel_id=1, replica_groups=mesh['gx'=8,'gy'=4] {'gx','gy'}, use_global_device_ids=true, to_apply=%region_21.22 | all-reduce | flops 4 | bytes 32 | tf_op jit(solution)/shard_map/psum | solution.py:174
  604.1 4.8 collective-permute-start.57
  627.1 5.0 collective-permute-start.61
  642.5 5.0 collective-permute-start.65
  650.5 5.4 collective-permute-start.67
  657.9 47.8 %psum.84 = f32[384,4]{0,1:T(4,128)S(1)} all-reduce(f32[384,4]{0,1:T(4,128)S(1)} %reshape.721), channel_id=1, replica_groups=mesh['gx'=8,'gy'=4] {'gx','gy'}, use_global_device_ids=true, to_apply=%region_25.26 | all-reduce | flops 1536 | bytes 12288 | tf_op jit(solution)/shard_map/psum | solution.py:157
  708.1 4.8 collective-permute-start.69
  722.1 5.4 collective-permute-start.73
  745.6 5.2 collective-permute-start.77
  755.0 5.8 collective-permute-start.79
  764.9 4.8 collective-permute-start.81
  774.0 6.4 collective-permute-start.83
  784.0 48.4 %psum.85 = f32[3,4]{1,0:T(4,128)S(1)} all-reduce(f32[3,4]{1,0:T(4,128)S(1)} %pad_maximum_fusion.419), channel_id=1, replica_groups=mesh['gx'=8,'gy'=4] {'gx','gy'}, use_global_device_ids=true, to_apply=%region_29.30 | all-reduce | flops 12 | bytes 96 | tf_op jit(solution)/shard_map/psum | solution.py:171
  833.9 40.3 %psum.86 = f32[4]{0:T(128)S(1)} all-reduce(f32[4]{0:T(128)S(1)} %multiply_reduce_fusion), channel_id=1, replica_groups=mesh['gx'=8,'gy'=4] {'gx','gy'}, use_global_device_ids=true, to_apply=%region_31.32 | all-reduce | flops 4 | bytes 32 | tf_op jit(solution)/shard_map/psum | solution.py:174
  875.9 4.8 collective-permute-start.85
  899.0 5.0 collective-permute-start.89
  914.4 5.0 collective-permute-start.93
  922.4 5.4 collective-permute-start.95
  929.7 47.7 %psum.87 = f32[384,4]{0,1:T(4,128)S(1)} all-reduce(f32[384,4]{0,1:T(4,128)S(1)} %reshape.735), channel_id=1, replica_groups=mesh['gx'=8,'gy'=4] {'gx','gy'}, use_global_device_ids=true, to_apply=%region_35.36 | all-reduce | flops 1536 | bytes 12288 | tf_op jit(solution)/shard_map/psum | solution.py:157
  979.9 4.8 collective-permute-start.97
  993.9 5.4 collective-permute-start.101
  1017.3 5.2 collective-permute-start.105
  1026.8 5.9 collective-permute-start.107
  (573 shorter events, 339.7 us)
Async XLA Ops:
  48.5 17.5 %collective-permute-start = (f32[4,6,1,8,48]{4,1,3,2,0:T(8,128)}, f32[4,6,1,8,48]{4,1,3,2,0:T(8,128)S(1)}, u32[]{:S(2)}, u32[]{:S(2)}) collective-permute-start(f32[4,6,1,8,48]{4,1,3,2,0:T(8,128)} %get-tuple-element.70), channel_id=1, source_target_pairs={{4,0},{8,4},{12,8},{16,12},{20,16},{24,20},{28,24},{5,1},{9,5},{13... | collective-permute-start | bytes 110600 | tf_op jit(solution)/shard_map/ppermute | solution.py:27
  49.8 16.3 %collective-permute-start.1 = (f32[4,6,1,8,48]{4,1,3,2,0:T(8,128)}, f32[4,6,1,8,48]{4,1,3,2,0:T(8,128)S(1)}, u32[]{:S(2)}, u32[]{:S(2)}) collective-permute-start(f32[4,6,1,8,48]{4,1,3,2,0:T(8,128)} %get-tuple-element.69), channel_id=1, source_target_pairs={{0,4},{4,8},{8,12},{12,16},{16,20},{20,24},{24,28},{1,5},{5,9},{9,... | collective-permute-start | bytes 110600 | tf_op jit(solution)/shard_map/ppermute | solution.py:24
  79.9 7.4 collective-permute-start.4
  81.2 8.2 collective-permute-start.5
  96.1 7.1 collective-permute-start.8
  174.7 7.2 collective-permute-start.16
  176.0 8.6 collective-permute-start.17
  196.8 19.8 %collective-permute-start.20 = (f32[4,6,1,8,48]{4,1,3,2,0:T(8,128)S(1)}, f32[4,6,1,8,48]{4,1,3,2,0:T(8,128)S(1)}, u32[]{:S(2)}, u32[]{:S(2)}) collective-permute-start(f32[4,6,1,8,48]{4,1,3,2,0:T(8,128)S(1)} %get-tuple-element.68), channel_id=1, source_target_pairs={{4,0},{8,4},{12,8},{16,12},{20,16},{24,20},{28,24},{5,1},{9,5},{13... | collective-permute-start | bytes 110600 | tf_op jit(solution)/shard_map/ppermute | solution.py:27
  198.1 18.5 %collective-permute-start.21 = (f32[4,6,1,8,48]{4,1,3,2,0:T(8,128)S(1)}, f32[4,6,1,8,48]{4,1,3,2,0:T(8,128)S(1)}, u32[]{:S(2)}, u32[]{:S(2)}) collective-permute-start(f32[4,6,1,8,48]{4,1,3,2,0:T(8,128)S(1)} %get-tuple-element.67), channel_id=1, source_target_pairs={{0,4},{4,8},{8,12},{12,16},{16,20},{20,24},{24,28},{1,5},{5,9},{9,... | collective-permute-start | bytes 110600 | tf_op jit(solution)/shard_map/ppermute | solution.py:24
  216.6 7.0 collective-permute-start.22
  225.9 8.1 collective-permute-start.24
  227.2 10.2 collective-permute-start.25
  334.6 7.1 collective-permute-start.28
  335.9 7.7 collective-permute-start.29
  358.4 8.3 collective-permute-start.33
  373.2 7.1 collective-permute-start.36
  452.2 7.2 collective-permute-start.44
  453.5 8.6 collective-permute-start.45
  476.0 7.3 collective-permute-start.48
  477.3 9.7 collective-permute-start.49
  495.0 7.0 collective-permute-start.52
  496.3 7.6 collective-permute-start.53
  503.9 8.4 collective-permute-start.54
  505.2 7.1 collective-permute-start.55
  602.8 7.1 collective-permute-start.56
  604.1 8.2 collective-permute-start.57
  627.1 7.6 collective-permute-start.61
  641.3 7.1 collective-permute-start.64
  649.2 6.9 collective-permute-start.66
  720.8 7.1 collective-permute-start.72
  722.1 8.1 collective-permute-start.73
  744.3 7.5 collective-permute-start.76
  745.6 8.1 collective-permute-start.77
  753.7 7.8 collective-permute-start.78
  763.6 7.1 collective-permute-start.80
  764.9 7.8 collective-permute-start.81
  772.7 8.3 collective-permute-start.82
  774.0 7.1 collective-permute-start.83
  874.6 7.1 collective-permute-start.84
  875.9 8.2 collective-permute-start.85
  899.0 7.6 collective-permute-start.89
  913.1 7.1 collective-permute-start.92
  921.1 6.9 collective-permute-start.94
  992.6 7.1 collective-permute-start.100
  993.9 8.1 collective-permute-start.101
  1016.0 7.5 collective-permute-start.104
  1017.3 8.1 collective-permute-start.105
  1025.5 7.8 collective-permute-start.106
  (64 other events, 617.0 us)
where the time goes:
time: 1060 us; the launch traced here: 1040 us
  blocking collectives  498 us (47%)
  starting transfers between devices  314 us (30%)
  waiting for transfers between devices  66 us (6%)
  matrix products  60.5 us (6%)
  local copies, waits for them, and re-layouts  60.4 us (6%)
  other arithmetic  34.5 us (3%)
    ppermute x54, starting transfers between devices, extended(): lax.ppermute(lax.slice_in_dim(block, block.shape[dim] - width, None, axis...  244 us
    psum x4, blocking collectives, coarsest(): summed = lax.psum(partial_value, ('gx', 'gy'))  191 us
    psum x3, blocking collectives, shards(): projection = lax.psum(local_terms, ('gx', 'gy'))  144 us
    psum x3, blocking collectives, shards(): norm_square = lax.psum(inner_product(mapped, mapped), ('gx', 'gy'))  121 us
    ppermute x54, starting transfers between devices, extended(): lax.ppermute(lax.slice_in_dim(block, 0, width, axis=dim), axis, backward)  69.9 us
    ppermute x54, waiting for transfers between devices, extended(): lax.ppermute(lax.slice_in_dim(block, block.shape[dim] - width, None, axis...  61.2 us
    dot_general x108, matrix products, couple(): return jnp.einsum('ab,vbxyz->vaxyz', matrix, values, precision=HIGHEST)  56.2 us
    psum x1, blocking collectives, shards(): lax.psum(inner_product(source, source), ('gx', 'gy'))  42 us
  transfers between devices with their start and end apart: 108, of which 66 were waited for; matrix products, arithmetic and copies ran while one was open for 4% of the time, Pallas kernels for 0%

commit v1 on v0

v1 whole, which is shorter than its diff:
```python
import functools
import math

import jax
import jax.numpy as jnp
from jax import lax
from jax.experimental import pallas as pl
from jax.experimental.pallas import tpu as pltpu
from jax.sharding import PartitionSpec as P

NZ = 48
BANDS = 6
VECS = 4
REGIONS = 3
ITERS = 3
NAGG = 64
OMEGA = 0.7

HIGHEST = lax.Precision.HIGHEST
F32 = jnp.float32
BF16 = jnp.bfloat16

TX = 4
TY = 8
YT = 2
ZT = 6
COMBOS = YT * ZT
ZQ = NZ // ZT
GROUP = (TY // YT) * ZQ
TILES = 3
FIELD_ROWS = TILES * BANDS * TX
LABEL_ROWS = TILES * TX
AGG_ROW = FIELD_ROWS + LABEL_ROWS
ROWS = 88
LANES = 128
CELLS = TY * NZ


def source_lane(target):
    combo = target // GROUP
    rest = target % GROUP
    return ((rest // ZQ) * YT + combo // ZT) * NZ + (rest % ZQ) * ZT + combo % ZT


def iota(shape, dim):
    return lax.broadcasted_iota(jnp.int32, shape, dim)


def pack_kernel(groups, right_hbm, labels_hbm, agg_hbm, *rest):
    outs, (stack, right_ref, labels_ref, agg_ref, arrived) = rest[:VECS], rest[VECS:]
    own = lax.axis_index("gx") // groups
    copies = [
        pltpu.make_async_copy(source, target, arrived.at[i])
        for i, (source, target) in enumerate(
            ((right_hbm, right_ref), (labels_hbm, labels_ref), (agg_hbm, agg_ref))
        )
    ]
    for copy in copies:
        copy.start()
    permute = (iota((CELLS, CELLS), 0) == source_lane(iota((1, CELLS), 1))).astype(F32)
    count = BANDS * TX
    for copy in copies:
        copy.wait()
    for k in range(VECS):
        for b in range(BANDS):
            stack[pl.ds(k * count + b * TX, TX), :] = right_ref[own ^ k, b]
    stack[pl.ds(VECS * count, TX), :] = labels_ref[...].astype(F32)
    stack[pl.ds(VECS * count + TX, TX), :] = jnp.zeros((TX, CELLS), F32)
    moved = jnp.dot(stack[...], permute, precision=HIGHEST, preferred_element_type=F32)
    lane = iota((1, LANES), 1)
    inner = lane % GROUP
    wanted = (inner // (2 * ZQ)) * (NZ // 4) + 3 * ((inner % ZQ) // 2) + lane // GROUP
    wanted = jnp.where(lane < 3 * GROUP, wanted, -1)
    cells = agg_ref.shape[1]
    pick = (iota((cells, LANES), 0) == wanted).astype(F32)
    agg = jnp.dot(
        jnp.broadcast_to(agg_ref[...].astype(F32), (8, cells)),
        pick,
        precision=HIGHEST,
        preferred_element_type=F32,
    )
    for k in range(VECS):
        for t in range(TILES):
            tile = slice(t * LANES, (t + 1) * LANES)
            outs[k][pl.ds(t * count, count), :] = moved[k * count : (k + 1) * count, tile]
            outs[k][pl.ds(FIELD_ROWS + t * TX, TX), :] = moved[
                VECS * count : VECS * count + TX, tile
            ]
        outs[k][pl.ds(AGG_ROW, ROWS - AGG_ROW), :] = agg[: ROWS - AGG_ROW]


def unpack_kernel(groups, *refs):
    ins, out_ref, stack = refs[:VECS], refs[VECS], refs[VECS + 1]
    own = lax.axis_index("gx") // groups
    count = BANDS * TX
    permute = (iota((CELLS, CELLS), 1) == source_lane(iota((CELLS, 1), 0))).astype(F32)
    for k in range(VECS):
        for t in range(TILES):
            stack[pl.ds(k * count, count), t * LANES : (t + 1) * LANES] = ins[k][
                pl.ds(t * count, count), :
            ]
    moved = jnp.dot(stack[...], permute, precision=HIGHEST, preferred_element_type=F32)
    for k in range(VECS):
        for b in range(BANDS):
            first = k * count + b * TX
            out_ref[own ^ k, b] = moved[first : first + TX]


def order_kernel(source_ref, out_ref):
    size = NAGG * BANDS
    column = iota((1, size), 1)
    inputs = (iota((size, size), 0) == (column % NAGG) * BANDS + column // NAGG).astype(F32)
    wide = iota((1, BANDS * LANES), 1)
    place = wide % LANES
    wanted = jnp.where(place < NAGG, place * BANDS + wide // LANES, -1)
    outputs = (iota((size, BANDS * LANES), 0) == wanted).astype(F32)
    turned = jnp.dot(source_ref[...], inputs, precision=HIGHEST, preferred_element_type=F32)
    out_ref[...] = lax.dot_general(
        turned,
        outputs,
        (((0,), (0,)), ((), ())),
        precision=HIGHEST,
        preferred_element_type=F32,
    ).reshape(BANDS, NAGG, BANDS * LANES)


def solve_kernel(size_x, size_y, steps, *refs):
    count = len(steps) + 1
    pieces, (coef, table, inverse_ref) = refs[:count], refs[count : count + 3]
    refs = refs[count - 1 :]
    outs = refs[4 : 4 + VECS]
    (
        scratch, basis, ext_a, ext_b, pots, winv, sums, labels, aggs, onehot, pots_1, winv_1,
        pots_2, winv_2, res_1, cor_1, res_2, cor_2, cells_2, kept, hess, scale, answer, arrived,
    ) = refs[4 + VECS :]
    groups = size_x // VECS
    lanes = size_y * GROUP
    plane = (size_x, lanes)
    halves = lanes // LANES
    my_x = lax.axis_index("gx")
    my_y = lax.axis_index("gy")
    own = my_x // groups
    my_g = my_x % groups

    sub = iota(plane, 0)
    lane = iota(plane, 1)
    first_x, last_x = sub == 0, sub == size_x - 1
    first_y, last_y = lane < ZQ, lane >= lanes - ZQ
    first_z, last_z = lane % ZQ == 0, lane % ZQ == ZQ - 1

    def shifted(value, amount, axis, mask):
        moved = pltpu.roll(value, amount % value.shape[axis], axis)
        return jnp.where(mask, 0.0, moved)

    def coupling(direction, a, b):
        return coef[direction, a, b]

    def centre(band):
        return 2.0 * (coupling(0, band, band) + coupling(1, band, band) + coupling(2, band, band))

    copies = []
    for i, piece in enumerate(pieces):
        first = (1 << i) >> 1
        for place in range(first, 1 << i):
            mask_g = mask_y = 0
            for n, (axis, bit) in enumerate(steps):
                here = ((place >> n) & 1) << bit
                mask_g, mask_y = (mask_g | here, mask_y) if axis == "gx" else (mask_g, mask_y | here)
            for k in range(VECS):
                target = scratch.at[:, my_y ^ mask_y, (own ^ k) * groups + (my_g ^ mask_g), :]
                source = piece.at[(place - first) * VECS + k]
                copies.append(pltpu.make_async_copy(source, target, arrived.at[len(copies)]))
    for copy in copies:
        copy.start()
    for copy in copies:
        copy.wait()

    one_lane = iota((size_x, LANES), 1)
    low_64, low_32 = one_lane < 64, one_lane % 64 < 32

    def regroup(row):
        result = []
        for h in range(halves):
            g = [scratch[row, 4 * h + i] for i in range(4)]
            for i in (0, 1):
                low, high = g[i], g[i + 2]
                g[i] = jnp.where(low_64, low, pltpu.roll(high, 64, 1))
                g[i + 2] = jnp.where(low_64, pltpu.roll(low, 64, 1), high)
            for i in (0, 2):
                low, high = g[i], g[i + 1]
                g[i] = jnp.where(low_32, low, pltpu.roll(high, 32, 1))
                g[i + 1] = jnp.where(low_32, pltpu.roll(low, 96, 1), high)
            result.append(g)
        return [
            result[0][c] if halves == 1 else jnp.concatenate([r[c] for r in result], axis=1)
            for c in range(4)
        ]

    def load_field(x, total):
        for t in range(TILES):
            for b in range(BANDS):
                for c, value in enumerate(regroup(t * BANDS * TX + b * TX + x)):
                    basis[0, x, t * 4 + c, b] = value
                    total = total + value * value
            for c, value in enumerate(regroup(FIELD_ROWS + t * TX + x)):
                labels[x, t * 4 + c] = value
        return total

    total = lax.fori_loop(0, TX, load_field, jnp.zeros(plane, F32))
    for k, value in enumerate(regroup(AGG_ROW)[:3]):
        aggs[k] = value

    def total_of(value):
        return jnp.broadcast_to(jnp.sum(value, keepdims=True), plane)

    beta = jnp.sqrt(total_of(total))
    scale[...] = 1.0 / beta
    for i in range((ITERS + 1) * ITERS):
        hess[i] = jnp.zeros(plane, F32)

    def fill(x, carry):
        for b in range(BANDS):
            diagonal = centre(b)
            for zt in range(ZT):
                for yt in range(YT):
                    label = labels[x, yt * ZT + zt]
                    value = jnp.zeros(plane, F32)
                    for r in range(REGIONS):
                        value = jnp.where(label == float(r), table[r, b], value)
                    pots[x, yt * ZT + zt, b] = value
                    winv[x, yt * ZT + zt, b] = OMEGA * (1.0 / (diagonal + value))
                    if zt % 2 == 0 and yt == 0:
                        four = value
                    else:
                        four = four + value
                if zt % 2 == 1:
                    sums[x, zt // 2, b] = four
        return carry

    lax.fori_loop(0, TX, fill, 0)

    even_z = lane % 2 == 0
    even_y = (lane // ZQ) % 2 == 0

    def restrict_2(q):
        near, far = q[0] + q[1], q[1] + q[2]
        p = [
            jnp.where(even_z, near, pltpu.roll(near, 1, 1)),
            jnp.where(even_z, q[2], q[0])
            + jnp.where(even_z, pltpu.roll(q[0], lanes - 1, 1), pltpu.roll(q[2], 1, 1)),
            jnp.where(even_z, pltpu.roll(far, lanes - 1, 1), far),
        ]
        return [
            0.125
            * (v + jnp.where(even_y, pltpu.roll(v, lanes - ZQ, 1), pltpu.roll(v, ZQ, 1)))
            for v in p
        ]

    for b in range(BANDS):
        q = []
        for z in range(3):
            pair = []
            for x in range(2):
                value = 0.125 * (sums[2 * x, z, b] + sums[2 * x + 1, z, b])
                pots_1[x, z, b] = value
                winv_1[x, z, b] = OMEGA * (1.0 / (0.25 * centre(b) + value))
                pair.append(value)
            q.append(pair[0] + pair[1])
        for k, value in enumerate(restrict_2(q)):
            pots_2[k, b] = value
            winv_2[k, b] = OMEGA * (1.0 / (0.0625 * centre(b) + value))

    for k in range(3):
        for h in range(halves):
            for x in range(size_x):
                n = (k * halves + h) * size_x + x
                row = aggs[k, x : x + 1, h * LANES : (h + 1) * LANES]
                onehot[:, n * LANES : (n + 1) * LANES] = (
                    (row == iota((NAGG, LANES), 0).astype(F32)).astype(F32).astype(BF16)
                )

    def ghosts(ext):
        for c in range(COMBOS):
            for b in range(BANDS):
                ext[TX + 1, c, b] = shifted(ext[1, c, b], -1, 0, last_x)
                ext[0, c, b] = shifted(ext[TX, c, b], 1, 0, first_x)

    def combine(neighbours, count):
        acc = None
        for b in range(BANDS):
            differences = neighbours(b)
            new = []
            for a in range(BANDS):
                c = [coupling(d, a, b) for d in range(3)]
                row = []
                for n in range(count):
                    value = c[0] * differences[0][n]
                    value = value + c[1] * differences[1][n]
                    value = value + c[2] * differences[2][n]
                    row.append(value if acc is None else acc[a][n] + value)
                new.append(row)
            acc = new
        return acc

    def operator_0(ext, x, finish):
        for pair in range(ZT // 2):
            cells = [(yt, 2 * pair + i) for i in range(2) for yt in range(YT)]

            def neighbours(b):
                def at(dx, yt, zt):
                    return ext[x + 1 + dx, yt * ZT + zt, b]

                mid = {cell: at(0, *cell) for cell in cells}
                along = [[], [], []]
                for yt, zt in cells:
                    twice = mid[yt, zt] + mid[yt, zt]
                    along[0].append(twice - (at(1, yt, zt) + at(-1, yt, zt)))
                    partner = mid[1 - yt, zt]
                    if yt == 0:
                        outer = shifted(partner, ZQ, 1, first_y)
                    else:
                        outer = shifted(partner, -ZQ, 1, last_y)
                    along[1].append(twice - (partner + outer))
                    if zt % 2 == 0:
                        inside = mid[yt, zt + 1]
                        if zt == 0:
                            outer = shifted(at(0, yt, ZT - 1), 1, 1, first_z)
                        else:
                            outer = at(0, yt, zt - 1)
                    else:
                        inside = mid[yt, zt - 1]
                        if zt == ZT - 1:
                            outer = shifted(at(0, yt, 0), -1, 1, last_z)
                        else:
                            outer = at(0, yt, zt + 1)
                    along[2].append(twice - (inside + outer))
                return along

            acc = combine(neighbours, len(cells))
            values = [
                [
                    acc[b][n] + pots[x, yt * ZT + zt, b] * ext[x + 1, yt * ZT + zt, b]
                    for n, (yt, zt) in enumerate(cells)
                ]
                for b in range(BANDS)
            ]
            finish(pair, cells, values)

    def operator_1(src, finish):
        for x in range(2):

            def neighbours(b):
                along = [[], [], []]
                mid = [src[x, z, b] for z in range(3)]
                for z in range(3):
                    twice = mid[z] + mid[z]
                    partner = src[1 - x, z, b]
                    if x == 0:
                        outer = shifted(partner, 1, 0, first_x)
                    else:
                        outer = shifted(partner, -1, 0, last_x)
                    along[0].append(twice - (partner + outer))
                    along[1].append(
                        twice
                        - (shifted(mid[z], ZQ, 1, first_y) + shifted(mid[z], -ZQ, 1, last_y))
                    )
                    below = mid[z - 1] if z > 0 else shifted(mid[2], 1, 1, first_z)
                    above = mid[z + 1] if z < 2 else shifted(mid[0], -1, 1, last_z)
                    along[2].append(twice - (below + above))
                return along

            acc = combine(neighbours, 3)
            finish(
                x,
                [
                    [0.25 * acc[b][z] + pots_1[x, z, b] * src[x, z, b] for z in range(3)]
                    for b in range(BANDS)
                ],
            )

    first_y2, last_y2 = lane < 2 * ZQ, lane >= lanes - 2 * ZQ
    first_z2, last_z2 = lane % ZQ < 2, lane % ZQ >= ZQ - 2

    def operator_2(src):
        def neighbours(b):
            along = [[], [], []]
            mid = [src[z, b] for z in range(3)]
            for z in range(3):
                twice = mid[z] + mid[z]
                along[0].append(
                    twice - (shifted(mid[z], 1, 0, first_x) + shifted(mid[z], -1, 0, last_x))
                )
                along[1].append(
                    twice
                    - (
                        shifted(mid[z], 2 * ZQ, 1, first_y2)
                        + shifted(mid[z], -2 * ZQ, 1, last_y2)
                    )
                )
                below = mid[z - 1] if z > 0 else shifted(mid[2], 2, 1, first_z2)
                above = mid[z + 1] if z < 2 else shifted(mid[0], -2, 1, last_z2)
                along[2].append(twice - (below + above))
            return along

        acc = combine(neighbours, 3)
        return [
            [0.0625 * acc[b][z] + pots_2[z, b] * src[z, b] for z in range(3)] for b in range(BANDS)
        ]

    def split(value):
        high = value.astype(BF16)
        left = value - high.astype(F32)
        middle = left.astype(BF16)
        low = (left - middle.astype(F32)).astype(BF16)
        return jnp.concatenate([high, middle, low], axis=0)

    single = even_y & even_z
    count_2 = 3 * halves * size_x

    def coarse(defect):
        for z in range(3):
            for b in range(8):
                if b < BANDS:
                    value = jnp.where(single, defect[b][z], 0.0)
                else:
                    value = jnp.zeros(plane, F32)
                for h in range(halves):
                    n = (z * halves + h) * size_x
                    cells_2[pl.ds(n * 8 + b, size_x, stride=8), :] = value[
                        :, h * LANES : (h + 1) * LANES
                    ]
        wide = jnp.concatenate(
            [cells_2[pl.ds(n * 8, 8), :] for n in range(count_2)], axis=1
        )
        partial = lax.dot_general(
            onehot[...],
            split(wide),
            (((1,), (1,)), ((), ())),
            preferred_element_type=F32,
        )
        partial = partial[:, :8] + partial[:, 8:16] + partial[:, 16:24]
        acc = [jnp.zeros((8, LANES), F32)] * BANDS
        for b in range(BANDS):
            column = jnp.broadcast_to(partial[:, b : b + 1], (NAGG, LANES))
            for i in range(NAGG // 8):
                for a in range(BANDS):
                    acc[a] = (
                        acc[a]
                        + inverse_ref[b, pl.ds(i * 8, 8), a * LANES : (a + 1) * LANES]
                        * column[i * 8 : (i + 1) * 8]
                    )
        band = iota((8, LANES), 0)
        solved = jnp.zeros((8, LANES), F32)
        for a in range(BANDS):
            solved = jnp.where(band == a, jnp.sum(acc[a], axis=0, keepdims=True), solved)
        spread_out = jnp.dot(
            split(solved[:, :NAGG]), onehot[...], preferred_element_type=F32
        )
        spread_out = spread_out[:8] + spread_out[8:16] + spread_out[16:24]
        for n in range(count_2):
            cells_2[pl.ds(n * 8, 8), :] = spread_out[:, n * LANES : (n + 1) * LANES]

        def correction(b, z):
            parts = [
                cells_2[pl.ds(((z * halves + h) * size_x) * 8 + b, size_x, stride=8), :]
                for h in range(halves)
            ]
            return parts[0] if halves == 1 else jnp.concatenate(parts, axis=1)

        return correction

    def iteration(j, carry):
        factor = scale[...]

        def smooth(x, c_):
            for c in range(COMBOS):
                for b in range(BANDS):
                    value = basis[j, x, c, b] * factor
                    basis[j, x, c, b] = value
                    ext_a[x + 1, c, b] = winv[x, c, b] * value
            return c_

        lax.fori_loop(0, TX, smooth, 0)
        ghosts(ext_a)

        def down(x, c_):
            def finish(pair, cells, values):
                for b in range(BANDS):
                    defects = [
                        basis[j, x, yt * ZT + zt, b] - values[b][n]
                        for n, (yt, zt) in enumerate(cells)
                    ]
                    sums[x, pair, b] = (defects[0] + defects[1]) + (defects[2] + defects[3])

            operator_0(ext_a, x, finish)
            return c_

        lax.fori_loop(0, TX, down, 0)

        for x in range(2):
            for z in range(3):
                for b in range(BANDS):
                    value = 0.125 * (sums[2 * x, z, b] + sums[2 * x + 1, z, b])
                    res_1[x, z, b] = value
                    cor_1[x, z, b] = winv_1[x, z, b] * value

        held = {}

        def defect_1(x, values):
            for b in range(BANDS):
                for z in range(3):
                    value = res_1[x, z, b] - values[b][z]
                    if x == 0:
                        sums[0, z, b] = value
                    else:
                        sums[0, z, b] = sums[0, z, b] + value

        operator_1(cor_1, defect_1)
        for b in range(BANDS):
            for z, value in enumerate(restrict_2([sums[0, z, b] for z in range(3)])):
                res_2[z, b] = value
                cor_2[z, b] = winv_2[z, b] * value
        values = operator_2(cor_2)
        correction = coarse(
            [[res_2[z, b] - values[b][z] for z in range(3)] for b in range(BANDS)]
        )
        for b in range(BANDS):
            for z in range(3):
                cor_2[z, b] = cor_2[z, b] + correction(b, z)
        values = operator_2(cor_2)
        for b in range(BANDS):
            e = [
                cor_2[z, b] + winv_2[z, b] * (res_2[z, b] - values[b][z]) for z in range(3)
            ]
            fine = [
                jnp.where(even_z, e[0], e[1]),
                jnp.where(even_z, e[0], e[2]),
                jnp.where(even_z, e[1], e[2]),
            ]
            for x in range(2):
                for z in range(3):
                    cor_1[x, z, b] = cor_1[x, z, b] + fine[z]

        def post_1(x, values):
            for b in range(BANDS):
                for z in range(3):
                    sums[x, z, b] = cor_1[x, z, b] + winv_1[x, z, b] * (
                        res_1[x, z, b] - values[b][z]
                    )

        operator_1(cor_1, post_1)

        def prolong(x, c_):
            for c in range(COMBOS):
                for b in range(BANDS):
                    ext_a[x + 1, c, b] = ext_a[x + 1, c, b] + sums[x // 2, (c % ZT) // 2, b]
            return c_

        lax.fori_loop(0, TX, prolong, 0)
        ghosts(ext_a)

        def up(x, c_):
            def finish(pair, cells, values):
                for b in range(BANDS):
                    for n, (yt, zt) in enumerate(cells):
                        c = yt * ZT + zt
                        ext_b[x + 1, c, b] = ext_a[x + 1, c, b] + winv[x, c, b] * (
                            basis[j, x, c, b] - values[b][n]
                        )

            operator_0(ext_a, x, finish)
            return c_

        lax.fori_loop(0, TX, up, 0)
        ghosts(ext_b)

        def apply(x, c_):
            def finish(pair, cells, values):
                for b in range(BANDS):
                    for n, (yt, zt) in enumerate(cells):
                        basis[j + 1, x, yt * ZT + zt, b] = values[b][n]

            operator_0(ext_b, x, finish)
            quarter = one_lane // GROUP
            for b in range(BANDS):
                for t in range(TILES):
                    merged = None
                    for i in range(4):
                        moved = pltpu.roll(
                            ext_b[x + 1, t * 4 + i, b], (GROUP * i + lanes - GROUP * my_y) % lanes, 1
                        )[:, :LANES]
                        merged = moved if i == 0 else jnp.where(quarter == i, moved, merged)
                    kept[j, x, b * TILES + t] = merged
            return c_

        lax.fori_loop(0, TX, apply, 0)

        def project(i, c_):
            def body(x, parts):
                parts = list(parts)
                for c in range(COMBOS):
                    for b in range(BANDS):
                        n = (c * BANDS + b) % 4
                        parts[n] = parts[n] + basis[i, x, c, b] * basis[j + 1, x, c, b]
                return tuple(parts)

            parts = lax.fori_loop(0, TX, body, (jnp.zeros(plane, F32),) * 4)
            hess[i * ITERS + j] = total_of((parts[0] + parts[1]) + (parts[2] + parts[3]))
            return c_

        lax.fori_loop(0, j + 1, project, 0)

        def subtract(i, c_):
            weight = hess[i * ITERS + j]

            def body(x, parts):
                parts = list(parts)
                for c in range(COMBOS):
                    for b in range(BANDS):
                        n = (c * BANDS + b) % 4
                        value = basis[j + 1, x, c, b] - weight * basis[i, x, c, b]
                        basis[j + 1, x, c, b] = value
                        parts[n] = parts[n] + value * value
                return tuple(parts)

            parts = lax.fori_loop(0, TX, body, (jnp.zeros(plane, F32),) * 4)
            return (parts[0] + parts[1]) + (parts[2] + parts[3])

        total = lax.fori_loop(0, j + 1, subtract, jnp.zeros(plane, F32))
        norm = jnp.sqrt(total_of(total))
        hess[(j + 1) * ITERS + j] = norm
        scale[...] = 1.0 / norm
        return carry

    lax.fori_loop(0, ITERS, iteration, 0)

    h = [[hess[i * ITERS + j][:, :LANES] for j in range(ITERS)] for i in range(ITERS + 1)]
    normal = [
        [sum(h[i][j] * h[i][k] for i in range(ITERS + 1)) for k in range(ITERS)]
        for j in range(ITERS)
    ]
    first = beta[:, :LANES]
    weights = solve_small(normal, [first * h[0][j] for j in range(ITERS)], ITERS)

    for x in range(TX):
        for b in range(BANDS):
            for t in range(TILES):
                value = weights[0] * kept[0, x, b * TILES + t]
                for j in range(1, ITERS):
                    value = value + weights[j] * kept[j, x, b * TILES + t]
                value = pltpu.roll(value, (size_x - my_g) % size_x, 0)
                row = t * BANDS * TX + b * TX + x
                for z in range(VECS):
                    answer[z, row : row + 1, :] = value[z * groups : z * groups + 1]
    for k in range(VECS):
        outs[k][...] = answer[own ^ k]


def solve_small(normal_matrix, right_side, count):
    factor = {}
    for i in range(count):
        for k in range(i + 1):
            running = normal_matrix[i][k]
            for m in range(k):
                running = running - factor[i, m] * factor[k, m]
            if i == k:
                factor[i, i] = jnp.sqrt(running)
            else:
                factor[i, k] = running / factor[k, k]
    forward = []
    for i in range(count):
        running = right_side[i]
        for k in range(i):
            running = running - factor[i, k] * forward[k]
        forward.append(running / factor[i, i])
    answer = [None] * count
    for i in reversed(range(count)):
        running = forward[i]
        for k in range(i + 1, count):
            running = running - factor[k, i] * answer[k]
        answer[i] = running / factor[i, i]
    return answer


VMEM_SPEC = pl.BlockSpec(memory_space=pltpu.VMEM)
ANY_SPEC = pl.BlockSpec(memory_space=pl.ANY)
SMEM_SPEC = pl.BlockSpec(memory_space=pltpu.SMEM)


def bits(count):
    return count.bit_length() - 1


def shards(
    size_x, size_y, right_hand, region_labels, potential_table, coupling, aggregate_map,
    coarse_inverse,
):
    groups = size_x // VECS
    devices = size_x * size_y
    names = ("gx", "gy")
    stride = groups * size_y

    def exchanged(value, mask):
        return lax.ppermute(value, names, [(i, i ^ mask) for i in range(devices)])

    row_shape = jax.ShapeDtypeStruct((ROWS, LANES), F32)
    count = BANDS * TX
    packed = pl.pallas_call(
        functools.partial(pack_kernel, groups),
        out_shape=[row_shape] * VECS,
        in_specs=[ANY_SPEC] * 3,
        out_specs=[VMEM_SPEC] * VECS,
        scratch_shapes=[
            pltpu.VMEM((VECS * count + 8, CELLS), F32),
            pltpu.VMEM(right_hand.shape, F32),
            pltpu.VMEM(region_labels.shape, jnp.int32),
            pltpu.VMEM(aggregate_map.shape, jnp.int32),
            pltpu.SemaphoreType.DMA((3,)),
        ],
        compiler_params=pltpu.CompilerParams(vmem_limit_bytes=8 * 2**20),
        name="pack",
    )(right_hand, region_labels, aggregate_map)
    parts = [packed[0]] + [exchanged(packed[k], k * stride) for k in range(1, VECS)]
    block = jnp.stack(parts)
    steps = [("gy", i) for i in range(bits(size_y) - 1, 0, -1)]
    steps += [("gx", i) for i in range(bits(groups))]
    steps += [("gy", 0)]
    pieces = [block]
    for axis, bit in steps:
        mask = (1 << bit) * (size_y if axis == "gx" else 1)
        pieces.append(exchanged(jnp.concatenate(pieces, axis=0), mask))

    inverse = pl.pallas_call(
        order_kernel,
        out_shape=jax.ShapeDtypeStruct((BANDS, NAGG, BANDS * LANES), F32),
        in_specs=[VMEM_SPEC],
        out_specs=VMEM_SPEC,
        compiler_params=pltpu.CompilerParams(vmem_limit_bytes=16 * 2**20),
        cost_estimate=pl.CostEstimate(
            flops=6 * (NAGG * BANDS) ** 3, bytes_accessed=2**21, transcendentals=0
        ),
        name="order",
    )(coarse_inverse)

    lanes = size_y * GROUP
    plane = (size_x, lanes)
    count_2 = 3 * (lanes // LANES) * size_x
    vmem = lambda *shape: pltpu.VMEM(shape + plane, F32)
    scratch = [
            pltpu.VMEM((ROWS, size_y, size_x, LANES), F32),
            vmem(ITERS + 1, TX, COMBOS, BANDS),
            vmem(TX + 2, COMBOS, BANDS),
            vmem(TX + 2, COMBOS, BANDS),
            vmem(TX, COMBOS, BANDS),
            vmem(TX, COMBOS, BANDS),
            vmem(TX, 3, BANDS),
            vmem(TX, COMBOS),
            vmem(3),
            pltpu.VMEM((NAGG, count_2 * LANES), BF16),
            vmem(2, 3, BANDS),
            vmem(2, 3, BANDS),
            vmem(3, BANDS),
            vmem(3, BANDS),
            vmem(2, 3, BANDS),
            vmem(2, 3, BANDS),
            vmem(3, BANDS),
            vmem(3, BANDS),
            pltpu.VMEM((count_2 * 8, LANES), F32),
            pltpu.VMEM((ITERS, TX, BANDS * TILES, size_x, LANES), F32),
            vmem((ITERS + 1) * ITERS),
            vmem(),
            pltpu.VMEM((VECS, FIELD_ROWS, LANES), F32),
            pltpu.SemaphoreType.DMA((devices,)),
    ]
    held = sum(math.prod(ref.shape) * 4 for ref in scratch)
    answers = pl.pallas_call(
        functools.partial(solve_kernel, size_x, size_y, tuple(steps)),
        out_shape=[jax.ShapeDtypeStruct((FIELD_ROWS, LANES), F32)] * VECS,
        in_specs=[ANY_SPEC] * len(pieces) + [SMEM_SPEC, SMEM_SPEC, VMEM_SPEC],
        out_specs=[VMEM_SPEC] * VECS,
        scratch_shapes=scratch,
        compiler_params=pltpu.CompilerParams(
            vmem_limit_bytes=min(held + 6 * 2**20, 63 * 2**20)
        ),
        name="solve",
    )(*pieces, coupling, potential_table, inverse)
    received = [answers[0]] + [exchanged(answers[k], k * stride) for k in range(1, VECS)]
    return pl.pallas_call(
        functools.partial(unpack_kernel, groups),
        out_shape=jax.ShapeDtypeStruct(right_hand.shape, F32),
        in_specs=[VMEM_SPEC] * VECS,
        out_specs=VMEM_SPEC,
        scratch_shapes=[pltpu.VMEM((VECS * count, CELLS), F32)],
        compiler_params=pltpu.CompilerParams(vmem_limit_bytes=8 * 2**20),
        name="unpack",
    )(*received)


def solution(mesh):
    return jax.shard_map(
        functools.partial(shards, mesh.shape["gx"], mesh.shape["gy"]),
        mesh=mesh,
        in_specs=(P(None, None, "gx", "gy"), P("gx", "gy"), P(), P(), P("gx", "gy"), P()),
        out_specs=P(None, None, "gx", "gy"),
        check_vma=False,
    )
```

time: 1060 us -> 81.9 us (0.08); the launches traced: 1040 us -> 81.7 us
  blocking collectives: 498 us -> 0 us
  starting transfers between devices: 314 us -> 13.3 us
  matrix products: 60.5 us -> 0 us
  local copies, waits for them, and re-layouts: 60.4 us -> 2.41 us
  waiting for transfers between devices: 66 us -> 18.4 us
  Pallas kernels: 0 us -> 47.5 us
  other arithmetic: 34.5 us -> 0.02 us
    psum x11 -> x0, blocking collectives: 498 us -> none  [the longest x4 191 us: coarsest(): summed = lax.psum(partial_value, ('gx', 'gy'))]
    ppermute x108 -> x9, starting transfers between devices: 314 us -> 13.3 us  [exchanged(): return lax.ppermute(value, names, [(i, i ^ mask) for i in range(devices)])]
    dot_general x120 -> x0, matrix products: 60.5 us -> none  [the longest x108 56.2 us: couple(): return jnp.einsum('ab,vbxyz->vaxyz', matrix, values, precision=HIGHEST)]
    ppermute x108 -> x9, waiting for transfers between devices: 66 us -> 18.4 us  [exchanged(): return lax.ppermute(value, names, [(i, i ^ mask) for i in range(devices)])]
    pallas_call x0 -> x4, Pallas kernels: none -> 47.5 us  [the longest x1 40.8 us: shards(): pl.pallas_call(functools.partial(solve_kernel, size_x, size_y, tuple(step...]
    reduce_sum x14 -> x0, other arithmetic: 19.9 us -> none  [the longest x10 16.5 us: restrict(): return jnp.mean(grouped, axis=(offset + 1, offset + 3, offset + 5))]
    reshape x29 -> x0, local copies, waits for them, and re-layouts: 18.6 us -> none  [the longest x4 10.2 us: prolong(): jnp.repeat(jnp.repeat(jnp.repeat(values, 2, axis=2), 2, axis=3), 2, axis=4)]
    broadcast_in_dim x25 -> x0, local copies, waits for them, and re-layouts: 15.8 us -> none  [the longest x12 14.1 us: prolong(): jnp.repeat(jnp.repeat(jnp.repeat(values, 2, axis=2), 2, axis=3), 2, axis=4)]
  transfers between devices with their start and end apart: 108 -> 9, of which waited for: 66 -> 6; matrix products, arithmetic and copies ran while one was open for 4% -> 0% of each run, Pallas kernels for 0% -> 5%
where the time goes in v1:
time: 81.9 us; the launch traced here: 81.7 us
  Pallas kernels  47.5 us (58%)
  waiting for transfers between devices  18.4 us (22%)
  starting transfers between devices  13.3 us (16%)
  local copies, waits for them, and re-layouts  2.41 us (3%)
    pallas_call x1, Pallas kernels, shards(): pl.pallas_call(functools.partial(solve_kernel, size_x, size_y, tuple(step...  40.8 us
    ppermute x9, waiting for transfers between devices, exchanged(): return lax.ppermute(value, names, [(i, i ^ mask) for i in range(devices)])  18.4 us
    ppermute x9, starting transfers between devices, exchanged(): return lax.ppermute(value, names, [(i, i ^ mask) for i in range(devices)])  13.3 us
    pallas_call x1, Pallas kernels, shards(): pl.pallas_call(order_kernel, out_shape=jax.ShapeDtypeStruct((BANDS, NAGG,...  4.43 us
    unnamed x17, local copies, waits for them, and re-layouts  2.38 us
  transfers between devices with their start and end apart: 9, of which 6 were waited for; matrix products, arithmetic and copies ran while one was open for 0% of the time, Pallas kernels for 5%

profile of v1, /device:TPU:0, one launch (start us, length us, event | category | flops | bytes accessed | tf_op | source)
XLA Modules:
  0.0 81.7 jit_solution(2934418573564967033)
XLA Ops:
  0.0 0.0 copy-start
  0.0 0.0 copy-start.1
  0.0 1.0 %copy-done.1 = f32[4,6,4,384]{3,2,1,0:T(4,128)S(1)} copy-done((f32[4,6,4,384]{3,2,1,0:T(4,128)S(1)}, f32[4,6,4,384]{3,2,1,0:T(4,128)}, u32[]{:S(2)}) %copy-start.1) | copy-done | bytes 147480
  1.0 0.0 copy-start.3
  1.0 0.7 copy-done.3
  1.7 0.0 copy-start.5
  1.7 0.7 copy-done.5
  2.3 0.9 %pack.1 = (f32[88,128]{1,0:T(8,128)S(1)}, f32[88,128]{1,0:T(8,128)S(1)}, f32[88,128]{1,0:T(8,128)S(1)}, f32[88,128]{1,0:T(8,128)S(1)}) custom-call(f32[4,6,4,384]{3,2,1,0:T(4,128)S(1)} %copy-done.1, s32[4,384]{1,0:T(4,128)S(1)} %copy-done.3, s32[1,24]{1,0:T(1,128)S(1)} %copy-done.5), custom_call_target="tpu_custom_call" | custom-call | tf_op jit(solution)/shard_map/pack/pallas_call | solution.py:708
  3.2 3.1 %collective-permute-start = (f32[88,128]{1,0:T(8,128)S(1)}, f32[88,128]{1,0:T(8,128)S(1)}, u32[]{:S(2)}, u32[]{:S(2)}) collective-permute-start(f32[88,128]{1,0:T(8,128)S(1)} %get-tuple-element.14), channel_id=1, source_target_pairs={{0,8},{1,9},{2,10},{3,11},{4,12},{5,13},{6,14},{7,15},{8,0},{9,1},... | collective-permute-start | bytes 135176 | tf_op jit(solution)/shard_map/ppermute | solution.py:704
  6.3 2.6 %collective-permute-start.1 = (f32[88,128]{1,0:T(8,128)S(1)}, f32[88,128]{1,0:T(8,128)S(1)}, u32[]{:S(2)}, u32[]{:S(2)}) collective-permute-start(f32[88,128]{1,0:T(8,128)S(1)} %get-tuple-element.15), channel_id=1, source_target_pairs={{0,16},{1,17},{2,18},{3,19},{4,20},{5,21},{6,22},{7,23},{8,24},{9,... | collective-permute-start | bytes 135176 | tf_op jit(solution)/shard_map/ppermute | solution.py:704
  8.9 0.0 collective-permute-start.2
  8.9 0.0 collective-permute-done
  8.9 3.2 %collective-permute-done.1 = f32[88,128]{1,0:T(8,128)S(1)} collective-permute-done((f32[88,128]{1,0:T(8,128)S(1)}, f32[88,128]{1,0:T(8,128)S(1)}, u32[]{:S(2)}, u32[]{:S(2)}) %collective-permute-start.1) | collective-permute-done | bytes 45088 | tf_op jit(solution)/shard_map/ppermute | solution.py:704
  12.1 2.6 %collective-permute-done.2 = f32[88,128]{1,0:T(8,128)S(1)} collective-permute-done((f32[88,128]{1,0:T(8,128)S(1)}, f32[88,128]{1,0:T(8,128)S(1)}, u32[]{:S(2)}, u32[]{:S(2)}) %collective-permute-start.2) | collective-permute-done | bytes 45088 | tf_op jit(solution)/shard_map/ppermute | solution.py:704
  14.8 1.6 %collective-permute-start.3 = (f32[4,88,128]{2,1,0:T(8,128)S(1)}, f32[4,88,128]{2,1,0:T(8,128)S(1)}, u32[]{:S(2)}, u32[]{:S(2)}) collective-permute-start(f32[4,88,128]{2,1,0:T(8,128)S(1)} %pad_maximum_fusion.refs_0_), channel_id=1, source_target_pairs={{0,2},{1,3},{2,0},{3,1},{4,6},{5,7},{6,4},{7,5},{8,10},{9,11},{10,... | collective-permute-start | bytes 540680 | tf_op jit(solution)/shard_map/ppermute | solution.py:704
  16.4 4.0 %collective-permute-done.3.refs_1_ = f32[4,88,128]{2,1,0:T(8,128)S(1)} collective-permute-done((f32[4,88,128]{2,1,0:T(8,128)S(1)}, f32[4,88,128]{2,1,0:T(8,128)S(1)}, u32[]{:S(2)}, u32[]{:S(2)}) %collective-permute-start.3) | collective-permute-done | bytes 180256 | tf_op jit(solution)/shard_map/ppermute | solution.py:704
  20.4 1.6 %collective-permute-start.4 = (f32[8,88,128]{2,1,0:T(8,128)S(1)}, f32[8,88,128]{2,1,0:T(8,128)S(1)}, u32[]{:S(2)}, u32[]{:S(2)}) collective-permute-start(f32[8,88,128]{2,1,0:T(8,128)S(1)} %get-tuple-element.22), channel_id=1, source_target_pairs={{0,4},{1,5},{2,6},{3,7},{4,0},{5,1},{6,2},{7,3},{8,12},{9,13},{10,... | collective-permute-start | bytes 1081352 | tf_op jit(solution)/shard_map/ppermute | solution.py:704
  22.0 5.9 %collective-permute-done.4.refs_2_ = f32[8,88,128]{2,1,0:T(8,128)S(1)} collective-permute-done((f32[8,88,128]{2,1,0:T(8,128)S(1)}, f32[8,88,128]{2,1,0:T(8,128)S(1)}, u32[]{:S(2)}, u32[]{:S(2)}) %collective-permute-start.4) | collective-permute-done | bytes 360480 | tf_op jit(solution)/shard_map/ppermute | solution.py:704
  27.9 0.0 copy-start.2
  27.9 0.0 copy-start.4
  27.9 0.1 collective-permute-start.5
  28.0 0.0 copy-done
  28.0 4.4 %order.1.refs_6_ = f32[6,64,768]{2,1,0:T(8,128)S(1)} custom-call(f32[384,384]{1,0:T(8,128)S(1)} %copy-done), custom_call_target="tpu_custom_call" | custom-call | flops 339738624 | bytes 2097152 | tf_op jit(solution)/shard_map/order/pallas_call | solution.py:733
  32.4 0.0 collective-permute-done.5.refs_3_
  32.4 0.0 copy-done.2
  32.4 0.0 copy-done.4
  32.5 40.8 %solve.1 = (f32[72,128]{1,0:T(8,128)S(1)}, f32[72,128]{1,0:T(8,128)S(1)}, f32[72,128]{1,0:T(8,128)S(1)}, f32[72,128]{1,0:T(8,128)S(1)}) custom-call(f32[4,88,128]{2,1,0:T(8,128)S(1)} %pad_maximum_fusion.refs_0_, f32[4,88,128]{2,1,0:T(8,128)S(1)} %collective-permute-done.3.refs_1_, f32[8,88,128]{2,1,0:T(8,128)S(1)} %collective-permute-done.4.refs_2_, ...), custom_call_target="tpu_custom_call" | custom-call | tf_op jit(solution)/shard_map/solve/pallas_call | solution.py:776
  73.3 0.1 collective-permute-start.6
  73.4 1.2 %collective-permute-start.7 = (f32[72,128]{1,0:T(8,128)S(1)}, f32[72,128]{1,0:T(8,128)S(1)}, u32[]{:S(2)}, u32[]{:S(2)}) collective-permute-start(f32[72,128]{1,0:T(8,128)S(1)} %get-tuple-element.19), channel_id=1, source_target_pairs={{0,16},{1,17},{2,18},{3,19},{4,20},{5,21},{6,22},{7,23},{8,24},{9,... | collective-permute-start | bytes 110600 | tf_op jit(solution)/shard_map/ppermute | solution.py:704
  74.6 3.1 %collective-permute-start.8 = (f32[72,128]{1,0:T(8,128)S(1)}, f32[72,128]{1,0:T(8,128)S(1)}, u32[]{:S(2)}, u32[]{:S(2)}) collective-permute-start(f32[72,128]{1,0:T(8,128)S(1)} %get-tuple-element.20), channel_id=1, source_target_pairs={{0,24},{1,25},{2,26},{3,27},{4,28},{5,29},{6,30},{7,31},{8,16},{9,... | collective-permute-start | bytes 110600 | tf_op jit(solution)/shard_map/ppermute | solution.py:704
  77.7 0.0 collective-permute-done.6.refs_1_
  77.7 0.9 %collective-permute-done.7.refs_2_ = f32[72,128]{1,0:T(8,128)S(1)} collective-permute-done((f32[72,128]{1,0:T(8,128)S(1)}, f32[72,128]{1,0:T(8,128)S(1)}, u32[]{:S(2)}, u32[]{:S(2)}) %collective-permute-start.7) | collective-permute-done | bytes 36896 | tf_op jit(solution)/shard_map/ppermute | solution.py:704
  78.6 1.8 %collective-permute-done.8.refs_3_ = f32[72,128]{1,0:T(8,128)S(1)} collective-permute-done((f32[72,128]{1,0:T(8,128)S(1)}, f32[72,128]{1,0:T(8,128)S(1)}, u32[]{:S(2)}, u32[]{:S(2)}) %collective-permute-start.8) | collective-permute-done | bytes 36896 | tf_op jit(solution)/shard_map/ppermute | solution.py:704
  80.4 1.3 %unpack.1 = f32[4,6,4,384]{3,2,1,0:T(4,128)} custom-call(f32[72,128]{1,0:T(8,128)S(1)} %get-tuple-element.17.refs_0_, f32[72,128]{1,0:T(8,128)S(1)} %collective-permute-done.6.refs_1_, f32[72,128]{1,0:T(8,128)S(1)} %collective-permute-done.7.refs_2_, f32[72,128]{1,0:T(8,128)S(1)} %collective-permute-done.8.refs_3_), custom_call_target="tpu_custom_call" | custom-call | tf_op jit(solution)/shard_map/unpack/pallas_call | solution.py:788
  (7 shorter events, 0.1 us)
Async XLA Ops:
  0.0 28.0 %copy-start = (f32[384,384]{1,0:T(8,128)S(1)}, f32[384,384]{1,0:T(8,128)}, u32[]{:S(2)}) copy-start(f32[384,384]{1,0:T(8,128)} %source_ref.1) | copy-start | bytes 1769476
  0.0 1.0 %copy-start.1 = (f32[4,6,4,384]{3,2,1,0:T(4,128)S(1)}, f32[4,6,4,384]{3,2,1,0:T(4,128)}, u32[]{:S(2)}) copy-start(f32[4,6,4,384]{3,2,1,0:T(4,128)} %right_hbm.1) | copy-start | bytes 442372
  1.0 0.7 copy-start.3
  1.7 0.7 copy-start.5
  3.2 5.7 %collective-permute-start = (f32[88,128]{1,0:T(8,128)S(1)}, f32[88,128]{1,0:T(8,128)S(1)}, u32[]{:S(2)}, u32[]{:S(2)}) collective-permute-start(f32[88,128]{1,0:T(8,128)S(1)} %get-tuple-element.14), channel_id=1, source_target_pairs={{0,8},{1,9},{2,10},{3,11},{4,12},{5,13},{6,14},{7,15},{8,0},{9,1},... | collective-permute-start | bytes 135176 | tf_op jit(solution)/shard_map/ppermute | solution.py:704
  6.3 5.8 %collective-permute-start.1 = (f32[88,128]{1,0:T(8,128)S(1)}, f32[88,128]{1,0:T(8,128)S(1)}, u32[]{:S(2)}, u32[]{:S(2)}) collective-permute-start(f32[88,128]{1,0:T(8,128)S(1)} %get-tuple-element.15), channel_id=1, source_target_pairs={{0,16},{1,17},{2,18},{3,19},{4,20},{5,21},{6,22},{7,23},{8,24},{9,... | collective-permute-start | bytes 135176 | tf_op jit(solution)/shard_map/ppermute | solution.py:704
  8.9 5.8 %collective-permute-start.2 = (f32[88,128]{1,0:T(8,128)S(1)}, f32[88,128]{1,0:T(8,128)S(1)}, u32[]{:S(2)}, u32[]{:S(2)}) collective-permute-start(f32[88,128]{1,0:T(8,128)S(1)} %get-tuple-element.16), channel_id=1, source_target_pairs={{0,24},{1,25},{2,26},{3,27},{4,28},{5,29},{6,30},{7,31},{8,16},{9,... | collective-permute-start | bytes 135176 | tf_op jit(solution)/shard_map/ppermute | solution.py:704
  14.8 5.6 %collective-permute-start.3 = (f32[4,88,128]{2,1,0:T(8,128)S(1)}, f32[4,88,128]{2,1,0:T(8,128)S(1)}, u32[]{:S(2)}, u32[]{:S(2)}) collective-permute-start(f32[4,88,128]{2,1,0:T(8,128)S(1)} %pad_maximum_fusion.refs_0_), channel_id=1, source_target_pairs={{0,2},{1,3},{2,0},{3,1},{4,6},{5,7},{6,4},{7,5},{8,10},{9,11},{10,... | collective-permute-start | bytes 540680 | tf_op jit(solution)/shard_map/ppermute | solution.py:704
  20.4 7.5 %collective-permute-start.4 = (f32[8,88,128]{2,1,0:T(8,128)S(1)}, f32[8,88,128]{2,1,0:T(8,128)S(1)}, u32[]{:S(2)}, u32[]{:S(2)}) collective-permute-start(f32[8,88,128]{2,1,0:T(8,128)S(1)} %get-tuple-element.22), channel_id=1, source_target_pairs={{0,4},{1,5},{2,6},{3,7},{4,0},{5,1},{6,2},{7,3},{8,12},{9,13},{10,... | collective-permute-start | bytes 1081352 | tf_op jit(solution)/shard_map/ppermute | solution.py:704
  27.9 4.6 %copy-start.2 = (f32[3,6,6]{2,1,0:T(8,128)S(1)}, f32[3,6,6]{2,1,0:T(8,128)}, u32[]{:S(2)}) copy-start(f32[3,6,6]{2,1,0:T(8,128)} %refs_4_.1) | copy-start | bytes 1300
  27.9 4.6 %copy-start.4 = (f32[3,6]{1,0:T(4,128)S(1)}, f32[3,6]{1,0:T(4,128)}, u32[]{:S(2)}) copy-start(f32[3,6]{1,0:T(4,128)} %refs_5_.1) | copy-start | bytes 220
  27.9 4.5 %collective-permute-start.5 = (f32[16,88,128]{2,1,0:T(8,128)S(1)}, f32[16,88,128]{2,1,0:T(8,128)S(1)}, u32[]{:S(2)}, u32[]{:S(2)}) collective-permute-start(f32[16,88,128]{2,1,0:T(8,128)S(1)} %constant_dynamic-update-slice_fusion.5), channel_id=1, source_target_pairs={{0,1},{1,0},{2,3},{3,2},{4,5},{5,4},{6,7},{7,6},{8,9},{9,8},{10,11... | collective-permute-start | bytes 2162696 | tf_op jit(solution)/shard_map/ppermute | solution.py:704
  73.3 4.5 %collective-permute-start.6 = (f32[72,128]{1,0:T(8,128)S(1)}, f32[72,128]{1,0:T(8,128)S(1)}, u32[]{:S(2)}, u32[]{:S(2)}) collective-permute-start(f32[72,128]{1,0:T(8,128)S(1)} %get-tuple-element.18), channel_id=1, source_target_pairs={{0,8},{1,9},{2,10},{3,11},{4,12},{5,13},{6,14},{7,15},{8,0},{9,1},... | collective-permute-start | bytes 110600 | tf_op jit(solution)/shard_map/ppermute | solution.py:704
  73.4 5.2 %collective-permute-start.7 = (f32[72,128]{1,0:T(8,128)S(1)}, f32[72,128]{1,0:T(8,128)S(1)}, u32[]{:S(2)}, u32[]{:S(2)}) collective-permute-start(f32[72,128]{1,0:T(8,128)S(1)} %get-tuple-element.19), channel_id=1, source_target_pairs={{0,16},{1,17},{2,18},{3,19},{4,20},{5,21},{6,22},{7,23},{8,24},{9,... | collective-permute-start | bytes 110600 | tf_op jit(solution)/shard_map/ppermute | solution.py:704
  74.6 5.8 %collective-permute-start.8 = (f32[72,128]{1,0:T(8,128)S(1)}, f32[72,128]{1,0:T(8,128)S(1)}, u32[]{:S(2)}, u32[]{:S(2)}) collective-permute-start(f32[72,128]{1,0:T(8,128)S(1)} %get-tuple-element.20), channel_id=1, source_target_pairs={{0,24},{1,25},{2,26},{3,27},{4,28},{5,29},{6,30},{7,31},{8,16},{9,... | collective-permute-start | bytes 110600 | tf_op jit(solution)/shard_map/ppermute | solution.py:704

commit v2 on v1

--- a/solution.py
+++ b/solution.py
@@ -130,8 +130,8 @@
     refs = refs[count - 1 :]
     outs = refs[4 : 4 + VECS]
     (
-        scratch, basis, ext_a, ext_b, pots, winv, sums, labels, aggs, onehot, pots_1, winv_1,
-        pots_2, winv_2, res_1, cor_1, res_2, cor_2, cells_2, kept, hess, scale, answer, arrived,
+        scratch, basis, fresh, ext, work, pots, winv, sums, labels, aggs, onehot, pots_1, winv_1,
+        pots_2, winv_2, sides, res_1, cor_1, res_2, cor_2, cells_2, kept, hess, scale, answer, arrived,
     ) = refs[4 + VECS :]
     groups = size_x // VECS
     lanes = size_y * GROUP
@@ -200,7 +200,9 @@
         for t in range(TILES):
             for b in range(BANDS):
                 for c, value in enumerate(regroup(t * BANDS * TX + b * TX + x)):
-                    basis[0, x, t * 4 + c, b] = value
+                    work[x, t * 4 + c, b] = value
+                    for i in range(1, ITERS):
+                        basis[i, x, t * 4 + c, b] = jnp.zeros(plane, F32)
                     total = total + value * value
             for c, value in enumerate(regroup(FIELD_ROWS + t * TX + x)):
                 labels[x, t * 4 + c] = value
@@ -279,7 +281,7 @@
                     (row == iota((NAGG, LANES), 0).astype(F32)).astype(F32).astype(BF16)
                 )
 
-    def ghosts(ext):
+    def ghosts():
         for c in range(COMBOS):
             for b in range(BANDS):
                 ext[TX + 1, c, b] = shifted(ext[1, c, b], -1, 0, last_x)
@@ -302,7 +304,7 @@
             acc = new
         return acc
 
-    def operator_0(ext, x, finish):
+    def operator_0(x, finish):
         for pair in range(ZT // 2):
             cells = [(yt, 2 * pair + i) for i in range(2) for yt in range(YT)]
 
@@ -475,24 +477,26 @@
         def smooth(x, c_):
             for c in range(COMBOS):
                 for b in range(BANDS):
-                    value = basis[j, x, c, b] * factor
+                    value = work[x, c, b] * factor
                     basis[j, x, c, b] = value
-                    ext_a[x + 1, c, b] = winv[x, c, b] * value
+                    ext[x + 1, c, b] = winv[x, c, b] * value
             return c_
 
         lax.fori_loop(0, TX, smooth, 0)
-        ghosts(ext_a)
+        ghosts()
 
         def down(x, c_):
             def finish(pair, cells, values):
                 for b in range(BANDS):
-                    defects = [
-                        basis[j, x, yt * ZT + zt, b] - values[b][n]
-                        for n, (yt, zt) in enumerate(cells)
-                    ]
+                    defects = []
+                    for n, (yt, zt) in enumerate(cells):
+                        residual = basis[j, x, yt * ZT + zt, b]
+                        defect = residual - values[b][n]
+                        defects.append(defect)
+                        work[x, yt * ZT + zt, b] = residual + defect
                     sums[x, pair, b] = (defects[0] + defects[1]) + (defects[2] + defects[3])
 
-            operator_0(ext_a, x, finish)
+            operator_0(x, finish)
             return c_
 
         lax.fori_loop(0, TX, down, 0)
@@ -503,8 +507,6 @@
                     value = 0.125 * (sums[2 * x, z, b] + sums[2 * x + 1, z, b])
                     res_1[x, z, b] = value
                     cor_1[x, z, b] = winv_1[x, z, b] * value
-
-        held = {}
 
         def defect_1(x, values):
             for b in range(BANDS):
@@ -550,83 +552,107 @@
 
         operator_1(cor_1, post_1)
 
-        def prolong(x, c_):
-            for c in range(COMBOS):
+        for x in range(2):
+            for z in range(3):
+
+                def neighbours(b):
+                    mid = sums[x, z, b]
+                    near_x = sums[1 - x, z, b]
+                    if x == 0:
+                        low_x, high_x = shifted(near_x, 1, 0, first_x), near_x
+                    else:
+                        low_x, high_x = near_x, shifted(near_x, -1, 0, last_x)
+                    low_y, high_y = shifted(mid, ZQ, 1, first_y), shifted(mid, -ZQ, 1, last_y)
+                    low_z = sums[x, z - 1, b] if z > 0 else shifted(sums[x, 2, b], 1, 1, first_z)
+                    high_z = sums[x, z + 1, b] if z < 2 else shifted(sums[x, 0, b], -1, 1, last_z)
+                    return [
+                        [mid - low_x, mid - high_x],
+                        [mid - low_y, mid - high_y],
+                        [mid - low_z, mid - high_z],
+                    ]
+
+                acc = [None] * 3
                 for b in range(BANDS):
-                    ext_a[x + 1, c, b] = ext_a[x + 1, c, b] + sums[x // 2, (c % ZT) // 2, b]
+                    differences = neighbours(b)
+                    for d in range(3):
+                        new = []
+                        for a in range(BANDS):
+                            c = coupling(d, a, b)
+                            row = [c * value for value in differences[d]]
+                            new.append(
+                                row if b == 0 else [acc[d][a][i] + row[i] for i in range(2)]
+                            )
+                        acc[d] = new
+                for d in range(3):
+                    for side in range(2):
+                        for a in range(BANDS):
+                            sides[d, side, x, z, a] = acc[d][a][side]
+
+        def up(x, c_):
+            for z in range(3):
+                for b in range(BANDS):
+                    coarse_value = sums[x // 2, z, b]
+                    along_x = sides[0, x % 2, x // 2, z, b]
+                    for yt in range(YT):
+                        along_xy = along_x + sides[1, yt, x // 2, z, b]
+                        for i in range(2):
+                            c = yt * ZT + 2 * z + i
+                            applied = (
+                                along_xy
+                                + sides[2, i, x // 2, z, b]
+                                + pots[x, c, b] * coarse_value
+                            )
+                            ext[x + 1, c, b] = coarse_value + winv[x, c, b] * (
+                                work[x, c, b] - applied
+                            )
             return c_
 
-        lax.fori_loop(0, TX, prolong, 0)
-        ghosts(ext_a)
-
-        def up(x, c_):
+        lax.fori_loop(0, TX, up, 0)
+        ghosts()
+
+        def apply(x, parts):
+            parts = list(parts)
+
             def finish(pair, cells, values):
                 for b in range(BANDS):
                     for n, (yt, zt) in enumerate(cells):
                         c = yt * ZT + zt
-                        ext_b[x + 1, c, b] = ext_a[x + 1, c, b] + winv[x, c, b] * (
-                            basis[j, x, c, b] - values[b][n]
-                        )
-
-            operator_0(ext_a, x, finish)
-            return c_
-
-        lax.fori_loop(0, TX, up, 0)
-        ghosts(ext_b)
-
-        def apply(x, c_):
-            def finish(pair, cells, values):
-                for b in range(BANDS):
-                    for n, (yt, zt) in enumerate(cells):
-                        basis[j + 1, x, yt * ZT + zt, b] = values[b][n]
-
-            operator_0(ext_b, x, finish)
+                        fresh[x, c, b] = values[b][n]
+                        for i in range(ITERS):
+                            parts[i] = parts[i] + basis[i, x, c, b] * values[b][n]
+
+            operator_0(x, finish)
             quarter = one_lane // GROUP
             for b in range(BANDS):
                 for t in range(TILES):
                     merged = None
                     for i in range(4):
                         moved = pltpu.roll(
-                            ext_b[x + 1, t * 4 + i, b], (GROUP * i + lanes - GROUP * my_y) % lanes, 1
+                            ext[x + 1, t * 4 + i, b], (GROUP * i + lanes - GROUP * my_y) % lanes, 1
                         )[:, :LANES]
                         merged = moved if i == 0 else jnp.where(quarter == i, moved, merged)
                     kept[j, x, b * TILES + t] = merged
-            return c_
-
-        lax.fori_loop(0, TX, apply, 0)
-
-        def project(i, c_):
-            def body(x, parts):
-                parts = list(parts)
-                for c in range(COMBOS):
-                    for b in range(BANDS):
-                        n = (c * BANDS + b) % 4
-                        parts[n] = parts[n] + basis[i, x, c, b] * basis[j + 1, x, c, b]
-                return tuple(parts)
-
-            parts = lax.fori_loop(0, TX, body, (jnp.zeros(plane, F32),) * 4)
-            hess[i * ITERS + j] = total_of((parts[0] + parts[1]) + (parts[2] + parts[3]))
-            return c_
-
-        lax.fori_loop(0, j + 1, project, 0)
-
-        def subtract(i, c_):
-            weight = hess[i * ITERS + j]
-
-            def body(x, parts):
-                parts = list(parts)
-                for c in range(COMBOS):
-                    for b in range(BANDS):
-                        n = (c * BANDS + b) % 4
-                        value = basis[j + 1, x, c, b] - weight * basis[i, x, c, b]
-                        basis[j + 1, x, c, b] = value
-                        parts[n] = parts[n] + value * value
-                return tuple(parts)
-
-            parts = lax.fori_loop(0, TX, body, (jnp.zeros(plane, F32),) * 4)
-            return (parts[0] + parts[1]) + (parts[2] + parts[3])
-
-        total = lax.fori_loop(0, j + 1, subtract, jnp.zeros(plane, F32))
+            return tuple(parts)
+
+        parts = lax.fori_loop(0, TX, apply, (jnp.zeros(plane, F32),) * ITERS)
+        projections = [total_of(part) for part in parts]
+        for i in range(ITERS):
+            hess[i * ITERS + j] = projections[i]
+
+        def subtract(x, parts):
+            parts = list(parts)
+            for c in range(COMBOS):
+                for b in range(BANDS):
+                    n = (c * BANDS + b) % 4
+                    value = fresh[x, c, b]
+                    for i in range(ITERS):
+                        value = value - projections[i] * basis[i, x, c, b]
+                    work[x, c, b] = value
+                    parts[n] = parts[n] + value * value
+            return tuple(parts)
+
+        parts = lax.fori_loop(0, TX, subtract, (jnp.zeros(plane, F32),) * 4)
+        total = (parts[0] + parts[1]) + (parts[2] + parts[3])
         norm = jnp.sqrt(total_of(total))
         hess[(j + 1) * ITERS + j] = norm
         scale[...] = 1.0 / norm
@@ -683,6 +709,7 @@
 
 
 VMEM_SPEC = pl.BlockSpec(memory_space=pltpu.VMEM)
+HBM_SPEC = pl.BlockSpec(memory_space=pltpu.HBM)
 ANY_SPEC = pl.BlockSpec(memory_space=pl.ANY)
 SMEM_SPEC = pl.BlockSpec(memory_space=pltpu.SMEM)
 
@@ -708,7 +735,7 @@
     packed = pl.pallas_call(
         functools.partial(pack_kernel, groups),
         out_shape=[row_shape] * VECS,
-        in_specs=[ANY_SPEC] * 3,
+        in_specs=[HBM_SPEC] * 3,
         out_specs=[VMEM_SPEC] * VECS,
         scratch_shapes=[
             pltpu.VMEM((VECS * count + 8, CELLS), F32),
@@ -720,16 +747,8 @@
         compiler_params=pltpu.CompilerParams(vmem_limit_bytes=8 * 2**20),
         name="pack",
     )(right_hand, region_labels, aggregate_map)
+    packed, coarse_inverse = lax.optimization_barrier((packed, coarse_inverse))
     parts = [packed[0]] + [exchanged(packed[k], k * stride) for k in range(1, VECS)]
-    block = jnp.stack(parts)
-    steps = [("gy", i) for i in range(bits(size_y) - 1, 0, -1)]
-    steps += [("gx", i) for i in range(bits(groups))]
-    steps += [("gy", 0)]
-    pieces = [block]
-    for axis, bit in steps:
-        mask = (1 << bit) * (size_y if axis == "gx" else 1)
-        pieces.append(exchanged(jnp.concatenate(pieces, axis=0), mask))
-
     inverse = pl.pallas_call(
         order_kernel,
         out_shape=jax.ShapeDtypeStruct((BANDS, NAGG, BANDS * LANES), F32),
@@ -742,35 +761,46 @@
         name="order",
     )(coarse_inverse)
 
+    block, inverse = lax.optimization_barrier((jnp.stack(parts), inverse))
+    steps = [("gy", i) for i in range(bits(size_y) - 1, 0, -1)]
+    steps += [("gx", i) for i in range(bits(groups))]
+    steps += [("gy", 0)]
+    pieces = [block]
+    for axis, bit in steps:
+        mask = (1 << bit) * (size_y if axis == "gx" else 1)
+        pieces.append(exchanged(jnp.concatenate(pieces, axis=0), mask))
+
     lanes = size_y * GROUP
     plane = (size_x, lanes)
     count_2 = 3 * (lanes // LANES) * size_x
     vmem = lambda *shape: pltpu.VMEM(shape + plane, F32)
     scratch = [
-            pltpu.VMEM((ROWS, size_y, size_x, LANES), F32),
-            vmem(ITERS + 1, TX, COMBOS, BANDS),
-            vmem(TX + 2, COMBOS, BANDS),
-            vmem(TX + 2, COMBOS, BANDS),
-            vmem(TX, COMBOS, BANDS),
-            vmem(TX, COMBOS, BANDS),
-            vmem(TX, 3, BANDS),
-            vmem(TX, COMBOS),
-            vmem(3),
-            pltpu.VMEM((NAGG, count_2 * LANES), BF16),
-            vmem(2, 3, BANDS),
-            vmem(2, 3, BANDS),
-            vmem(3, BANDS),
-            vmem(3, BANDS),
-            vmem(2, 3, BANDS),
-            vmem(2, 3, BANDS),
-            vmem(3, BANDS),
-            vmem(3, BANDS),
-            pltpu.VMEM((count_2 * 8, LANES), F32),
-            pltpu.VMEM((ITERS, TX, BANDS * TILES, size_x, LANES), F32),
-            vmem((ITERS + 1) * ITERS),
-            vmem(),
-            pltpu.VMEM((VECS, FIELD_ROWS, LANES), F32),
-            pltpu.SemaphoreType.DMA((devices,)),
+        pltpu.VMEM((ROWS, size_y, size_x, LANES), F32),
+        vmem(ITERS, TX, COMBOS, BANDS),
+        vmem(TX, COMBOS, BANDS),
+        vmem(TX + 2, COMBOS, BANDS),
+        vmem(TX, COMBOS, BANDS),
+        vmem(TX, COMBOS, BANDS),
+        vmem(TX, COMBOS, BANDS),
+        vmem(TX, 3, BANDS),
+        vmem(TX, COMBOS),
+        vmem(3),
+        pltpu.VMEM((NAGG, count_2 * LANES), BF16),
+        vmem(2, 3, BANDS),
+        vmem(2, 3, BANDS),
+        vmem(3, BANDS),
+        vmem(3, BANDS),
+        vmem(3, 2, 2, 3, BANDS),
+        vmem(2, 3, BANDS),
+        vmem(2, 3, BANDS),
+        vmem(3, BANDS),
+        vmem(3, BANDS),
+        pltpu.VMEM((count_2 * 8, LANES), F32),
+        pltpu.VMEM((ITERS, TX, BANDS * TILES, size_x, LANES), F32),
+        vmem((ITERS + 1) * ITERS),
+        vmem(),
+        pltpu.VMEM((VECS, FIELD_ROWS, LANES), F32),
+        pltpu.SemaphoreType.DMA((devices,)),
     ]
     held = sum(math.prod(ref.shape) * 4 for ref in scratch)
     answers = pl.pallas_call(

time: 81.9 us -> 71.8 us (0.88)
  Pallas kernels: 47.5 us -> 36.1 us
  local copies, waits for them, and re-layouts: 2.41 us -> 3.33 us
    pallas_call x1, Pallas kernels: 40.8 us -> 29.4 us  [shards(): pl.pallas_call(functools.partial(solve_kernel, size_x, size_y, tuple(step...]
    unnamed x17 -> x12, local copies, waits for them, and re-layouts: 2.38 us -> 3.33 us
  transfers between devices with their start and end apart: 9 -> 9, of which waited for: 6 -> 6; matrix products, arithmetic and copies ran while one was open for 0% -> 0% of each run, Pallas kernels for 5% -> 6%
where the time goes in v2:
time: 71.8 us; the launch traced here: 71.6 us
  Pallas kernels  36.1 us (50%)
  waiting for transfers between devices  18.6 us (26%)
  starting transfers between devices  13.3 us (19%)
  local copies, waits for them, and re-layouts  3.33 us (5%)
    pallas_call x1, Pallas kernels, shards(): pl.pallas_call(functools.partial(solve_kernel, size_x, size_y, tuple(step...  29.4 us
    ppermute x9, waiting for transfers between devices, exchanged(): return lax.ppermute(value, names, [(i, i ^ mask) for i in range(devices)])  18.6 us
    ppermute x9, starting transfers between devices, exchanged(): return lax.ppermute(value, names, [(i, i ^ mask) for i in range(devices)])  13.3 us
    pallas_call x1, Pallas kernels, shards(): pl.pallas_call(order_kernel, out_shape=jax.ShapeDtypeStruct((BANDS, NAGG,...  4.43 us
    unnamed x12, local copies, waits for them, and re-layouts  3.33 us
  transfers between devices with their start and end apart: 9, of which 6 were waited for; matrix products, arithmetic and copies ran while one was open for 0% of the time, Pallas kernels for 6%

profile of v2, /device:TPU:0, one launch (start us, length us, event | category | flops | bytes accessed | tf_op | source)
XLA Modules:
  0.0 71.6 jit_solution(4307160507801148826)
XLA Ops:
  0.0 0.0 copy-start.1
  0.0 0.9 %copy-done.1 = f32[4,6,4,384]{3,2,1,0:T(4,128)S(1)} copy-done((f32[4,6,4,384]{3,2,1,0:T(4,128)S(1)}, f32[4,6,4,384]{3,2,1,0:T(4,128)}, u32[]{:S(2)}) %copy-start.1) | copy-done | bytes 147480
  0.9 0.0 copy-start.3
  0.9 0.7 copy-done.3
  1.6 0.0 copy-start.5
  1.6 0.7 copy-done.5
  2.3 0.9 %pack.1 = (f32[88,128]{1,0:T(8,128)S(1)}, f32[88,128]{1,0:T(8,128)S(1)}, f32[88,128]{1,0:T(8,128)S(1)}, f32[88,128]{1,0:T(8,128)S(1)}) custom-call(f32[4,6,4,384]{3,2,1,0:T(4,128)S(1)} %copy-done.1, s32[4,384]{1,0:T(4,128)S(1)} %copy-done.3, s32[1,24]{1,0:T(1,128)S(1)} %copy-done.5), custom_call_target="tpu_custom_call" | custom-call | tf_op jit(solution)/shard_map/pack/pallas_call | solution.py:735
  3.2 3.1 %collective-permute-start = (f32[88,128]{1,0:T(8,128)S(1)}, f32[88,128]{1,0:T(8,128)S(1)}, u32[]{:S(2)}, u32[]{:S(2)}) collective-permute-start(f32[88,128]{1,0:T(8,128)S(1)} %get-tuple-element.25), channel_id=1, source_target_pairs={{0,8},{1,9},{2,10},{3,11},{4,12},{5,13},{6,14},{7,15},{8,0},{9,1},... | collective-permute-start | bytes 135176 | tf_op jit(solution)/shard_map/ppermute | solution.py:731
  6.3 2.6 %collective-permute-start.1 = (f32[88,128]{1,0:T(8,128)S(1)}, f32[88,128]{1,0:T(8,128)S(1)}, u32[]{:S(2)}, u32[]{:S(2)}) collective-permute-start(f32[88,128]{1,0:T(8,128)S(1)} %get-tuple-element.26), channel_id=1, source_target_pairs={{0,16},{1,17},{2,18},{3,19},{4,20},{5,21},{6,22},{7,23},{8,24},{9,... | collective-permute-start | bytes 135176 | tf_op jit(solution)/shard_map/ppermute | solution.py:731
  8.9 0.0 collective-permute-start.2
  8.9 0.0 copy-start
  8.9 1.1 %copy-done = f32[384,384]{1,0:T(8,128)S(1)} copy-done((f32[384,384]{1,0:T(8,128)S(1)}, f32[384,384]{1,0:T(8,128)}, u32[]{:S(2)}) %copy-start) | copy-done | bytes 589848
  9.9 4.4 %order.1.refs_6_ = f32[6,64,768]{2,1,0:T(8,128)S(1)} custom-call(f32[384,384]{1,0:T(8,128)S(1)} %copy-done), custom_call_target="tpu_custom_call" | custom-call | flops 339738624 | bytes 2097152 | tf_op jit(solution)/shard_map/order/pallas_call | solution.py:752
  14.4 0.0 collective-permute-done
  14.4 0.0 collective-permute-done.1
  14.4 0.3 collective-permute-done.2
  14.7 0.0 copy-start.2
  14.7 0.0 copy-start.4
  14.7 1.6 %collective-permute-start.3 = (f32[4,88,128]{2,1,0:T(8,128)S(1)}, f32[4,88,128]{2,1,0:T(8,128)S(1)}, u32[]{:S(2)}, u32[]{:S(2)}) collective-permute-start(f32[4,88,128]{2,1,0:T(8,128)S(1)} %pad_maximum_fusion.2.refs_0_), channel_id=1, source_target_pairs={{0,2},{1,3},{2,0},{3,1},{4,6},{5,7},{6,4},{7,5},{8,10},{9,11},{10,... | collective-permute-start | bytes 540680 | tf_op jit(solution)/shard_map/ppermute | solution.py:731
  16.3 4.0 %collective-permute-done.3.refs_1_ = f32[4,88,128]{2,1,0:T(8,128)S(1)} collective-permute-done((f32[4,88,128]{2,1,0:T(8,128)S(1)}, f32[4,88,128]{2,1,0:T(8,128)S(1)}, u32[]{:S(2)}, u32[]{:S(2)}) %collective-permute-start.3) | collective-permute-done | bytes 180256 | tf_op jit(solution)/shard_map/ppermute | solution.py:731
  20.3 1.6 %collective-permute-start.4 = (f32[8,88,128]{2,1,0:T(8,128)S(1)}, f32[8,88,128]{2,1,0:T(8,128)S(1)}, u32[]{:S(2)}, u32[]{:S(2)}) collective-permute-start(f32[8,88,128]{2,1,0:T(8,128)S(1)} %pad_maximum_fusion.1), channel_id=1, source_target_pairs={{0,4},{1,5},{2,6},{3,7},{4,0},{5,1},{6,2},{7,3},{8,12},{9,13},{10,... | collective-permute-start | bytes 1081352 | tf_op jit(solution)/shard_map/ppermute | solution.py:731
  21.9 6.6 %collective-permute-done.4.refs_2_ = f32[8,88,128]{2,1,0:T(8,128)S(1)} collective-permute-done((f32[8,88,128]{2,1,0:T(8,128)S(1)}, f32[8,88,128]{2,1,0:T(8,128)S(1)}, u32[]{:S(2)}, u32[]{:S(2)}) %collective-permute-start.4) | collective-permute-done | bytes 360480 | tf_op jit(solution)/shard_map/ppermute | solution.py:731
  28.6 0.1 collective-permute-start.5
  28.7 2.2 %collective-permute-done.5.refs_3_ = f32[16,88,128]{2,1,0:T(8,128)S(1)} collective-permute-done((f32[16,88,128]{2,1,0:T(8,128)S(1)}, f32[16,88,128]{2,1,0:T(8,128)S(1)}, u32[]{:S(2)}, u32[]{:S(2)}) %collective-permute-start.5) | collective-permute-done | bytes 720928 | tf_op jit(solution)/shard_map/ppermute | solution.py:731
  30.8 0.0 copy-done.2
  30.8 0.0 copy-done.4
  30.9 29.4 %solve.1 = (f32[72,128]{1,0:T(8,128)S(1)}, f32[72,128]{1,0:T(8,128)S(1)}, f32[72,128]{1,0:T(8,128)S(1)}, f32[72,128]{1,0:T(8,128)S(1)}) custom-call(f32[4,88,128]{2,1,0:T(8,128)S(1)} %pad_maximum_fusion.2.refs_0_, f32[4,88,128]{2,1,0:T(8,128)S(1)} %collective-permute-done.3.refs_1_, f32[8,88,128]{2,1,0:T(8,128)S(1)} %collective-permute-done.4.refs_2_, ...), custom_call_target="tpu_custom_call" | custom-call | tf_op jit(solution)/shard_map/solve/pallas_call | solution.py:806
  60.3 0.7 collective-permute-start.6
  61.0 3.5 %collective-permute-start.7 = (f32[72,128]{1,0:T(8,128)S(1)}, f32[72,128]{1,0:T(8,128)S(1)}, u32[]{:S(2)}, u32[]{:S(2)}) collective-permute-start(f32[72,128]{1,0:T(8,128)S(1)} %get-tuple-element.33), channel_id=1, source_target_pairs={{0,16},{1,17},{2,18},{3,19},{4,20},{5,21},{6,22},{7,23},{8,24},{9,... | collective-permute-start | bytes 110600 | tf_op jit(solution)/shard_map/ppermute | solution.py:731
  64.5 0.3 collective-permute-start.8
  64.8 0.0 collective-permute-done.6.refs_1_
  64.8 2.2 %collective-permute-done.7.refs_2_ = f32[72,128]{1,0:T(8,128)S(1)} collective-permute-done((f32[72,128]{1,0:T(8,128)S(1)}, f32[72,128]{1,0:T(8,128)S(1)}, u32[]{:S(2)}, u32[]{:S(2)}) %collective-permute-start.7) | collective-permute-done | bytes 36896 | tf_op jit(solution)/shard_map/ppermute | solution.py:731
  66.9 3.3 %collective-permute-done.8.refs_3_ = f32[72,128]{1,0:T(8,128)S(1)} collective-permute-done((f32[72,128]{1,0:T(8,128)S(1)}, f32[72,128]{1,0:T(8,128)S(1)}, u32[]{:S(2)}, u32[]{:S(2)}) %collective-permute-start.8) | collective-permute-done | bytes 36896 | tf_op jit(solution)/shard_map/ppermute | solution.py:731
  70.2 1.3 %unpack.1 = f32[4,6,4,384]{3,2,1,0:T(4,128)} custom-call(f32[72,128]{1,0:T(8,128)S(1)} %get-tuple-element.31.refs_0_, f32[72,128]{1,0:T(8,128)S(1)} %collective-permute-done.6.refs_1_, f32[72,128]{1,0:T(8,128)S(1)} %collective-permute-done.7.refs_2_, f32[72,128]{1,0:T(8,128)S(1)} %collective-permute-done.8.refs_3_), custom_call_target="tpu_custom_call" | custom-call | tf_op jit(solution)/shard_map/unpack/pallas_call | solution.py:818
  (3 shorter events, 0.1 us)
Async XLA Ops:
  0.0 0.9 %copy-start.1 = (f32[4,6,4,384]{3,2,1,0:T(4,128)S(1)}, f32[4,6,4,384]{3,2,1,0:T(4,128)}, u32[]{:S(2)}) copy-start(f32[4,6,4,384]{3,2,1,0:T(4,128)} %right_hbm.1) | copy-start | bytes 442372
  0.9 0.7 copy-start.3
  1.6 0.7 copy-start.5
  3.2 11.2 %collective-permute-start = (f32[88,128]{1,0:T(8,128)S(1)}, f32[88,128]{1,0:T(8,128)S(1)}, u32[]{:S(2)}, u32[]{:S(2)}) collective-permute-start(f32[88,128]{1,0:T(8,128)S(1)} %get-tuple-element.25), channel_id=1, source_target_pairs={{0,8},{1,9},{2,10},{3,11},{4,12},{5,13},{6,14},{7,15},{8,0},{9,1},... | collective-permute-start | bytes 135176 | tf_op jit(solution)/shard_map/ppermute | solution.py:731
  6.3 8.1 %collective-permute-start.1 = (f32[88,128]{1,0:T(8,128)S(1)}, f32[88,128]{1,0:T(8,128)S(1)}, u32[]{:S(2)}, u32[]{:S(2)}) collective-permute-start(f32[88,128]{1,0:T(8,128)S(1)} %get-tuple-element.26), channel_id=1, source_target_pairs={{0,16},{1,17},{2,18},{3,19},{4,20},{5,21},{6,22},{7,23},{8,24},{9,... | collective-permute-start | bytes 135176 | tf_op jit(solution)/shard_map/ppermute | solution.py:731
  8.9 5.8 %collective-permute-start.2 = (f32[88,128]{1,0:T(8,128)S(1)}, f32[88,128]{1,0:T(8,128)S(1)}, u32[]{:S(2)}, u32[]{:S(2)}) collective-permute-start(f32[88,128]{1,0:T(8,128)S(1)} %get-tuple-element.27), channel_id=1, source_target_pairs={{0,24},{1,25},{2,26},{3,27},{4,28},{5,29},{6,30},{7,31},{8,16},{9,... | collective-permute-start | bytes 135176 | tf_op jit(solution)/shard_map/ppermute | solution.py:731
  8.9 1.1 %copy-start = (f32[384,384]{1,0:T(8,128)S(1)}, f32[384,384]{1,0:T(8,128)}, u32[]{:S(2)}) copy-start(f32[384,384]{1,0:T(8,128)} %source_ref) | copy-start | bytes 1769476
  14.7 16.1 %copy-start.2 = (f32[3,6,6]{2,1,0:T(8,128)S(1)}, f32[3,6,6]{2,1,0:T(8,128)}, u32[]{:S(2)}) copy-start(f32[3,6,6]{2,1,0:T(8,128)} %refs_4_.1) | copy-start | bytes 1300
  14.7 16.1 %copy-start.4 = (f32[3,6]{1,0:T(4,128)S(1)}, f32[3,6]{1,0:T(4,128)}, u32[]{:S(2)}) copy-start(f32[3,6]{1,0:T(4,128)} %refs_5_.1) | copy-start | bytes 220
  14.7 5.6 %collective-permute-start.3 = (f32[4,88,128]{2,1,0:T(8,128)S(1)}, f32[4,88,128]{2,1,0:T(8,128)S(1)}, u32[]{:S(2)}, u32[]{:S(2)}) collective-permute-start(f32[4,88,128]{2,1,0:T(8,128)S(1)} %pad_maximum_fusion.2.refs_0_), channel_id=1, source_target_pairs={{0,2},{1,3},{2,0},{3,1},{4,6},{5,7},{6,4},{7,5},{8,10},{9,11},{10,... | collective-permute-start | bytes 540680 | tf_op jit(solution)/shard_map/ppermute | solution.py:731
  20.3 8.2 %collective-permute-start.4 = (f32[8,88,128]{2,1,0:T(8,128)S(1)}, f32[8,88,128]{2,1,0:T(8,128)S(1)}, u32[]{:S(2)}, u32[]{:S(2)}) collective-permute-start(f32[8,88,128]{2,1,0:T(8,128)S(1)} %pad_maximum_fusion.1), channel_id=1, source_target_pairs={{0,4},{1,5},{2,6},{3,7},{4,0},{5,1},{6,2},{7,3},{8,12},{9,13},{10,... | collective-permute-start | bytes 1081352 | tf_op jit(solution)/shard_map/ppermute | solution.py:731
  28.6 2.3 %collective-permute-start.5 = (f32[16,88,128]{2,1,0:T(8,128)S(1)}, f32[16,88,128]{2,1,0:T(8,128)S(1)}, u32[]{:S(2)}, u32[]{:S(2)}) collective-permute-start(f32[16,88,128]{2,1,0:T(8,128)S(1)} %pad_maximum_fusion), channel_id=1, source_target_pairs={{0,1},{1,0},{2,3},{3,2},{4,5},{5,4},{6,7},{7,6},{8,9},{9,8},{10,11... | collective-permute-start | bytes 2162696 | tf_op jit(solution)/shard_map/ppermute | solution.py:731
  60.3 4.5 %collective-permute-start.6 = (f32[72,128]{1,0:T(8,128)S(1)}, f32[72,128]{1,0:T(8,128)S(1)}, u32[]{:S(2)}, u32[]{:S(2)}) collective-permute-start(f32[72,128]{1,0:T(8,128)S(1)} %get-tuple-element.32), channel_id=1, source_target_pairs={{0,8},{1,9},{2,10},{3,11},{4,12},{5,13},{6,14},{7,15},{8,0},{9,1},... | collective-permute-start | bytes 110600 | tf_op jit(solution)/shard_map/ppermute | solution.py:731
  61.0 5.9 %collective-permute-start.7 = (f32[72,128]{1,0:T(8,128)S(1)}, f32[72,128]{1,0:T(8,128)S(1)}, u32[]{:S(2)}, u32[]{:S(2)}) collective-permute-start(f32[72,128]{1,0:T(8,128)S(1)} %get-tuple-element.33), channel_id=1, source_target_pairs={{0,16},{1,17},{2,18},{3,19},{4,20},{5,21},{6,22},{7,23},{8,24},{9,... | collective-permute-start | bytes 110600 | tf_op jit(solution)/shard_map/ppermute | solution.py:731
  64.5 5.8 %collective-permute-start.8 = (f32[72,128]{1,0:T(8,128)S(1)}, f32[72,128]{1,0:T(8,128)S(1)}, u32[]{:S(2)}, u32[]{:S(2)}) collective-permute-start(f32[72,128]{1,0:T(8,128)S(1)} %get-tuple-element.34), channel_id=1, source_target_pairs={{0,24},{1,25},{2,26},{3,27},{4,28},{5,29},{6,30},{7,31},{8,16},{9,... | collective-permute-start | bytes 110600 | tf_op jit(solution)/shard_map/ppermute | solution.py:731

commit v3 on v2

--- a/solution.py
+++ b/solution.py
@@ -34,6 +34,9 @@
 ROWS = 88
 LANES = 128
 CELLS = TY * NZ
+SUBLANES = 8
+MIXED = 4 * BANDS * SUBLANES
+PARTS = 3 * BANDS * SUBLANES
 
 
 def source_lane(target):
@@ -106,32 +109,40 @@
             out_ref[own ^ k, b] = moved[first : first + TX]
 
 
+def split(value):
+    high = value.astype(BF16)
+    left = value - high.astype(F32)
+    middle = left.astype(BF16)
+    return high, middle, (left - middle.astype(F32)).astype(BF16)
+
+
 def order_kernel(source_ref, out_ref):
     size = NAGG * BANDS
-    column = iota((1, size), 1)
-    inputs = (iota((size, size), 0) == (column % NAGG) * BANDS + column // NAGG).astype(F32)
-    wide = iota((1, BANDS * LANES), 1)
-    place = wide % LANES
-    wanted = jnp.where(place < NAGG, place * BANDS + wide // LANES, -1)
-    outputs = (iota((size, BANDS * LANES), 0) == wanted).astype(F32)
-    turned = jnp.dot(source_ref[...], inputs, precision=HIGHEST, preferred_element_type=F32)
-    out_ref[...] = lax.dot_general(
-        turned,
-        outputs,
-        (((0,), (0,)), ((), ())),
-        precision=HIGHEST,
-        preferred_element_type=F32,
-    ).reshape(BANDS, NAGG, BANDS * LANES)
-
-
-def solve_kernel(size_x, size_y, steps, *refs):
-    count = len(steps) + 1
+    row, column = iota((size, 1), 0), iota((1, size), 1)
+    inputs = (iota((size, size), 1) == (row % NAGG) * BANDS + row // NAGG).astype(F32).astype(BF16)
+    outputs = (
+        (iota((size, size), 0) == (column % NAGG) * BANDS + column // NAGG).astype(F32).astype(BF16)
+    )
+    turned = sum(
+        lax.dot_general(inputs, part, (((1,), (1,)), ((), ())), preferred_element_type=F32)
+        for part in split(source_ref[...])
+    )
+    ordered = jnp.dot(
+        jnp.concatenate(split(turned), axis=0), outputs, preferred_element_type=F32
+    )
+    out_ref[...] = (ordered[:size] + ordered[size : 2 * size] + ordered[2 * size :]).reshape(
+        BANDS, NAGG, size
+    )
+
+
+def solve_kernel(size_x, size_y, places, *refs):
+    count = len(places)
     pieces, (coef, table, inverse_ref) = refs[:count], refs[count : count + 3]
     refs = refs[count - 1 :]
     outs = refs[4 : 4 + VECS]
     (
         scratch, basis, fresh, ext, work, pots, winv, sums, labels, aggs, onehot, pots_1, winv_1,
-        pots_2, winv_2, sides, res_1, cor_1, res_2, cor_2, cells_2, kept, hess, scale, answer, arrived,
+        pots_2, winv_2, sides, weights_f, weights, coupled, coupled_1, res_1, cor_1, res_2, cor_2, cells_2, kept, hess, scale, answer, arrived,
     ) = refs[4 + VECS :]
     groups = size_x // VECS
     lanes = size_y * GROUP
@@ -158,22 +169,52 @@
     def centre(band):
         return 2.0 * (coupling(0, band, band) + coupling(1, band, band) + coupling(2, band, band))
 
+    narrow = plane == (SUBLANES, LANES)
     copies = []
-    for i, piece in enumerate(pieces):
-        first = (1 << i) >> 1
-        for place in range(first, 1 << i):
-            mask_g = mask_y = 0
-            for n, (axis, bit) in enumerate(steps):
-                here = ((place >> n) & 1) << bit
-                mask_g, mask_y = (mask_g | here, mask_y) if axis == "gx" else (mask_g, mask_y | here)
-            for k in range(VECS):
-                target = scratch.at[:, my_y ^ mask_y, (own ^ k) * groups + (my_g ^ mask_g), :]
-                source = piece.at[(place - first) * VECS + k]
-                copies.append(pltpu.make_async_copy(source, target, arrived.at[len(copies)]))
+    for piece, blocks in zip(pieces, places):
+        for i, (k, mask_g, mask_y) in enumerate(blocks):
+            other_x, other_y = (own ^ k) * groups + (my_g ^ mask_g), my_y ^ mask_y
+            if narrow:
+                first = other_y * size_x + other_x
+                scratch[pl.ds(first, ROWS, stride=size_x * size_y), :] = piece[i]
+            else:
+                target = scratch.at[:, other_y, other_x, :]
+                copies.append(pltpu.make_async_copy(piece.at[i], target, arrived.at[len(copies)]))
     for copy in copies:
         copy.start()
-    for copy in copies:
-        copy.wait()
+
+    if narrow:
+        row = iota((SUBLANES, PARTS), 0)
+        column = iota((SUBLANES, PARTS), 1)
+        band, part = (column // SUBLANES) % BANDS, column // (BANDS * SUBLANES)
+        same = column % SUBLANES == row
+        for a in range(BANDS):
+            rows = [jnp.zeros((SUBLANES, PARTS), F32)] * 3
+            for b in range(BANDS):
+                rows = [jnp.where(band == b, coupling(d, a, b), rows[d]) for d in range(3)]
+            rows = [2.0 * (rows[0] + rows[1] + rows[2])] + [-value for value in rows]
+            for g, value in enumerate(rows):
+                value = jnp.where(same, value, 0.0)
+                high = value.astype(BF16).astype(F32)
+                weights_f[pl.ds((g * BANDS + a) * SUBLANES, SUBLANES), :] = jnp.where(
+                    part < 2, high, value - high
+                )
+        weights[...] = weights_f[...].astype(BF16)
+
+    def mix(columns):
+        parts = []
+        for values in columns:
+            value = jnp.concatenate(values, axis=0)
+            high = value.astype(BF16)
+            low = (value - high.astype(F32)).astype(BF16)
+            parts.append(jnp.concatenate([high, low, high], axis=0))
+        return jnp.dot(
+            weights[...], jnp.concatenate(parts, axis=1), preferred_element_type=F32
+        )
+
+    def block_of(g, a, n):
+        first = (g * BANDS + a) * SUBLANES
+        return slice(first, first + SUBLANES), slice(n * LANES, (n + 1) * LANES)
 
     one_lane = iota((size_x, LANES), 1)
     low_64, low_32 = one_lane < 64, one_lane % 64 < 32
@@ -181,7 +222,11 @@
     def regroup(row):
         result = []
         for h in range(halves):
-            g = [scratch[row, 4 * h + i] for i in range(4)]
+            if narrow:
+                first = row * size_y * size_x
+                g = [scratch[pl.ds(first + i * size_x, size_x), :] for i in range(4)]
+            else:
+                g = [scratch[row, 4 * h + i] for i in range(4)]
             for i in (0, 1):
                 low, high = g[i], g[i + 2]
                 g[i] = jnp.where(low_64, low, pltpu.roll(high, 64, 1))
@@ -208,6 +253,8 @@
                 labels[x, t * 4 + c] = value
         return total
 
+    for copy in copies:
+        copy.wait()
     total = lax.fori_loop(0, TX, load_field, jnp.zeros(plane, F32))
     for k, value in enumerate(regroup(AGG_ROW)[:3]):
         aggs[k] = value
@@ -215,8 +262,6 @@
     def total_of(value):
         return jnp.broadcast_to(jnp.sum(value, keepdims=True), plane)
 
-    beta = jnp.sqrt(total_of(total))
-    scale[...] = 1.0 / beta
     for i in range((ITERS + 1) * ITERS):
         hess[i] = jnp.zeros(plane, F32)
 
@@ -281,9 +326,17 @@
                     (row == iota((NAGG, LANES), 0).astype(F32)).astype(F32).astype(BF16)
                 )
 
+    beta = jnp.sqrt(total_of(total))
+    scale[...] = 1.0 / beta
+
     def ghosts():
         for c in range(COMBOS):
             for b in range(BANDS):
+                if narrow:
+                    rows, columns = block_of(1, b, c)
+                    coupled[TX + 1, rows, columns] = shifted(coupled[1, rows, columns], -1, 0, last_x)
+                    coupled[0, rows, columns] = shifted(coupled[TX, rows, columns], 1, 0, first_x)
+                    continue
                 ext[TX + 1, c, b] = shifted(ext[1, c, b], -1, 0, last_x)
                 ext[0, c, b] = shifted(ext[TX, c, b], 1, 0, first_x)
 
@@ -304,9 +357,70 @@
             acc = new
         return acc
 
+    def mix_some(x, c, row, columns):
+        if not narrow:
+            return
+        columns.append(row)
+        if len(columns) == 4:
+            coupled[x + 1, :, (c - 3) * LANES : (c + 1) * LANES] = mix(columns)
+            columns.clear()
+
+    def mixed_0(x, cells):
+        def at(g, a, yt, zt, dx=0):
+            rows, columns = block_of(g, a, yt * ZT + zt)
+            return coupled[x + 1 + dx, rows, columns]
+
+        values = []
+        for a in range(BANDS):
+            row = []
+            for yt, zt in cells:
+                value = at(0, a, yt, zt) + (at(1, a, yt, zt, 1) + at(1, a, yt, zt, -1))
+                partner = at(2, a, 1 - yt, zt)
+                if yt == 0:
+                    outer = shifted(partner, ZQ, 1, first_y)
+                else:
+                    outer = shifted(partner, -ZQ, 1, last_y)
+                value = value + (partner + outer)
+                if zt == 0:
+                    below = shifted(at(3, a, yt, ZT - 1), 1, 1, first_z)
+                else:
+                    below = at(3, a, yt, zt - 1)
+                if zt == ZT - 1:
+                    above = shifted(at(3, a, yt, 0), -1, 1, last_z)
+                else:
+                    above = at(3, a, yt, zt + 1)
+                value = value + (below + above)
+                row.append(value + pots[x, yt * ZT + zt, a] * ext[x + 1, yt * ZT + zt, a])
+            values.append(row)
+        return values
+
+    def mix_1(src):
+        coupled_1[...] = mix([[src[x, z, b] for b in range(BANDS)] for x in range(2) for z in range(3)])
+
+        def sides_of(d, a, x, z):
+            def at(x, z):
+                return coupled_1[block_of(d + 1, a, x * 3 + z)]
+
+            mid = at(x, z)
+            if d == 0:
+                other = at(1 - x, z)
+                if x == 0:
+                    return mid, shifted(other, 1, 0, first_x), other
+                return mid, other, shifted(other, -1, 0, last_x)
+            if d == 1:
+                return mid, shifted(mid, ZQ, 1, first_y), shifted(mid, -ZQ, 1, last_y)
+            below = at(x, z - 1) if z > 0 else shifted(at(x, 2), 1, 1, first_z)
+            above = at(x, z + 1) if z < 2 else shifted(at(x, 0), -1, 1, last_z)
+            return mid, below, above
+
+        return sides_of
+
     def operator_0(x, finish):
         for pair in range(ZT // 2):
             cells = [(yt, 2 * pair + i) for i in range(2) for yt in range(YT)]
+            if narrow:
+                finish(pair, cells, mixed_0(x, cells))
+                continue
 
             def neighbours(b):
                 def at(dx, yt, zt):
@@ -409,13 +523,6 @@
             [0.0625 * acc[b][z] + pots_2[z, b] * src[z, b] for z in range(3)] for b in range(BANDS)
         ]
 
-    def split(value):
-        high = value.astype(BF16)
-        left = value - high.astype(F32)
-        middle = left.astype(BF16)
-        low = (left - middle.astype(F32)).astype(BF16)
-        return jnp.concatenate([high, middle, low], axis=0)
-
     single = even_y & even_z
     count_2 = 3 * halves * size_x
 
@@ -436,16 +543,17 @@
         )
         partial = lax.dot_general(
             onehot[...],
-            split(wide),
+            jnp.concatenate(split(wide), axis=0),
             (((1,), (1,)), ((), ())),
             preferred_element_type=F32,
         )
         partial = partial[:, :8] + partial[:, 8:16] + partial[:, 16:24]
-        acc = [jnp.zeros((8, LANES), F32)] * BANDS
+        pairs = NAGG * BANDS // LANES
+        acc = [jnp.zeros((8, LANES), F32)] * pairs
         for b in range(BANDS):
             column = jnp.broadcast_to(partial[:, b : b + 1], (NAGG, LANES))
             for i in range(NAGG // 8):
-                for a in range(BANDS):
+                for a in range(pairs):
                     acc[a] = (
                         acc[a]
                         + inverse_ref[b, pl.ds(i * 8, 8), a * LANES : (a + 1) * LANES]
@@ -453,10 +561,12 @@
                     )
         band = iota((8, LANES), 0)
         solved = jnp.zeros((8, LANES), F32)
-        for a in range(BANDS):
-            solved = jnp.where(band == a, jnp.sum(acc[a], axis=0, keepdims=True), solved)
+        for a in range(pairs):
+            both = jnp.broadcast_to(jnp.sum(acc[a], axis=0, keepdims=True), (8, LANES))
+            solved = jnp.where(band == 2 * a, both, solved)
+            solved = jnp.where(band == 2 * a + 1, pltpu.roll(both, NAGG, 1), solved)
         spread_out = jnp.dot(
-            split(solved[:, :NAGG]), onehot[...], preferred_element_type=F32
+            jnp.concatenate(split(solved[:, :NAGG]), axis=0), onehot[...], preferred_element_type=F32
         )
         spread_out = spread_out[:8] + spread_out[8:16] + spread_out[16:24]
         for n in range(count_2):
@@ -471,18 +581,67 @@
 
         return correction
 
+    def prolonged_sides():
+        for x in range(2):
+            for z in range(3):
+
+                def neighbours(b):
+                    mid = sums[x, z, b]
+                    near_x = sums[1 - x, z, b]
+                    if x == 0:
+                        low_x, high_x = shifted(near_x, 1, 0, first_x), near_x
+                    else:
+                        low_x, high_x = near_x, shifted(near_x, -1, 0, last_x)
+                    low_y, high_y = shifted(mid, ZQ, 1, first_y), shifted(mid, -ZQ, 1, last_y)
+                    low_z = sums[x, z - 1, b] if z > 0 else shifted(sums[x, 2, b], 1, 1, first_z)
+                    high_z = sums[x, z + 1, b] if z < 2 else shifted(sums[x, 0, b], -1, 1, last_z)
+                    return [
+                        [mid - low_x, mid - high_x],
+                        [mid - low_y, mid - high_y],
+                        [mid - low_z, mid - high_z],
+                    ]
+
+                acc = [None] * 3
+                for b in range(BANDS):
+                    differences = neighbours(b)
+                    for d in range(3):
+                        new = []
+                        for a in range(BANDS):
+                            c = coupling(d, a, b)
+                            row = [c * value for value in differences[d]]
+                            new.append(
+                                row if b == 0 else [acc[d][a][i] + row[i] for i in range(2)]
+                            )
+                        acc[d] = new
+                for d in range(3):
+                    for side in range(2):
+                        for a in range(BANDS):
+                            sides[d, side, x, z, a] = acc[d][a][side]
+
+    def over_x(body, carry):
+        if not narrow:
+            return lax.fori_loop(0, TX, body, carry)
+        for x in range(TX):
+            carry = body(x, carry)
+        return carry
+
     def iteration(j, carry):
         factor = scale[...]
 
         def smooth(x, c_):
+            columns = []
             for c in range(COMBOS):
+                row = []
                 for b in range(BANDS):
                     value = work[x, c, b] * factor
                     basis[j, x, c, b] = value
-                    ext[x + 1, c, b] = winv[x, c, b] * value
+                    value = winv[x, c, b] * value
+                    ext[x + 1, c, b] = value
+                    row.append(value)
+                mix_some(x, c, row, columns)
             return c_
 
-        lax.fori_loop(0, TX, smooth, 0)
+        over_x(smooth, 0)
         ghosts()
 
         def down(x, c_):
@@ -499,7 +658,7 @@
             operator_0(x, finish)
             return c_
 
-        lax.fori_loop(0, TX, down, 0)
+        over_x(down, 0)
 
         for x in range(2):
             for z in range(3):
@@ -552,62 +711,38 @@
 
         operator_1(cor_1, post_1)
 
-        for x in range(2):
-            for z in range(3):
-
-                def neighbours(b):
-                    mid = sums[x, z, b]
-                    near_x = sums[1 - x, z, b]
-                    if x == 0:
-                        low_x, high_x = shifted(near_x, 1, 0, first_x), near_x
-                    else:
-                        low_x, high_x = near_x, shifted(near_x, -1, 0, last_x)
-                    low_y, high_y = shifted(mid, ZQ, 1, first_y), shifted(mid, -ZQ, 1, last_y)
-                    low_z = sums[x, z - 1, b] if z > 0 else shifted(sums[x, 2, b], 1, 1, first_z)
-                    high_z = sums[x, z + 1, b] if z < 2 else shifted(sums[x, 0, b], -1, 1, last_z)
-                    return [
-                        [mid - low_x, mid - high_x],
-                        [mid - low_y, mid - high_y],
-                        [mid - low_z, mid - high_z],
-                    ]
-
-                acc = [None] * 3
-                for b in range(BANDS):
-                    differences = neighbours(b)
-                    for d in range(3):
-                        new = []
+        if narrow:
+            sides_of = mix_1(sums)
+            for d in range(3):
+                for x in range(2):
+                    for z in range(3):
                         for a in range(BANDS):
-                            c = coupling(d, a, b)
-                            row = [c * value for value in differences[d]]
-                            new.append(
-                                row if b == 0 else [acc[d][a][i] + row[i] for i in range(2)]
-                            )
-                        acc[d] = new
-                for d in range(3):
-                    for side in range(2):
-                        for a in range(BANDS):
-                            sides[d, side, x, z, a] = acc[d][a][side]
+                            mid, low, high = sides_of(d, a, x, z)
+                            sides[d, 0, x, z, a] = low - mid
+                            sides[d, 1, x, z, a] = high - mid
+        else:
+            prolonged_sides()
 
         def up(x, c_):
-            for z in range(3):
-                for b in range(BANDS):
-                    coarse_value = sums[x // 2, z, b]
-                    along_x = sides[0, x % 2, x // 2, z, b]
-                    for yt in range(YT):
-                        along_xy = along_x + sides[1, yt, x // 2, z, b]
-                        for i in range(2):
-                            c = yt * ZT + 2 * z + i
-                            applied = (
-                                along_xy
-                                + sides[2, i, x // 2, z, b]
-                                + pots[x, c, b] * coarse_value
-                            )
-                            ext[x + 1, c, b] = coarse_value + winv[x, c, b] * (
-                                work[x, c, b] - applied
-                            )
+            columns = []
+            for yt in range(YT):
+                for zt in range(ZT):
+                    z, c = zt // 2, yt * ZT + zt
+                    row = []
+                    for b in range(BANDS):
+                        coarse_value = sums[x // 2, z, b]
+                        applied = (
+                            (sides[0, x % 2, x // 2, z, b] + sides[1, yt, x // 2, z, b])
+                            + sides[2, zt % 2, x // 2, z, b]
+                            + pots[x, c, b] * coarse_value
+                        )
+                        value = coarse_value + winv[x, c, b] * (work[x, c, b] - applied)
+                        ext[x + 1, c, b] = value
+                        row.append(value)
+                    mix_some(x, c, row, columns)
             return c_
 
-        lax.fori_loop(0, TX, up, 0)
+        over_x(up, 0)
         ghosts()
 
         def apply(x, parts):
@@ -634,7 +769,7 @@
                     kept[j, x, b * TILES + t] = merged
             return tuple(parts)
 
-        parts = lax.fori_loop(0, TX, apply, (jnp.zeros(plane, F32),) * ITERS)
+        parts = over_x(apply, (jnp.zeros(plane, F32),) * ITERS)
         projections = [total_of(part) for part in parts]
         for i in range(ITERS):
             hess[i * ITERS + j] = projections[i]
@@ -744,14 +879,14 @@
             pltpu.VMEM(aggregate_map.shape, jnp.int32),
             pltpu.SemaphoreType.DMA((3,)),
         ],
-        compiler_params=pltpu.CompilerParams(vmem_limit_bytes=8 * 2**20),
+        compiler_params=pltpu.CompilerParams(vmem_limit_bytes=60 * 2**20),
         name="pack",
     )(right_hand, region_labels, aggregate_map)
     packed, coarse_inverse = lax.optimization_barrier((packed, coarse_inverse))
     parts = [packed[0]] + [exchanged(packed[k], k * stride) for k in range(1, VECS)]
     inverse = pl.pallas_call(
         order_kernel,
-        out_shape=jax.ShapeDtypeStruct((BANDS, NAGG, BANDS * LANES), F32),
+        out_shape=jax.ShapeDtypeStruct((BANDS, NAGG, BANDS * NAGG), F32),
         in_specs=[VMEM_SPEC],
         out_specs=VMEM_SPEC,
         compiler_params=pltpu.CompilerParams(vmem_limit_bytes=16 * 2**20),
@@ -761,21 +896,36 @@
         name="order",
     )(coarse_inverse)
 
-    block, inverse = lax.optimization_barrier((jnp.stack(parts), inverse))
     steps = [("gy", i) for i in range(bits(size_y) - 1, 0, -1)]
     steps += [("gx", i) for i in range(bits(groups))]
-    steps += [("gy", 0)]
-    pieces = [block]
-    for axis, bit in steps:
-        mask = (1 << bit) * (size_y if axis == "gx" else 1)
-        pieces.append(exchanged(jnp.concatenate(pieces, axis=0), mask))
+    second, inverse = lax.optimization_barrier((jnp.stack(parts[2:]), inverse))
+    halves = [[jnp.stack(parts[:2])], [second]]
+    places = [[[(k, 0, 0) for k in (0, 1)]], [[(k, 0, 0) for k in (2, 3)]]]
+
+    def widen(half, axis, bit):
+        mask = 1 << bit
+        sent = halves[half][0] if len(halves[half]) == 1 else jnp.concatenate(halves[half])
+        halves[half].append(exchanged(sent, mask * (size_y if axis == "gx" else 1)))
+        mask_g, mask_y = (mask, 0) if axis == "gx" else (0, mask)
+        places[half].append(
+            [(k, g ^ mask_g, y ^ mask_y) for blocks in places[half] for k, g, y in blocks]
+        )
+
+    for first, last in zip(steps, steps[::-1]):
+        widen(0, *first)
+        widen(1, *last)
+    widen(0, "gy", 0)
+    widen(1, "gy", 0)
+    pieces = halves[0] + halves[1]
+    places = places[0] + places[1]
 
     lanes = size_y * GROUP
     plane = (size_x, lanes)
     count_2 = 3 * (lanes // LANES) * size_x
+    narrow = plane == (SUBLANES, LANES)
     vmem = lambda *shape: pltpu.VMEM(shape + plane, F32)
     scratch = [
-        pltpu.VMEM((ROWS, size_y, size_x, LANES), F32),
+        pltpu.VMEM((ROWS * devices, LANES) if narrow else (ROWS, size_y, size_x, LANES), F32),
         vmem(ITERS, TX, COMBOS, BANDS),
         vmem(TX, COMBOS, BANDS),
         vmem(TX + 2, COMBOS, BANDS),
@@ -791,6 +941,10 @@
         vmem(3, BANDS),
         vmem(3, BANDS),
         vmem(3, 2, 2, 3, BANDS),
+        pltpu.VMEM((MIXED, PARTS), F32),
+        pltpu.VMEM((MIXED, PARTS), BF16),
+        pltpu.VMEM((TX + 2, MIXED, COMBOS * LANES) if narrow else (8, LANES), F32),
+        pltpu.VMEM((MIXED, 2 * TILES * LANES), F32),
         vmem(2, 3, BANDS),
         vmem(2, 3, BANDS),
         vmem(3, BANDS),
@@ -804,9 +958,9 @@
     ]
     held = sum(math.prod(ref.shape) * 4 for ref in scratch)
     answers = pl.pallas_call(
-        functools.partial(solve_kernel, size_x, size_y, tuple(steps)),
+        functools.partial(solve_kernel, size_x, size_y, places),
         out_shape=[jax.ShapeDtypeStruct((FIELD_ROWS, LANES), F32)] * VECS,
-        in_specs=[ANY_SPEC] * len(pieces) + [SMEM_SPEC, SMEM_SPEC, VMEM_SPEC],
+        in_specs=[VMEM_SPEC if narrow else ANY_SPEC] * len(pieces) + [SMEM_SPEC, SMEM_SPEC, VMEM_SPEC],
         out_specs=[VMEM_SPEC] * VECS,
         scratch_shapes=scratch,
         compiler_params=pltpu.CompilerParams(

time: 71.8 us -> 58.2 us (0.81)
  Pallas kernels: 36.1 us -> 26.5 us
  waiting for transfers between devices: 18.6 us -> 13.7 us
  starting transfers between devices: 13.3 us -> 16.6 us
  local copies, waits for them, and re-layouts: 3.33 us -> 1.08 us
    pallas_call x1, Pallas kernels: 29.4 us -> 21.5 us  [shards(): pl.pallas_call(functools.partial(solve_kernel, size_x, size_y, places), o...]
    ppermute x9 -> x12, waiting for transfers between devices: 18.6 us -> 13.7 us  [exchanged(): return lax.ppermute(value, names, [(i, i ^ mask) for i in range(devices)])]
    ppermute x9 -> x12, starting transfers between devices: 13.3 us -> 16.6 us  [exchanged(): return lax.ppermute(value, names, [(i, i ^ mask) for i in range(devices)])]
    pallas_call x1, Pallas kernels: 4.43 us -> 1.51 us  [shards(): pl.pallas_call(order_kernel, out_shape=jax.ShapeDtypeStruct((BANDS, NAGG,...]
    unnamed x12 -> x8, local copies, waits for them, and re-layouts: 3.33 us -> 1.08 us
    pallas_call x1, Pallas kernels: 0.91 us -> 2.2 us  [shards(): pl.pallas_call(functools.partial(pack_kernel, groups), out_shape=[row_sha...]
  transfers between devices with their start and end apart: 9 -> 12, of which waited for: 6 -> 7; matrix products, arithmetic and copies ran while one was open for 0% -> 0% of each run, Pallas kernels for 6% -> 3%
where the time goes in v3:
time: 58.2 us; the launch traced here: 58 us
  Pallas kernels  26.5 us (46%)
  starting transfers between devices  16.6 us (29%)
  waiting for transfers between devices  13.7 us (24%)
  local copies, waits for them, and re-layouts  1.08 us (2%)
    pallas_call x1, Pallas kernels, shards(): pl.pallas_call(functools.partial(solve_kernel, size_x, size_y, places), o...  21.5 us
    ppermute x12, starting transfers between devices, exchanged(): return lax.ppermute(value, names, [(i, i ^ mask) for i in range(devices)])  16.6 us
    ppermute x12, waiting for transfers between devices, exchanged(): return lax.ppermute(value, names, [(i, i ^ mask) for i in range(devices)])  13.7 us
    pallas_call x1, Pallas kernels, shards(): pl.pallas_call(functools.partial(pack_kernel, groups), out_shape=[row_sha...  2.2 us
    pallas_call x1, Pallas kernels, shards(): pl.pallas_call(order_kernel, out_shape=jax.ShapeDtypeStruct((BANDS, NAGG,...  1.51 us
    pallas_call x1, Pallas kernels, shards(): pl.pallas_call(functools.partial(unpack_kernel, groups), out_shape=jax.Sh...  1.33 us
  transfers between devices with their start and end apart: 12, of which 7 were waited for; matrix products, arithmetic and copies ran while one was open for 0% of the time, Pallas kernels for 3%

profile of v3, /device:TPU:0, one launch (start us, length us, event | category | flops | bytes accessed | tf_op | source)
XLA Modules:
  0.0 58.0 jit_solution(14961573718787776991)
XLA Ops:
  0.0 2.2 %pack.1 = (f32[88,128]{1,0:T(8,128)}, f32[88,128]{1,0:T(8,128)}, f32[88,128]{1,0:T(8,128)}, f32[88,128]{1,0:T(8,128)}) custom-call(f32[4,6,4,384]{3,2,1,0:T(4,128)} %right_hbm.1, s32[4,384]{1,0:T(4,128)} %labels_hbm.1, s32[1,24]{1,0:T(1,128)} %agg_hbm.1), custom_call_target="tpu_custom_call" | custom-call | tf_op jit(solution)/shard_map/pack/pallas_call | solution.py:870
  2.2 3.1 %collective-permute-start = (f32[88,128]{1,0:T(8,128)}, f32[88,128]{1,0:T(8,128)S(1)}, u32[]{:S(2)}, u32[]{:S(2)}) collective-permute-start(f32[88,128]{1,0:T(8,128)} %get-tuple-element.25), channel_id=1, source_target_pairs={{0,8},{1,9},{2,10},{3,11},{4,12},{5,13},{6,14},{7,15},{8,0},{9,1},... | collective-permute-start | bytes 135176 | tf_op jit(solution)/shard_map/ppermute | solution.py:866
  5.3 2.6 %collective-permute-start.4 = (f32[88,128]{1,0:T(8,128)}, f32[88,128]{1,0:T(8,128)S(1)}, u32[]{:S(2)}, u32[]{:S(2)}) collective-permute-start(f32[88,128]{1,0:T(8,128)} %get-tuple-element.26), channel_id=1, source_target_pairs={{0,16},{1,17},{2,18},{3,19},{4,20},{5,21},{6,22},{7,23},{8,24},{9,... | collective-permute-start | bytes 135176 | tf_op jit(solution)/shard_map/ppermute | solution.py:866
  7.9 0.0 collective-permute-start.5
  7.9 0.0 copy-start.2
  7.9 1.1 %copy-done.2 = f32[384,384]{1,0:T(8,128)S(1)} copy-done((f32[384,384]{1,0:T(8,128)S(1)}, f32[384,384]{1,0:T(8,128)}, u32[]{:S(2)}) %copy-start.2) | copy-done | bytes 589848
  9.0 0.0 copy-start.3
  9.0 1.5 %order.1.refs_10_ = f32[6,64,384]{2,1,0:T(8,128)S(1)} custom-call(f32[384,384]{1,0:T(8,128)S(1)} %copy-done.2), custom_call_target="tpu_custom_call" | custom-call | flops 339738624 | bytes 2097152 | tf_op jit(solution)/shard_map/order/pallas_call | solution.py:887
  10.5 0.0 collective-permute-done
  10.5 0.0 copy-done.3
  10.5 1.8 %collective-permute-start.1 = (f32[2,88,128]{2,1,0:T(8,128)S(1)}, f32[2,88,128]{2,1,0:T(8,128)S(1)}, u32[]{:S(2)}, u32[]{:S(2)}) collective-permute-start(f32[2,88,128]{2,1,0:T(8,128)S(1)} %pad_maximum_fusion.4.refs_0_), channel_id=1, source_target_pairs={{0,2},{1,3},{2,0},{3,1},{4,6},{5,7},{6,4},{7,5},{8,10},{9,11},{10,... | collective-permute-start | bytes 270344 | tf_op jit(solution)/shard_map/ppermute | solution.py:866
  12.3 0.0 collective-permute-done.4
  12.3 1.7 %collective-permute-done.5 = f32[88,128]{1,0:T(8,128)S(1)} collective-permute-done((f32[88,128]{1,0:T(8,128)}, f32[88,128]{1,0:T(8,128)S(1)}, u32[]{:S(2)}, u32[]{:S(2)}) %collective-permute-start.5) | collective-permute-done | bytes 45088 | tf_op jit(solution)/shard_map/ppermute | solution.py:866
  14.0 1.6 %collective-permute-start.6 = (f32[2,88,128]{2,1,0:T(8,128)S(1)}, f32[2,88,128]{2,1,0:T(8,128)S(1)}, u32[]{:S(2)}, u32[]{:S(2)}) collective-permute-start(f32[2,88,128]{2,1,0:T(8,128)S(1)} %pad_maximum_fusion.5.refs_4_), channel_id=1, source_target_pairs={{0,4},{1,5},{2,6},{3,7},{4,0},{5,1},{6,2},{7,3},{8,12},{9,13},{10,... | collective-permute-start | bytes 270344 | tf_op jit(solution)/shard_map/ppermute | solution.py:866
  15.5 0.0 collective-permute-done.1.refs_1_
  15.6 1.4 %collective-permute-start.2 = (f32[4,88,128]{2,1,0:T(8,128)S(1)}, f32[4,88,128]{2,1,0:T(8,128)S(1)}, u32[]{:S(2)}, u32[]{:S(2)}) collective-permute-start(f32[4,88,128]{2,1,0:T(8,128)S(1)} %pad_maximum_fusion.2), channel_id=1, source_target_pairs={{0,4},{1,5},{2,6},{3,7},{4,0},{5,1},{6,2},{7,3},{8,12},{9,13},{10,... | collective-permute-start | bytes 540680 | tf_op jit(solution)/shard_map/ppermute | solution.py:866
  16.9 2.2 %collective-permute-done.6.refs_5_ = f32[2,88,128]{2,1,0:T(8,128)S(1)} collective-permute-done((f32[2,88,128]{2,1,0:T(8,128)S(1)}, f32[2,88,128]{2,1,0:T(8,128)S(1)}, u32[]{:S(2)}, u32[]{:S(2)}) %collective-permute-start.6) | collective-permute-done | bytes 90144 | tf_op jit(solution)/shard_map/ppermute | solution.py:866
  19.1 1.6 %collective-permute-start.7 = (f32[4,88,128]{2,1,0:T(8,128)S(1)}, f32[4,88,128]{2,1,0:T(8,128)S(1)}, u32[]{:S(2)}, u32[]{:S(2)}) collective-permute-start(f32[4,88,128]{2,1,0:T(8,128)S(1)} %pad_maximum_fusion.3), channel_id=1, source_target_pairs={{0,2},{1,3},{2,0},{3,1},{4,6},{5,7},{6,4},{7,5},{8,10},{9,11},{10,... | collective-permute-start | bytes 540680 | tf_op jit(solution)/shard_map/ppermute | solution.py:866
  20.7 0.4 collective-permute-done.2.refs_2_
  21.1 0.0 copy-start
  21.2 0.0 copy-start.1
  21.2 0.1 collective-permute-start.3
  21.2 3.4 %collective-permute-done.7.refs_6_ = f32[4,88,128]{2,1,0:T(8,128)S(1)} collective-permute-done((f32[4,88,128]{2,1,0:T(8,128)S(1)}, f32[4,88,128]{2,1,0:T(8,128)S(1)}, u32[]{:S(2)}, u32[]{:S(2)}) %collective-permute-start.7) | collective-permute-done | bytes 180256 | tf_op jit(solution)/shard_map/ppermute | solution.py:866
  24.7 0.1 collective-permute-start.8
  24.8 0.0 collective-permute-done.3.refs_3_
  24.8 1.7 %collective-permute-done.8.refs_7_ = f32[8,88,128]{2,1,0:T(8,128)S(1)} collective-permute-done((f32[8,88,128]{2,1,0:T(8,128)S(1)}, f32[8,88,128]{2,1,0:T(8,128)S(1)}, u32[]{:S(2)}, u32[]{:S(2)}) %collective-permute-start.8) | collective-permute-done | bytes 360480 | tf_op jit(solution)/shard_map/ppermute | solution.py:866
  26.4 0.0 copy-done
  26.4 0.0 copy-done.1
  26.4 21.5 %solve.1 = (f32[72,128]{1,0:T(8,128)S(1)}, f32[72,128]{1,0:T(8,128)S(1)}, f32[72,128]{1,0:T(8,128)S(1)}, f32[72,128]{1,0:T(8,128)S(1)}) custom-call(f32[2,88,128]{2,1,0:T(8,128)S(1)} %pad_maximum_fusion.4.refs_0_, f32[2,88,128]{2,1,0:T(8,128)S(1)} %collective-permute-done.1.refs_1_, f32[4,88,128]{2,1,0:T(8,128)S(1)} %collective-permute-done.2.refs_2_, ...), custom_call_target="tpu_custom_call" | custom-call | tf_op jit(solution)/shard_map/solve/pallas_call | solution.py:960
  48.0 0.1 collective-permute-start.9
  48.0 2.9 %collective-permute-start.10 = (f32[72,128]{1,0:T(8,128)S(1)}, f32[72,128]{1,0:T(8,128)S(1)}, u32[]{:S(2)}, u32[]{:S(2)}) collective-permute-start(f32[72,128]{1,0:T(8,128)S(1)} %get-tuple-element.33), channel_id=1, source_target_pairs={{0,16},{1,17},{2,18},{3,19},{4,20},{5,21},{6,22},{7,23},{8,24},{9,... | collective-permute-start | bytes 110600 | tf_op jit(solution)/shard_map/ppermute | solution.py:866
  50.9 1.5 %collective-permute-start.11 = (f32[72,128]{1,0:T(8,128)S(1)}, f32[72,128]{1,0:T(8,128)S(1)}, u32[]{:S(2)}, u32[]{:S(2)}) collective-permute-start(f32[72,128]{1,0:T(8,128)S(1)} %get-tuple-element.34), channel_id=1, source_target_pairs={{0,24},{1,25},{2,26},{3,27},{4,28},{5,29},{6,30},{7,31},{8,16},{9,... | collective-permute-start | bytes 110600 | tf_op jit(solution)/shard_map/ppermute | solution.py:866
  52.4 0.0 collective-permute-done.9.refs_1_
  52.4 1.1 %collective-permute-done.10.refs_2_ = f32[72,128]{1,0:T(8,128)S(1)} collective-permute-done((f32[72,128]{1,0:T(8,128)S(1)}, f32[72,128]{1,0:T(8,128)S(1)}, u32[]{:S(2)}, u32[]{:S(2)}) %collective-permute-start.10) | collective-permute-done | bytes 36896 | tf_op jit(solution)/shard_map/ppermute | solution.py:866
  53.5 3.2 %collective-permute-done.11.refs_3_ = f32[72,128]{1,0:T(8,128)S(1)} collective-permute-done((f32[72,128]{1,0:T(8,128)S(1)}, f32[72,128]{1,0:T(8,128)S(1)}, u32[]{:S(2)}, u32[]{:S(2)}) %collective-permute-start.11) | collective-permute-done | bytes 36896 | tf_op jit(solution)/shard_map/ppermute | solution.py:866
  56.7 1.3 %unpack.1 = f32[4,6,4,384]{3,2,1,0:T(4,128)} custom-call(f32[72,128]{1,0:T(8,128)S(1)} %get-tuple-element.31.refs_0_, f32[72,128]{1,0:T(8,128)S(1)} %collective-permute-done.9.refs_1_, f32[72,128]{1,0:T(8,128)S(1)} %collective-permute-done.10.refs_2_, f32[72,128]{1,0:T(8,128)S(1)} %collective-permute-done.11.refs_3_), custom_call_target="tpu_custom_call" | custom-call | tf_op jit(solution)/shard_map/unpack/pallas_call | solution.py:972
  (6 shorter events, 0.1 us)
Async XLA Ops:
  2.2 8.3 %collective-permute-start = (f32[88,128]{1,0:T(8,128)}, f32[88,128]{1,0:T(8,128)S(1)}, u32[]{:S(2)}, u32[]{:S(2)}) collective-permute-start(f32[88,128]{1,0:T(8,128)} %get-tuple-element.25), channel_id=1, source_target_pairs={{0,8},{1,9},{2,10},{3,11},{4,12},{5,13},{6,14},{7,15},{8,0},{9,1},... | collective-permute-start | bytes 135176 | tf_op jit(solution)/shard_map/ppermute | solution.py:866
  5.3 7.0 %collective-permute-start.4 = (f32[88,128]{1,0:T(8,128)}, f32[88,128]{1,0:T(8,128)S(1)}, u32[]{:S(2)}, u32[]{:S(2)}) collective-permute-start(f32[88,128]{1,0:T(8,128)} %get-tuple-element.26), channel_id=1, source_target_pairs={{0,16},{1,17},{2,18},{3,19},{4,20},{5,21},{6,22},{7,23},{8,24},{9,... | collective-permute-start | bytes 135176 | tf_op jit(solution)/shard_map/ppermute | solution.py:866
  7.9 6.1 %collective-permute-start.5 = (f32[88,128]{1,0:T(8,128)}, f32[88,128]{1,0:T(8,128)S(1)}, u32[]{:S(2)}, u32[]{:S(2)}) collective-permute-start(f32[88,128]{1,0:T(8,128)} %get-tuple-element.27), channel_id=1, source_target_pairs={{0,24},{1,25},{2,26},{3,27},{4,28},{5,29},{6,30},{7,31},{8,16},{9,... | collective-permute-start | bytes 135176 | tf_op jit(solution)/shard_map/ppermute | solution.py:866
  7.9 1.1 %copy-start.2 = (f32[384,384]{1,0:T(8,128)S(1)}, f32[384,384]{1,0:T(8,128)}, u32[]{:S(2)}) copy-start(f32[384,384]{1,0:T(8,128)} %source_ref) | copy-start | bytes 1769476
  9.0 1.5 %copy-start.3 = (f32[88,128]{1,0:T(8,128)S(1)}, f32[88,128]{1,0:T(8,128)}, u32[]{:S(2)}) copy-start(f32[88,128]{1,0:T(8,128)} %get-tuple-element.24) | copy-start | bytes 135172
  10.5 5.0 %collective-permute-start.1 = (f32[2,88,128]{2,1,0:T(8,128)S(1)}, f32[2,88,128]{2,1,0:T(8,128)S(1)}, u32[]{:S(2)}, u32[]{:S(2)}) collective-permute-start(f32[2,88,128]{2,1,0:T(8,128)S(1)} %pad_maximum_fusion.4.refs_0_), channel_id=1, source_target_pairs={{0,2},{1,3},{2,0},{3,1},{4,6},{5,7},{6,4},{7,5},{8,10},{9,11},{10,... | collective-permute-start | bytes 270344 | tf_op jit(solution)/shard_map/ppermute | solution.py:866
  14.0 5.1 %collective-permute-start.6 = (f32[2,88,128]{2,1,0:T(8,128)S(1)}, f32[2,88,128]{2,1,0:T(8,128)S(1)}, u32[]{:S(2)}, u32[]{:S(2)}) collective-permute-start(f32[2,88,128]{2,1,0:T(8,128)S(1)} %pad_maximum_fusion.5.refs_4_), channel_id=1, source_target_pairs={{0,4},{1,5},{2,6},{3,7},{4,0},{5,1},{6,2},{7,3},{8,12},{9,13},{10,... | collective-permute-start | bytes 270344 | tf_op jit(solution)/shard_map/ppermute | solution.py:866
  15.6 5.6 %collective-permute-start.2 = (f32[4,88,128]{2,1,0:T(8,128)S(1)}, f32[4,88,128]{2,1,0:T(8,128)S(1)}, u32[]{:S(2)}, u32[]{:S(2)}) collective-permute-start(f32[4,88,128]{2,1,0:T(8,128)S(1)} %pad_maximum_fusion.2), channel_id=1, source_target_pairs={{0,4},{1,5},{2,6},{3,7},{4,0},{5,1},{6,2},{7,3},{8,12},{9,13},{10,... | collective-permute-start | bytes 540680 | tf_op jit(solution)/shard_map/ppermute | solution.py:866
  19.1 5.6 %collective-permute-start.7 = (f32[4,88,128]{2,1,0:T(8,128)S(1)}, f32[4,88,128]{2,1,0:T(8,128)S(1)}, u32[]{:S(2)}, u32[]{:S(2)}) collective-permute-start(f32[4,88,128]{2,1,0:T(8,128)S(1)} %pad_maximum_fusion.3), channel_id=1, source_target_pairs={{0,2},{1,3},{2,0},{3,1},{4,6},{5,7},{6,4},{7,5},{8,10},{9,11},{10,... | collective-permute-start | bytes 540680 | tf_op jit(solution)/shard_map/ppermute | solution.py:866
  21.1 5.3 %copy-start = (f32[3,6,6]{2,1,0:T(8,128)S(1)}, f32[3,6,6]{2,1,0:T(8,128)}, u32[]{:S(2)}) copy-start(f32[3,6,6]{2,1,0:T(8,128)} %refs_8_.1) | copy-start | bytes 1300
  21.2 5.3 %copy-start.1 = (f32[3,6]{1,0:T(4,128)S(1)}, f32[3,6]{1,0:T(4,128)}, u32[]{:S(2)}) copy-start(f32[3,6]{1,0:T(4,128)} %refs_9_.1) | copy-start | bytes 220
  21.2 3.6 %collective-permute-start.3 = (f32[8,88,128]{2,1,0:T(8,128)S(1)}, f32[8,88,128]{2,1,0:T(8,128)S(1)}, u32[]{:S(2)}, u32[]{:S(2)}) collective-permute-start(f32[8,88,128]{2,1,0:T(8,128)S(1)} %pad_maximum_fusion), channel_id=1, source_target_pairs={{0,1},{1,0},{2,3},{3,2},{4,5},{5,4},{6,7},{7,6},{8,9},{9,8},{10,11... | collective-permute-start | bytes 1081352 | tf_op jit(solution)/shard_map/ppermute | solution.py:866
  24.7 1.7 %collective-permute-start.8 = (f32[8,88,128]{2,1,0:T(8,128)S(1)}, f32[8,88,128]{2,1,0:T(8,128)S(1)}, u32[]{:S(2)}, u32[]{:S(2)}) collective-permute-start(f32[8,88,128]{2,1,0:T(8,128)S(1)} %pad_maximum_fusion.1), channel_id=1, source_target_pairs={{0,1},{1,0},{2,3},{3,2},{4,5},{5,4},{6,7},{7,6},{8,9},{9,8},{10,11... | collective-permute-start | bytes 1081352 | tf_op jit(solution)/shard_map/ppermute | solution.py:866
  48.0 4.5 %collective-permute-start.9 = (f32[72,128]{1,0:T(8,128)S(1)}, f32[72,128]{1,0:T(8,128)S(1)}, u32[]{:S(2)}, u32[]{:S(2)}) collective-permute-start(f32[72,128]{1,0:T(8,128)S(1)} %get-tuple-element.32), channel_id=1, source_target_pairs={{0,8},{1,9},{2,10},{3,11},{4,12},{5,13},{6,14},{7,15},{8,0},{9,1},... | collective-permute-start | bytes 110600 | tf_op jit(solution)/shard_map/ppermute | solution.py:866
  48.0 5.5 %collective-permute-start.10 = (f32[72,128]{1,0:T(8,128)S(1)}, f32[72,128]{1,0:T(8,128)S(1)}, u32[]{:S(2)}, u32[]{:S(2)}) collective-permute-start(f32[72,128]{1,0:T(8,128)S(1)} %get-tuple-element.33), channel_id=1, source_target_pairs={{0,16},{1,17},{2,18},{3,19},{4,20},{5,21},{6,22},{7,23},{8,24},{9,... | collective-permute-start | bytes 110600 | tf_op jit(solution)/shard_map/ppermute | solution.py:866
  50.9 5.8 %collective-permute-start.11 = (f32[72,128]{1,0:T(8,128)S(1)}, f32[72,128]{1,0:T(8,128)S(1)}, u32[]{:S(2)}, u32[]{:S(2)}) collective-permute-start(f32[72,128]{1,0:T(8,128)S(1)} %get-tuple-element.34), channel_id=1, source_target_pairs={{0,24},{1,25},{2,26},{3,27},{4,28},{5,29},{6,30},{7,31},{8,16},{9,... | collective-permute-start | bytes 110600 | tf_op jit(solution)/shard_map/ppermute | solution.py:866

commit v4 on v3

--- a/solution.py
+++ b/solution.py
@@ -69,7 +69,9 @@
             stack[pl.ds(k * count + b * TX, TX), :] = right_ref[own ^ k, b]
     stack[pl.ds(VECS * count, TX), :] = labels_ref[...].astype(F32)
     stack[pl.ds(VECS * count + TX, TX), :] = jnp.zeros((TX, CELLS), F32)
-    moved = jnp.dot(stack[...], permute, precision=HIGHEST, preferred_element_type=F32)
+    moved = sum(
+        jnp.dot(part, permute.astype(BF16), preferred_element_type=F32) for part in split(stack[...])
+    )
     lane = iota((1, LANES), 1)
     inner = lane % GROUP
     wanted = (inner // (2 * ZQ)) * (NZ // 4) + 3 * ((inner % ZQ) // 2) + lane // GROUP
@@ -102,7 +104,9 @@
             stack[pl.ds(k * count, count), t * LANES : (t + 1) * LANES] = ins[k][
                 pl.ds(t * count, count), :
             ]
-    moved = jnp.dot(stack[...], permute, precision=HIGHEST, preferred_element_type=F32)
+    moved = sum(
+        jnp.dot(part, permute.astype(BF16), preferred_element_type=F32) for part in split(stack[...])
+    )
     for k in range(VECS):
         for b in range(BANDS):
             first = k * count + b * TX
@@ -883,7 +887,8 @@
         name="pack",
     )(right_hand, region_labels, aggregate_map)
     packed, coarse_inverse = lax.optimization_barrier((packed, coarse_inverse))
-    parts = [packed[0]] + [exchanged(packed[k], k * stride) for k in range(1, VECS)]
+    turns = (0, 2, 3, 1)
+    parts = [packed[0]] + [exchanged(packed[k], k * stride) for k in turns[1:]]
     inverse = pl.pallas_call(
         order_kernel,
         out_shape=jax.ShapeDtypeStruct((BANDS, NAGG, BANDS * NAGG), F32),
@@ -900,7 +905,7 @@
     steps += [("gx", i) for i in range(bits(groups))]
     second, inverse = lax.optimization_barrier((jnp.stack(parts[2:]), inverse))
     halves = [[jnp.stack(parts[:2])], [second]]
-    places = [[[(k, 0, 0) for k in (0, 1)]], [[(k, 0, 0) for k in (2, 3)]]]
+    places = [[[(k, 0, 0) for k in turns[:2]]], [[(k, 0, 0) for k in turns[2:]]]]
 
     def widen(half, axis, bit):
         mask = 1 << bit
@@ -911,7 +916,7 @@
             [(k, g ^ mask_g, y ^ mask_y) for blocks in places[half] for k, g, y in blocks]
         )
 
-    for first, last in zip(steps, steps[::-1]):
+    for first, last in zip(steps, steps):
         widen(0, *first)
         widen(1, *last)
     widen(0, "gy", 0)

time: 58.2 us -> 57 us (0.979)
  no operation moved by 1% of the time
where the time goes in v4:
time: 57 us; the launch traced here: 56.8 us
  Pallas kernels  26.1 us (46%)
  starting transfers between devices  16.3 us (29%)
  waiting for transfers between devices  13.2 us (23%)
  local copies, waits for them, and re-layouts  1.08 us (2%)
    pallas_call x1, Pallas kernels, shards(): pl.pallas_call(functools.partial(solve_kernel, size_x, size_y, places), o...  21.5 us
    ppermute x12, starting transfers between devices, exchanged(): return lax.ppermute(value, names, [(i, i ^ mask) for i in range(devices)])  16.3 us
    ppermute x12, waiting for transfers between devices, exchanged(): return lax.ppermute(value, names, [(i, i ^ mask) for i in range(devices)])  13.2 us
    pallas_call x1, Pallas kernels, shards(): pl.pallas_call(functools.partial(pack_kernel, groups), out_shape=[row_sha...  1.98 us
    pallas_call x1, Pallas kernels, shards(): pl.pallas_call(order_kernel, out_shape=jax.ShapeDtypeStruct((BANDS, NAGG,...  1.51 us
  transfers between devices with their start and end apart: 12, of which 7 were waited for; matrix products, arithmetic and copies ran while one was open for 0% of the time, Pallas kernels for 3%

profile of v4, /device:TPU:0, one launch (start us, length us, event | category | flops | bytes accessed | tf_op | source)
XLA Modules:
  0.0 56.8 jit_solution(13870770960159512965)
XLA Ops:
  0.0 2.0 %pack.1 = (f32[88,128]{1,0:T(8,128)}, f32[88,128]{1,0:T(8,128)}, f32[88,128]{1,0:T(8,128)}, f32[88,128]{1,0:T(8,128)}) custom-call(f32[4,6,4,384]{3,2,1,0:T(4,128)} %right_hbm.1, s32[4,384]{1,0:T(4,128)} %labels_hbm.1, s32[1,24]{1,0:T(1,128)} %agg_hbm.1), custom_call_target="tpu_custom_call" | custom-call | tf_op jit(solution)/shard_map/pack/pallas_call | solution.py:874
  2.0 4.1 %collective-permute-start = (f32[88,128]{1,0:T(8,128)}, f32[88,128]{1,0:T(8,128)S(1)}, u32[]{:S(2)}, u32[]{:S(2)}) collective-permute-start(f32[88,128]{1,0:T(8,128)} %get-tuple-element.25), channel_id=1, source_target_pairs={{0,16},{1,17},{2,18},{3,19},{4,20},{5,21},{6,22},{7,23},{8,24},{9,... | collective-permute-start | bytes 135176 | tf_op jit(solution)/shard_map/ppermute | solution.py:870
  6.1 1.3 %collective-permute-start.4 = (f32[88,128]{1,0:T(8,128)}, f32[88,128]{1,0:T(8,128)S(1)}, u32[]{:S(2)}, u32[]{:S(2)}) collective-permute-start(f32[88,128]{1,0:T(8,128)} %get-tuple-element.26), channel_id=1, source_target_pairs={{0,24},{1,25},{2,26},{3,27},{4,28},{5,29},{6,30},{7,31},{8,16},{9,... | collective-permute-start | bytes 135176 | tf_op jit(solution)/shard_map/ppermute | solution.py:870
  7.4 0.2 collective-permute-start.5
  7.7 0.0 copy-start.2
  7.7 1.1 %copy-done.2 = f32[384,384]{1,0:T(8,128)S(1)} copy-done((f32[384,384]{1,0:T(8,128)S(1)}, f32[384,384]{1,0:T(8,128)}, u32[]{:S(2)}) %copy-start.2) | copy-done | bytes 589848
  8.7 0.0 copy-start.3
  8.7 1.5 %order.1.refs_10_ = f32[6,64,384]{2,1,0:T(8,128)S(1)} custom-call(f32[384,384]{1,0:T(8,128)S(1)} %copy-done.2), custom_call_target="tpu_custom_call" | custom-call | flops 339738624 | bytes 2097152 | tf_op jit(solution)/shard_map/order/pallas_call | solution.py:892
  10.3 0.0 collective-permute-done
  10.3 0.0 copy-done.3
  10.3 1.6 %collective-permute-start.1 = (f32[2,88,128]{2,1,0:T(8,128)S(1)}, f32[2,88,128]{2,1,0:T(8,128)S(1)}, u32[]{:S(2)}, u32[]{:S(2)}) collective-permute-start(f32[2,88,128]{2,1,0:T(8,128)S(1)} %pad_maximum_fusion.4.refs_0_), channel_id=1, source_target_pairs={{0,2},{1,3},{2,0},{3,1},{4,6},{5,7},{6,4},{7,5},{8,10},{9,11},{10,... | collective-permute-start | bytes 270344 | tf_op jit(solution)/shard_map/ppermute | solution.py:870
  11.8 0.3 collective-permute-done.4
  12.2 0.0 collective-permute-done.5
  12.2 1.6 %collective-permute-start.6 = (f32[2,88,128]{2,1,0:T(8,128)S(1)}, f32[2,88,128]{2,1,0:T(8,128)S(1)}, u32[]{:S(2)}, u32[]{:S(2)}) collective-permute-start(f32[2,88,128]{2,1,0:T(8,128)S(1)} %pad_maximum_fusion.5.refs_4_), channel_id=1, source_target_pairs={{0,2},{1,3},{2,0},{3,1},{4,6},{5,7},{6,4},{7,5},{8,10},{9,11},{10,... | collective-permute-start | bytes 270344 | tf_op jit(solution)/shard_map/ppermute | solution.py:870
  13.8 1.7 %collective-permute-done.1.refs_1_ = f32[2,88,128]{2,1,0:T(8,128)S(1)} collective-permute-done((f32[2,88,128]{2,1,0:T(8,128)S(1)}, f32[2,88,128]{2,1,0:T(8,128)S(1)}, u32[]{:S(2)}, u32[]{:S(2)}) %collective-permute-start.1) | collective-permute-done | bytes 90144 | tf_op jit(solution)/shard_map/ppermute | solution.py:870
  15.5 1.6 %collective-permute-start.2 = (f32[4,88,128]{2,1,0:T(8,128)S(1)}, f32[4,88,128]{2,1,0:T(8,128)S(1)}, u32[]{:S(2)}, u32[]{:S(2)}) collective-permute-start(f32[4,88,128]{2,1,0:T(8,128)S(1)} %pad_maximum_fusion.2), channel_id=1, source_target_pairs={{0,4},{1,5},{2,6},{3,7},{4,0},{5,1},{6,2},{7,3},{8,12},{9,13},{10,... | collective-permute-start | bytes 540680 | tf_op jit(solution)/shard_map/ppermute | solution.py:870
  17.1 0.0 collective-permute-done.6.refs_5_
  17.1 1.3 %collective-permute-start.7 = (f32[4,88,128]{2,1,0:T(8,128)S(1)}, f32[4,88,128]{2,1,0:T(8,128)S(1)}, u32[]{:S(2)}, u32[]{:S(2)}) collective-permute-start(f32[4,88,128]{2,1,0:T(8,128)S(1)} %pad_maximum_fusion.3), channel_id=1, source_target_pairs={{0,4},{1,5},{2,6},{3,7},{4,0},{5,1},{6,2},{7,3},{8,12},{9,13},{10,... | collective-permute-start | bytes 540680 | tf_op jit(solution)/shard_map/ppermute | solution.py:870
  18.4 3.4 %collective-permute-done.2.refs_2_ = f32[4,88,128]{2,1,0:T(8,128)S(1)} collective-permute-done((f32[4,88,128]{2,1,0:T(8,128)S(1)}, f32[4,88,128]{2,1,0:T(8,128)S(1)}, u32[]{:S(2)}, u32[]{:S(2)}) %collective-permute-start.2) | collective-permute-done | bytes 180256 | tf_op jit(solution)/shard_map/ppermute | solution.py:870
  21.8 0.0 copy-start
  21.8 0.0 copy-start.1
  21.8 0.1 collective-permute-start.3
  21.9 1.8 %collective-permute-done.7.refs_6_ = f32[4,88,128]{2,1,0:T(8,128)S(1)} collective-permute-done((f32[4,88,128]{2,1,0:T(8,128)S(1)}, f32[4,88,128]{2,1,0:T(8,128)S(1)}, u32[]{:S(2)}, u32[]{:S(2)}) %collective-permute-start.7) | collective-permute-done | bytes 180256 | tf_op jit(solution)/shard_map/ppermute | solution.py:870
  23.7 0.1 collective-permute-start.8
  23.8 0.0 collective-permute-done.3.refs_3_
  23.8 1.7 %collective-permute-done.8.refs_7_ = f32[8,88,128]{2,1,0:T(8,128)S(1)} collective-permute-done((f32[8,88,128]{2,1,0:T(8,128)S(1)}, f32[8,88,128]{2,1,0:T(8,128)S(1)}, u32[]{:S(2)}, u32[]{:S(2)}) %collective-permute-start.8) | collective-permute-done | bytes 360480 | tf_op jit(solution)/shard_map/ppermute | solution.py:870
  25.5 0.0 copy-done
  25.5 0.0 copy-done.1
  25.5 21.5 %solve.1 = (f32[72,128]{1,0:T(8,128)S(1)}, f32[72,128]{1,0:T(8,128)S(1)}, f32[72,128]{1,0:T(8,128)S(1)}, f32[72,128]{1,0:T(8,128)S(1)}) custom-call(f32[2,88,128]{2,1,0:T(8,128)S(1)} %pad_maximum_fusion.4.refs_0_, f32[2,88,128]{2,1,0:T(8,128)S(1)} %collective-permute-done.1.refs_1_, f32[4,88,128]{2,1,0:T(8,128)S(1)} %collective-permute-done.2.refs_2_, ...), custom_call_target="tpu_custom_call" | custom-call | tf_op jit(solution)/shard_map/solve/pallas_call | solution.py:965
  47.0 1.3 %collective-permute-start.9 = (f32[72,128]{1,0:T(8,128)S(1)}, f32[72,128]{1,0:T(8,128)S(1)}, u32[]{:S(2)}, u32[]{:S(2)}) collective-permute-start(f32[72,128]{1,0:T(8,128)S(1)} %get-tuple-element.32), channel_id=1, source_target_pairs={{0,8},{1,9},{2,10},{3,11},{4,12},{5,13},{6,14},{7,15},{8,0},{9,1},... | collective-permute-start | bytes 110600 | tf_op jit(solution)/shard_map/ppermute | solution.py:870
  48.3 1.7 %collective-permute-start.10 = (f32[72,128]{1,0:T(8,128)S(1)}, f32[72,128]{1,0:T(8,128)S(1)}, u32[]{:S(2)}, u32[]{:S(2)}) collective-permute-start(f32[72,128]{1,0:T(8,128)S(1)} %get-tuple-element.33), channel_id=1, source_target_pairs={{0,16},{1,17},{2,18},{3,19},{4,20},{5,21},{6,22},{7,23},{8,24},{9,... | collective-permute-start | bytes 110600 | tf_op jit(solution)/shard_map/ppermute | solution.py:870
  50.0 1.5 %collective-permute-start.11 = (f32[72,128]{1,0:T(8,128)S(1)}, f32[72,128]{1,0:T(8,128)S(1)}, u32[]{:S(2)}, u32[]{:S(2)}) collective-permute-start(f32[72,128]{1,0:T(8,128)S(1)} %get-tuple-element.34), channel_id=1, source_target_pairs={{0,24},{1,25},{2,26},{3,27},{4,28},{5,29},{6,30},{7,31},{8,16},{9,... | collective-permute-start | bytes 110600 | tf_op jit(solution)/shard_map/ppermute | solution.py:870
  51.4 0.0 collective-permute-done.9.refs_1_
  51.4 2.3 %collective-permute-done.10.refs_2_ = f32[72,128]{1,0:T(8,128)S(1)} collective-permute-done((f32[72,128]{1,0:T(8,128)S(1)}, f32[72,128]{1,0:T(8,128)S(1)}, u32[]{:S(2)}, u32[]{:S(2)}) %collective-permute-start.10) | collective-permute-done | bytes 36896 | tf_op jit(solution)/shard_map/ppermute | solution.py:870
  53.8 1.9 %collective-permute-done.11.refs_3_ = f32[72,128]{1,0:T(8,128)S(1)} collective-permute-done((f32[72,128]{1,0:T(8,128)S(1)}, f32[72,128]{1,0:T(8,128)S(1)}, u32[]{:S(2)}, u32[]{:S(2)}) %collective-permute-start.11) | collective-permute-done | bytes 36896 | tf_op jit(solution)/shard_map/ppermute | solution.py:870
  55.7 1.1 %unpack.1 = f32[4,6,4,384]{3,2,1,0:T(4,128)} custom-call(f32[72,128]{1,0:T(8,128)S(1)} %get-tuple-element.31.refs_0_, f32[72,128]{1,0:T(8,128)S(1)} %collective-permute-done.9.refs_1_, f32[72,128]{1,0:T(8,128)S(1)} %collective-permute-done.10.refs_2_, f32[72,128]{1,0:T(8,128)S(1)} %collective-permute-done.11.refs_3_), custom_call_target="tpu_custom_call" | custom-call | tf_op jit(solution)/shard_map/unpack/pallas_call | solution.py:977
  (6 shorter events, 0.1 us)
Async XLA Ops:
  2.0 8.3 %collective-permute-start = (f32[88,128]{1,0:T(8,128)}, f32[88,128]{1,0:T(8,128)S(1)}, u32[]{:S(2)}, u32[]{:S(2)}) collective-permute-start(f32[88,128]{1,0:T(8,128)} %get-tuple-element.25), channel_id=1, source_target_pairs={{0,16},{1,17},{2,18},{3,19},{4,20},{5,21},{6,22},{7,23},{8,24},{9,... | collective-permute-start | bytes 135176 | tf_op jit(solution)/shard_map/ppermute | solution.py:870
  6.1 6.1 %collective-permute-start.4 = (f32[88,128]{1,0:T(8,128)}, f32[88,128]{1,0:T(8,128)S(1)}, u32[]{:S(2)}, u32[]{:S(2)}) collective-permute-start(f32[88,128]{1,0:T(8,128)} %get-tuple-element.26), channel_id=1, source_target_pairs={{0,24},{1,25},{2,26},{3,27},{4,28},{5,29},{6,30},{7,31},{8,16},{9,... | collective-permute-start | bytes 135176 | tf_op jit(solution)/shard_map/ppermute | solution.py:870
  7.4 4.7 %collective-permute-start.5 = (f32[88,128]{1,0:T(8,128)}, f32[88,128]{1,0:T(8,128)S(1)}, u32[]{:S(2)}, u32[]{:S(2)}) collective-permute-start(f32[88,128]{1,0:T(8,128)} %get-tuple-element.27), channel_id=1, source_target_pairs={{0,8},{1,9},{2,10},{3,11},{4,12},{5,13},{6,14},{7,15},{8,0},{9,1},... | collective-permute-start | bytes 135176 | tf_op jit(solution)/shard_map/ppermute | solution.py:870
  7.7 1.1 %copy-start.2 = (f32[384,384]{1,0:T(8,128)S(1)}, f32[384,384]{1,0:T(8,128)}, u32[]{:S(2)}) copy-start(f32[384,384]{1,0:T(8,128)} %source_ref) | copy-start | bytes 1769476
  8.7 1.5 %copy-start.3 = (f32[88,128]{1,0:T(8,128)S(1)}, f32[88,128]{1,0:T(8,128)}, u32[]{:S(2)}) copy-start(f32[88,128]{1,0:T(8,128)} %get-tuple-element.24) | copy-start | bytes 135172
  10.3 5.2 %collective-permute-start.1 = (f32[2,88,128]{2,1,0:T(8,128)S(1)}, f32[2,88,128]{2,1,0:T(8,128)S(1)}, u32[]{:S(2)}, u32[]{:S(2)}) collective-permute-start(f32[2,88,128]{2,1,0:T(8,128)S(1)} %pad_maximum_fusion.4.refs_0_), channel_id=1, source_target_pairs={{0,2},{1,3},{2,0},{3,1},{4,6},{5,7},{6,4},{7,5},{8,10},{9,11},{10,... | collective-permute-start | bytes 270344 | tf_op jit(solution)/shard_map/ppermute | solution.py:870
  12.2 4.9 %collective-permute-start.6 = (f32[2,88,128]{2,1,0:T(8,128)S(1)}, f32[2,88,128]{2,1,0:T(8,128)S(1)}, u32[]{:S(2)}, u32[]{:S(2)}) collective-permute-start(f32[2,88,128]{2,1,0:T(8,128)S(1)} %pad_maximum_fusion.5.refs_4_), channel_id=1, source_target_pairs={{0,2},{1,3},{2,0},{3,1},{4,6},{5,7},{6,4},{7,5},{8,10},{9,11},{10,... | collective-permute-start | bytes 270344 | tf_op jit(solution)/shard_map/ppermute | solution.py:870
  15.5 6.3 %collective-permute-start.2 = (f32[4,88,128]{2,1,0:T(8,128)S(1)}, f32[4,88,128]{2,1,0:T(8,128)S(1)}, u32[]{:S(2)}, u32[]{:S(2)}) collective-permute-start(f32[4,88,128]{2,1,0:T(8,128)S(1)} %pad_maximum_fusion.2), channel_id=1, source_target_pairs={{0,4},{1,5},{2,6},{3,7},{4,0},{5,1},{6,2},{7,3},{8,12},{9,13},{10,... | collective-permute-start | bytes 540680 | tf_op jit(solution)/shard_map/ppermute | solution.py:870
  17.1 6.6 %collective-permute-start.7 = (f32[4,88,128]{2,1,0:T(8,128)S(1)}, f32[4,88,128]{2,1,0:T(8,128)S(1)}, u32[]{:S(2)}, u32[]{:S(2)}) collective-permute-start(f32[4,88,128]{2,1,0:T(8,128)S(1)} %pad_maximum_fusion.3), channel_id=1, source_target_pairs={{0,4},{1,5},{2,6},{3,7},{4,0},{5,1},{6,2},{7,3},{8,12},{9,13},{10,... | collective-permute-start | bytes 540680 | tf_op jit(solution)/shard_map/ppermute | solution.py:870
  21.8 3.7 %copy-start = (f32[3,6,6]{2,1,0:T(8,128)S(1)}, f32[3,6,6]{2,1,0:T(8,128)}, u32[]{:S(2)}) copy-start(f32[3,6,6]{2,1,0:T(8,128)} %refs_8_.1) | copy-start | bytes 1300
  21.8 3.7 %copy-start.1 = (f32[3,6]{1,0:T(4,128)S(1)}, f32[3,6]{1,0:T(4,128)}, u32[]{:S(2)}) copy-start(f32[3,6]{1,0:T(4,128)} %refs_9_.1) | copy-start | bytes 220
  21.8 2.0 %collective-permute-start.3 = (f32[8,88,128]{2,1,0:T(8,128)S(1)}, f32[8,88,128]{2,1,0:T(8,128)S(1)}, u32[]{:S(2)}, u32[]{:S(2)}) collective-permute-start(f32[8,88,128]{2,1,0:T(8,128)S(1)} %pad_maximum_fusion), channel_id=1, source_target_pairs={{0,1},{1,0},{2,3},{3,2},{4,5},{5,4},{6,7},{7,6},{8,9},{9,8},{10,11... | collective-permute-start | bytes 1081352 | tf_op jit(solution)/shard_map/ppermute | solution.py:870
  23.7 1.7 %collective-permute-start.8 = (f32[8,88,128]{2,1,0:T(8,128)S(1)}, f32[8,88,128]{2,1,0:T(8,128)S(1)}, u32[]{:S(2)}, u32[]{:S(2)}) collective-permute-start(f32[8,88,128]{2,1,0:T(8,128)S(1)} %pad_maximum_fusion.1), channel_id=1, source_target_pairs={{0,1},{1,0},{2,3},{3,2},{4,5},{5,4},{6,7},{7,6},{8,9},{9,8},{10,11... | collective-permute-start | bytes 1081352 | tf_op jit(solution)/shard_map/ppermute | solution.py:870
  47.0 4.5 %collective-permute-start.9 = (f32[72,128]{1,0:T(8,128)S(1)}, f32[72,128]{1,0:T(8,128)S(1)}, u32[]{:S(2)}, u32[]{:S(2)}) collective-permute-start(f32[72,128]{1,0:T(8,128)S(1)} %get-tuple-element.32), channel_id=1, source_target_pairs={{0,8},{1,9},{2,10},{3,11},{4,12},{5,13},{6,14},{7,15},{8,0},{9,1},... | collective-permute-start | bytes 110600 | tf_op jit(solution)/shard_map/ppermute | solution.py:870
  48.3 5.5 %collective-permute-start.10 = (f32[72,128]{1,0:T(8,128)S(1)}, f32[72,128]{1,0:T(8,128)S(1)}, u32[]{:S(2)}, u32[]{:S(2)}) collective-permute-start(f32[72,128]{1,0:T(8,128)S(1)} %get-tuple-element.33), channel_id=1, source_target_pairs={{0,16},{1,17},{2,18},{3,19},{4,20},{5,21},{6,22},{7,23},{8,24},{9,... | collective-permute-start | bytes 110600 | tf_op jit(solution)/shard_map/ppermute | solution.py:870
  50.0 5.8 %collective-permute-start.11 = (f32[72,128]{1,0:T(8,128)S(1)}, f32[72,128]{1,0:T(8,128)S(1)}, u32[]{:S(2)}, u32[]{:S(2)}) collective-permute-start(f32[72,128]{1,0:T(8,128)S(1)} %get-tuple-element.34), channel_id=1, source_target_pairs={{0,24},{1,25},{2,26},{3,27},{4,28},{5,29},{6,30},{7,31},{8,16},{9,... | collective-permute-start | bytes 110600 | tf_op jit(solution)/shard_map/ppermute | solution.py:870

commit v5 on v4

--- a/solution.py
+++ b/solution.py
@@ -95,17 +95,16 @@
 
 
 def unpack_kernel(groups, *refs):
-    ins, out_ref, stack = refs[:VECS], refs[VECS], refs[VECS + 1]
+    ins, (permute_ref, out_ref, stack) = refs[:VECS], refs[VECS:]
     own = lax.axis_index("gx") // groups
     count = BANDS * TX
-    permute = (iota((CELLS, CELLS), 1) == source_lane(iota((CELLS, 1), 0))).astype(F32)
     for k in range(VECS):
         for t in range(TILES):
             stack[pl.ds(k * count, count), t * LANES : (t + 1) * LANES] = ins[k][
                 pl.ds(t * count, count), :
             ]
     moved = sum(
-        jnp.dot(part, permute.astype(BF16), preferred_element_type=F32) for part in split(stack[...])
+        jnp.dot(part, permute_ref[...], preferred_element_type=F32) for part in split(stack[...])
     )
     for k in range(VECS):
         for b in range(BANDS):
@@ -120,7 +119,10 @@
     return high, middle, (left - middle.astype(F32)).astype(BF16)
 
 
-def order_kernel(source_ref, out_ref):
+def order_kernel(source_ref, out_ref, permute_ref):
+    permute_ref[...] = (
+        (iota((CELLS, CELLS), 1) == source_lane(iota((CELLS, 1), 0))).astype(F32).astype(BF16)
+    )
     size = NAGG * BANDS
     row, column = iota((size, 1), 0), iota((1, size), 1)
     inputs = (iota((size, size), 1) == (row % NAGG) * BANDS + row // NAGG).astype(F32).astype(BF16)
@@ -889,11 +891,14 @@
     packed, coarse_inverse = lax.optimization_barrier((packed, coarse_inverse))
     turns = (0, 2, 3, 1)
     parts = [packed[0]] + [exchanged(packed[k], k * stride) for k in turns[1:]]
-    inverse = pl.pallas_call(
+    inverse, permute = pl.pallas_call(
         order_kernel,
-        out_shape=jax.ShapeDtypeStruct((BANDS, NAGG, BANDS * NAGG), F32),
+        out_shape=[
+            jax.ShapeDtypeStruct((BANDS, NAGG, BANDS * NAGG), F32),
+            jax.ShapeDtypeStruct((CELLS, CELLS), BF16),
+        ],
         in_specs=[VMEM_SPEC],
-        out_specs=VMEM_SPEC,
+        out_specs=[VMEM_SPEC] * 2,
         compiler_params=pltpu.CompilerParams(vmem_limit_bytes=16 * 2**20),
         cost_estimate=pl.CostEstimate(
             flops=6 * (NAGG * BANDS) ** 3, bytes_accessed=2**21, transcendentals=0
@@ -977,12 +982,12 @@
     return pl.pallas_call(
         functools.partial(unpack_kernel, groups),
         out_shape=jax.ShapeDtypeStruct(right_hand.shape, F32),
-        in_specs=[VMEM_SPEC] * VECS,
+        in_specs=[VMEM_SPEC] * (VECS + 1),
         out_specs=VMEM_SPEC,
         scratch_shapes=[pltpu.VMEM((VECS * count, CELLS), F32)],
         compiler_params=pltpu.CompilerParams(vmem_limit_bytes=8 * 2**20),
         name="unpack",
-    )(*received)
+    )(*received, permute)
 
 
 def solution(mesh):

time: 57 us -> 57 us (level)
  no operation moved by 1% of the time
where the time goes in v5:
time: 57 us; the launch traced here: 56.9 us
  Pallas kernels  26.1 us (46%)
  starting transfers between devices  16.1 us (28%)
  waiting for transfers between devices  13.3 us (23%)
  local copies, waits for them, and re-layouts  1.08 us (2%)
    pallas_call x1, Pallas kernels, shards(): pl.pallas_call(functools.partial(solve_kernel, size_x, size_y, places), o...  21.5 us
    ppermute x12, starting transfers between devices, exchanged(): return lax.ppermute(value, names, [(i, i ^ mask) for i in range(devices)])  16.1 us
    ppermute x12, waiting for transfers between devices, exchanged(): return lax.ppermute(value, names, [(i, i ^ mask) for i in range(devices)])  13.3 us
    pallas_call x1, Pallas kernels, shards(): pl.pallas_call(functools.partial(pack_kernel, groups), out_shape=[row_sha...  1.99 us
    pallas_call x1, Pallas kernels, shards(): pl.pallas_call(order_kernel, out_shape=[jax.ShapeDtypeStruct((BANDS, NAGG...  1.67 us
  transfers between devices with their start and end apart: 12, of which 7 were waited for; matrix products, arithmetic and copies ran while one was open for 0% of the time, Pallas kernels for 3%

profile of v5, /device:TPU:0, one launch (start us, length us, event | category | flops | bytes accessed | tf_op | source)
XLA Modules:
  0.0 56.9 jit_solution(566510424032485073)
XLA Ops:
  0.0 2.0 %pack.1 = (f32[88,128]{1,0:T(8,128)}, f32[88,128]{1,0:T(8,128)}, f32[88,128]{1,0:T(8,128)}, f32[88,128]{1,0:T(8,128)}) custom-call(f32[4,6,4,384]{3,2,1,0:T(4,128)} %right_hbm.1, s32[4,384]{1,0:T(4,128)} %labels_hbm.1, s32[1,24]{1,0:T(1,128)} %agg_hbm.1), custom_call_target="tpu_custom_call" | custom-call | tf_op jit(solution)/shard_map/pack/pallas_call | solution.py:876
  2.0 4.1 %collective-permute-start = (f32[88,128]{1,0:T(8,128)}, f32[88,128]{1,0:T(8,128)S(1)}, u32[]{:S(2)}, u32[]{:S(2)}) collective-permute-start(f32[88,128]{1,0:T(8,128)} %get-tuple-element.27), channel_id=1, source_target_pairs={{0,16},{1,17},{2,18},{3,19},{4,20},{5,21},{6,22},{7,23},{8,24},{9,... | collective-permute-start | bytes 135176 | tf_op jit(solution)/shard_map/ppermute | solution.py:872
  6.1 1.3 %collective-permute-start.4 = (f32[88,128]{1,0:T(8,128)}, f32[88,128]{1,0:T(8,128)S(1)}, u32[]{:S(2)}, u32[]{:S(2)}) collective-permute-start(f32[88,128]{1,0:T(8,128)} %get-tuple-element.28), channel_id=1, source_target_pairs={{0,24},{1,25},{2,26},{3,27},{4,28},{5,29},{6,30},{7,31},{8,16},{9,... | collective-permute-start | bytes 135176 | tf_op jit(solution)/shard_map/ppermute | solution.py:872
  7.4 0.2 collective-permute-start.5
  7.7 0.0 copy-start.2
  7.7 1.1 %copy-done.2 = f32[384,384]{1,0:T(8,128)S(1)} copy-done((f32[384,384]{1,0:T(8,128)S(1)}, f32[384,384]{1,0:T(8,128)}, u32[]{:S(2)}) %copy-start.2) | copy-done | bytes 589848
  8.7 0.0 copy-start.3
  8.7 1.7 %order.1 = (f32[6,64,384]{2,1,0:T(8,128)S(1)}, bf16[384,384]{1,0:T(8,128)(2,1)S(1)}) custom-call(f32[384,384]{1,0:T(8,128)S(1)} %copy-done.2), custom_call_target="tpu_custom_call" | custom-call | flops 339738624 | bytes 2097152 | tf_op jit(solution)/shard_map/order/pallas_call | solution.py:894
  10.4 0.0 collective-permute-done
  10.4 0.0 copy-done.3
  10.5 1.6 %collective-permute-start.1 = (f32[2,88,128]{2,1,0:T(8,128)S(1)}, f32[2,88,128]{2,1,0:T(8,128)S(1)}, u32[]{:S(2)}, u32[]{:S(2)}) collective-permute-start(f32[2,88,128]{2,1,0:T(8,128)S(1)} %pad_maximum_fusion.4.refs_0_), channel_id=1, source_target_pairs={{0,2},{1,3},{2,0},{3,1},{4,6},{5,7},{6,4},{7,5},{8,10},{9,11},{10,... | collective-permute-start | bytes 270344 | tf_op jit(solution)/shard_map/ppermute | solution.py:872
  12.0 0.2 collective-permute-done.4
  12.2 0.0 collective-permute-done.5
  12.2 1.6 %collective-permute-start.6 = (f32[2,88,128]{2,1,0:T(8,128)S(1)}, f32[2,88,128]{2,1,0:T(8,128)S(1)}, u32[]{:S(2)}, u32[]{:S(2)}) collective-permute-start(f32[2,88,128]{2,1,0:T(8,128)S(1)} %pad_maximum_fusion.5.refs_4_), channel_id=1, source_target_pairs={{0,2},{1,3},{2,0},{3,1},{4,6},{5,7},{6,4},{7,5},{8,10},{9,11},{10,... | collective-permute-start | bytes 270344 | tf_op jit(solution)/shard_map/ppermute | solution.py:872
  13.8 1.9 %collective-permute-done.1.refs_1_ = f32[2,88,128]{2,1,0:T(8,128)S(1)} collective-permute-done((f32[2,88,128]{2,1,0:T(8,128)S(1)}, f32[2,88,128]{2,1,0:T(8,128)S(1)}, u32[]{:S(2)}, u32[]{:S(2)}) %collective-permute-start.1) | collective-permute-done | bytes 90144 | tf_op jit(solution)/shard_map/ppermute | solution.py:872
  15.6 1.6 %collective-permute-start.2 = (f32[4,88,128]{2,1,0:T(8,128)S(1)}, f32[4,88,128]{2,1,0:T(8,128)S(1)}, u32[]{:S(2)}, u32[]{:S(2)}) collective-permute-start(f32[4,88,128]{2,1,0:T(8,128)S(1)} %pad_maximum_fusion.2), channel_id=1, source_target_pairs={{0,4},{1,5},{2,6},{3,7},{4,0},{5,1},{6,2},{7,3},{8,12},{9,13},{10,... | collective-permute-start | bytes 540680 | tf_op jit(solution)/shard_map/ppermute | solution.py:872
  17.2 0.0 collective-permute-done.6.refs_5_
  17.2 1.2 %collective-permute-start.7 = (f32[4,88,128]{2,1,0:T(8,128)S(1)}, f32[4,88,128]{2,1,0:T(8,128)S(1)}, u32[]{:S(2)}, u32[]{:S(2)}) collective-permute-start(f32[4,88,128]{2,1,0:T(8,128)S(1)} %pad_maximum_fusion.3), channel_id=1, source_target_pairs={{0,4},{1,5},{2,6},{3,7},{4,0},{5,1},{6,2},{7,3},{8,12},{9,13},{10,... | collective-permute-start | bytes 540680 | tf_op jit(solution)/shard_map/ppermute | solution.py:872
  18.4 3.6 %collective-permute-done.2.refs_2_ = f32[4,88,128]{2,1,0:T(8,128)S(1)} collective-permute-done((f32[4,88,128]{2,1,0:T(8,128)S(1)}, f32[4,88,128]{2,1,0:T(8,128)S(1)}, u32[]{:S(2)}, u32[]{:S(2)}) %collective-permute-start.2) | collective-permute-done | bytes 180256 | tf_op jit(solution)/shard_map/ppermute | solution.py:872
  22.0 0.0 copy-start
  22.0 0.0 copy-start.1
  22.0 0.1 collective-permute-start.3
  22.1 1.8 %collective-permute-done.7.refs_6_ = f32[4,88,128]{2,1,0:T(8,128)S(1)} collective-permute-done((f32[4,88,128]{2,1,0:T(8,128)S(1)}, f32[4,88,128]{2,1,0:T(8,128)S(1)}, u32[]{:S(2)}, u32[]{:S(2)}) %collective-permute-start.7) | collective-permute-done | bytes 180256 | tf_op jit(solution)/shard_map/ppermute | solution.py:872
  23.9 0.1 collective-permute-start.8
  24.0 0.0 collective-permute-done.3.refs_3_
  24.0 1.7 %collective-permute-done.8.refs_7_ = f32[8,88,128]{2,1,0:T(8,128)S(1)} collective-permute-done((f32[8,88,128]{2,1,0:T(8,128)S(1)}, f32[8,88,128]{2,1,0:T(8,128)S(1)}, u32[]{:S(2)}, u32[]{:S(2)}) %collective-permute-start.8) | collective-permute-done | bytes 360480 | tf_op jit(solution)/shard_map/ppermute | solution.py:872
  25.7 0.0 copy-done
  25.7 0.0 copy-done.1
  25.7 21.5 %solve.1 = (f32[72,128]{1,0:T(8,128)S(1)}, f32[72,128]{1,0:T(8,128)S(1)}, f32[72,128]{1,0:T(8,128)S(1)}, f32[72,128]{1,0:T(8,128)S(1)}) custom-call(f32[2,88,128]{2,1,0:T(8,128)S(1)} %pad_maximum_fusion.4.refs_0_, f32[2,88,128]{2,1,0:T(8,128)S(1)} %collective-permute-done.1.refs_1_, f32[4,88,128]{2,1,0:T(8,128)S(1)} %collective-permute-done.2.refs_2_, ...), custom_call_target="tpu_custom_call" | custom-call | tf_op jit(solution)/shard_map/solve/pallas_call | solution.py:970
  47.2 1.3 %collective-permute-start.9 = (f32[72,128]{1,0:T(8,128)S(1)}, f32[72,128]{1,0:T(8,128)S(1)}, u32[]{:S(2)}, u32[]{:S(2)}) collective-permute-start(f32[72,128]{1,0:T(8,128)S(1)} %get-tuple-element.35), channel_id=1, source_target_pairs={{0,8},{1,9},{2,10},{3,11},{4,12},{5,13},{6,14},{7,15},{8,0},{9,1},... | collective-permute-start | bytes 110600 | tf_op jit(solution)/shard_map/ppermute | solution.py:872
  48.5 1.6 %collective-permute-start.10 = (f32[72,128]{1,0:T(8,128)S(1)}, f32[72,128]{1,0:T(8,128)S(1)}, u32[]{:S(2)}, u32[]{:S(2)}) collective-permute-start(f32[72,128]{1,0:T(8,128)S(1)} %get-tuple-element.36), channel_id=1, source_target_pairs={{0,16},{1,17},{2,18},{3,19},{4,20},{5,21},{6,22},{7,23},{8,24},{9,... | collective-permute-start | bytes 110600 | tf_op jit(solution)/shard_map/ppermute | solution.py:872
  50.1 1.5 %collective-permute-start.11 = (f32[72,128]{1,0:T(8,128)S(1)}, f32[72,128]{1,0:T(8,128)S(1)}, u32[]{:S(2)}, u32[]{:S(2)}) collective-permute-start(f32[72,128]{1,0:T(8,128)S(1)} %get-tuple-element.37), channel_id=1, source_target_pairs={{0,24},{1,25},{2,26},{3,27},{4,28},{5,29},{6,30},{7,31},{8,16},{9,... | collective-permute-start | bytes 110600 | tf_op jit(solution)/shard_map/ppermute | solution.py:872
  51.6 0.0 collective-permute-done.9.refs_1_
  51.6 2.4 %collective-permute-done.10.refs_2_ = f32[72,128]{1,0:T(8,128)S(1)} collective-permute-done((f32[72,128]{1,0:T(8,128)S(1)}, f32[72,128]{1,0:T(8,128)S(1)}, u32[]{:S(2)}, u32[]{:S(2)}) %collective-permute-start.10) | collective-permute-done | bytes 36896 | tf_op jit(solution)/shard_map/ppermute | solution.py:872
  54.0 1.9 %collective-permute-done.11.refs_3_ = f32[72,128]{1,0:T(8,128)S(1)} collective-permute-done((f32[72,128]{1,0:T(8,128)S(1)}, f32[72,128]{1,0:T(8,128)S(1)}, u32[]{:S(2)}, u32[]{:S(2)}) %collective-permute-start.11) | collective-permute-done | bytes 36896 | tf_op jit(solution)/shard_map/ppermute | solution.py:872
  55.9 1.0 %unpack.1 = f32[4,6,4,384]{3,2,1,0:T(4,128)} custom-call(f32[72,128]{1,0:T(8,128)S(1)} %get-tuple-element.34.refs_0_, f32[72,128]{1,0:T(8,128)S(1)} %collective-permute-done.9.refs_1_, f32[72,128]{1,0:T(8,128)S(1)} %collective-permute-done.10.refs_2_, f32[72,128]{1,0:T(8,128)S(1)} %collective-permute-done.11.refs_3_, ...), custom_call_target="tpu_custom_call" | custom-call | tf_op jit(solution)/shard_map/unpack/pallas_call | solution.py:982
  (6 shorter events, 0.1 us)
Async XLA Ops:
  2.0 8.4 %collective-permute-start = (f32[88,128]{1,0:T(8,128)}, f32[88,128]{1,0:T(8,128)S(1)}, u32[]{:S(2)}, u32[]{:S(2)}) collective-permute-start(f32[88,128]{1,0:T(8,128)} %get-tuple-element.27), channel_id=1, source_target_pairs={{0,16},{1,17},{2,18},{3,19},{4,20},{5,21},{6,22},{7,23},{8,24},{9,... | collective-permute-start | bytes 135176 | tf_op jit(solution)/shard_map/ppermute | solution.py:872
  6.1 6.1 %collective-permute-start.4 = (f32[88,128]{1,0:T(8,128)}, f32[88,128]{1,0:T(8,128)S(1)}, u32[]{:S(2)}, u32[]{:S(2)}) collective-permute-start(f32[88,128]{1,0:T(8,128)} %get-tuple-element.28), channel_id=1, source_target_pairs={{0,24},{1,25},{2,26},{3,27},{4,28},{5,29},{6,30},{7,31},{8,16},{9,... | collective-permute-start | bytes 135176 | tf_op jit(solution)/shard_map/ppermute | solution.py:872
  7.4 4.7 %collective-permute-start.5 = (f32[88,128]{1,0:T(8,128)}, f32[88,128]{1,0:T(8,128)S(1)}, u32[]{:S(2)}, u32[]{:S(2)}) collective-permute-start(f32[88,128]{1,0:T(8,128)} %get-tuple-element.29), channel_id=1, source_target_pairs={{0,8},{1,9},{2,10},{3,11},{4,12},{5,13},{6,14},{7,15},{8,0},{9,1},... | collective-permute-start | bytes 135176 | tf_op jit(solution)/shard_map/ppermute | solution.py:872
  7.7 1.1 %copy-start.2 = (f32[384,384]{1,0:T(8,128)S(1)}, f32[384,384]{1,0:T(8,128)}, u32[]{:S(2)}) copy-start(f32[384,384]{1,0:T(8,128)} %source_ref) | copy-start | bytes 1769476
  8.7 1.7 %copy-start.3 = (f32[88,128]{1,0:T(8,128)S(1)}, f32[88,128]{1,0:T(8,128)}, u32[]{:S(2)}) copy-start(f32[88,128]{1,0:T(8,128)} %get-tuple-element.26) | copy-start | bytes 135172
  10.5 5.2 %collective-permute-start.1 = (f32[2,88,128]{2,1,0:T(8,128)S(1)}, f32[2,88,128]{2,1,0:T(8,128)S(1)}, u32[]{:S(2)}, u32[]{:S(2)}) collective-permute-start(f32[2,88,128]{2,1,0:T(8,128)S(1)} %pad_maximum_fusion.4.refs_0_), channel_id=1, source_target_pairs={{0,2},{1,3},{2,0},{3,1},{4,6},{5,7},{6,4},{7,5},{8,10},{9,11},{10,... | collective-permute-start | bytes 270344 | tf_op jit(solution)/shard_map/ppermute | solution.py:872
  12.2 5.0 %collective-permute-start.6 = (f32[2,88,128]{2,1,0:T(8,128)S(1)}, f32[2,88,128]{2,1,0:T(8,128)S(1)}, u32[]{:S(2)}, u32[]{:S(2)}) collective-permute-start(f32[2,88,128]{2,1,0:T(8,128)S(1)} %pad_maximum_fusion.5.refs_4_), channel_id=1, source_target_pairs={{0,2},{1,3},{2,0},{3,1},{4,6},{5,7},{6,4},{7,5},{8,10},{9,11},{10,... | collective-permute-start | bytes 270344 | tf_op jit(solution)/shard_map/ppermute | solution.py:872
  15.6 6.3 %collective-permute-start.2 = (f32[4,88,128]{2,1,0:T(8,128)S(1)}, f32[4,88,128]{2,1,0:T(8,128)S(1)}, u32[]{:S(2)}, u32[]{:S(2)}) collective-permute-start(f32[4,88,128]{2,1,0:T(8,128)S(1)} %pad_maximum_fusion.2), channel_id=1, source_target_pairs={{0,4},{1,5},{2,6},{3,7},{4,0},{5,1},{6,2},{7,3},{8,12},{9,13},{10,... | collective-permute-start | bytes 540680 | tf_op jit(solution)/shard_map/ppermute | solution.py:872
  17.2 6.6 %collective-permute-start.7 = (f32[4,88,128]{2,1,0:T(8,128)S(1)}, f32[4,88,128]{2,1,0:T(8,128)S(1)}, u32[]{:S(2)}, u32[]{:S(2)}) collective-permute-start(f32[4,88,128]{2,1,0:T(8,128)S(1)} %pad_maximum_fusion.3), channel_id=1, source_target_pairs={{0,4},{1,5},{2,6},{3,7},{4,0},{5,1},{6,2},{7,3},{8,12},{9,13},{10,... | collective-permute-start | bytes 540680 | tf_op jit(solution)/shard_map/ppermute | solution.py:872
  22.0 3.7 %copy-start = (f32[3,6,6]{2,1,0:T(8,128)S(1)}, f32[3,6,6]{2,1,0:T(8,128)}, u32[]{:S(2)}) copy-start(f32[3,6,6]{2,1,0:T(8,128)} %refs_8_.1) | copy-start | bytes 1300
  22.0 3.7 %copy-start.1 = (f32[3,6]{1,0:T(4,128)S(1)}, f32[3,6]{1,0:T(4,128)}, u32[]{:S(2)}) copy-start(f32[3,6]{1,0:T(4,128)} %refs_9_.1) | copy-start | bytes 220
  22.0 2.0 %collective-permute-start.3 = (f32[8,88,128]{2,1,0:T(8,128)S(1)}, f32[8,88,128]{2,1,0:T(8,128)S(1)}, u32[]{:S(2)}, u32[]{:S(2)}) collective-permute-start(f32[8,88,128]{2,1,0:T(8,128)S(1)} %pad_maximum_fusion), channel_id=1, source_target_pairs={{0,1},{1,0},{2,3},{3,2},{4,5},{5,4},{6,7},{7,6},{8,9},{9,8},{10,11... | collective-permute-start | bytes 1081352 | tf_op jit(solution)/shard_map/ppermute | solution.py:872
  23.9 1.7 %collective-permute-start.8 = (f32[8,88,128]{2,1,0:T(8,128)S(1)}, f32[8,88,128]{2,1,0:T(8,128)S(1)}, u32[]{:S(2)}, u32[]{:S(2)}) collective-permute-start(f32[8,88,128]{2,1,0:T(8,128)S(1)} %pad_maximum_fusion.1), channel_id=1, source_target_pairs={{0,1},{1,0},{2,3},{3,2},{4,5},{5,4},{6,7},{7,6},{8,9},{9,8},{10,11... | collective-permute-start | bytes 1081352 | tf_op jit(solution)/shard_map/ppermute | solution.py:872
  47.2 4.5 %collective-permute-start.9 = (f32[72,128]{1,0:T(8,128)S(1)}, f32[72,128]{1,0:T(8,128)S(1)}, u32[]{:S(2)}, u32[]{:S(2)}) collective-permute-start(f32[72,128]{1,0:T(8,128)S(1)} %get-tuple-element.35), channel_id=1, source_target_pairs={{0,8},{1,9},{2,10},{3,11},{4,12},{5,13},{6,14},{7,15},{8,0},{9,1},... | collective-permute-start | bytes 110600 | tf_op jit(solution)/shard_map/ppermute | solution.py:872
  48.5 5.5 %collective-permute-start.10 = (f32[72,128]{1,0:T(8,128)S(1)}, f32[72,128]{1,0:T(8,128)S(1)}, u32[]{:S(2)}, u32[]{:S(2)}) collective-permute-start(f32[72,128]{1,0:T(8,128)S(1)} %get-tuple-element.36), channel_id=1, source_target_pairs={{0,16},{1,17},{2,18},{3,19},{4,20},{5,21},{6,22},{7,23},{8,24},{9,... | collective-permute-start | bytes 110600 | tf_op jit(solution)/shard_map/ppermute | solution.py:872
  50.1 5.8 %collective-permute-start.11 = (f32[72,128]{1,0:T(8,128)S(1)}, f32[72,128]{1,0:T(8,128)S(1)}, u32[]{:S(2)}, u32[]{:S(2)}) collective-permute-start(f32[72,128]{1,0:T(8,128)S(1)} %get-tuple-element.37), channel_id=1, source_target_pairs={{0,24},{1,25},{2,26},{3,27},{4,28},{5,29},{6,30},{7,31},{8,16},{9,... | collective-permute-start | bytes 110600 | tf_op jit(solution)/shard_map/ppermute | solution.py:872
